TPU v7x, 32 devices: a whole 2x2x4 slice. The times are simulated.
32 devices in a mesh: row: 4 (over x, core), col: 8 (over z, y).
Axes of the slice: x: 2, y: 2, z: 4, core: 2. Of those that a mesh axis runs over, the one named last changes fastest.
Arguments:
- block_input: bfloat16 [2, 1152, 4096], P(None, 'col', 'row'), may hold values from -6 to 6
- text_tokens: bfloat16 [2, 480, 1152], P(None, 'row', 'col'), may hold values from -6 to 6
- text_length: int32 [2, 4], P(None, 'row'), may hold values from 1 to 120, as said below
- time_index: int32 [2, 4], P(None, 'row'), may hold values from 0 to 1023
- shift_table: float32 [6, 1152], P(None, 'col'), may hold values from -6 to 6
- time_table: float32 [6, 1152, 1024], P(None, 'col'), may hold values from -6 to 6
- query_weight: bfloat16 [1152, 1152], P('row', 'col'), may hold values from -0.1875 to 0.1875
- key_weight: bfloat16 [1152, 1152], P('row', 'col'), may hold values from -0.1875 to 0.1875
- value_weight: bfloat16 [1152, 1152], P('row', 'col'), may hold values from -0.1875 to 0.1875
- query_bias: float32 [1152], P('col'), may hold values from -4 to 4
- value_bias: float32 [1152], P('col'), may hold values from -4 to 4
- out_weight: bfloat16 [1152, 1152], P('col', 'row'), may hold values from -0.75 to 0.75
- out_bias: float32 [1152], P('col'), may hold values from -4 to 4
- cross_query: bfloat16 [1152, 1152], P('row', 'col'), may hold values from -0.1875 to 0.1875
- cross_key: bfloat16 [1152, 1152], P('row', 'col'), may hold values from -0.1875 to 0.1875
- cross_value: bfloat16 [1152, 1152], P('row', 'col'), may hold values from -0.1875 to 0.1875
- cross_query_bias: float32 [1152], P('col'), may hold values from -4 to 4
- cross_value_bias: float32 [1152], P('col'), may hold values from -4 to 4
- cross_out: bfloat16 [1152, 1152], P('col', 'row'), may hold values from -0.5 to 0.5
- cross_out_bias: float32 [1152], P('col'), may hold values from -4 to 4
- up_weight: bfloat16 [1152, 4608], P('row', 'col'), may hold values from -0.1875 to 0.1875
- up_bias: float32 [4608], P('col'), may hold values from -4 to 4
- down_weight: bfloat16 [4608, 1152], P('col', 'row'), may hold values from -0.09375 to 0.09375
- down_bias: float32 [1152], P('col'), may hold values from -4 to 4
- out_grad: bfloat16 [2, 1152, 4096], P(None, 'col', 'row'), may hold values from -6 to 6
Outputs:
- block_output: float32 [2, 1152, 4096], P(None, 'col', 'row')
- grad_input: float32 [2, 1152, 4096], P(None, 'col', 'row')
- grad_text: float32 [2, 480, 1152], P(None, 'row', 'col')
- grad_shift_table: float32 [6, 1152], P(None, 'col')
- grad_time_table: float32 [6, 1152, 1024], P(None, 'col')
- grad_query_weight: float32 [1152, 1152], P('row', 'col')
- grad_key_weight: float32 [1152, 1152], P('row', 'col')
- grad_value_weight: float32 [1152, 1152], P('row', 'col')
- grad_query_bias: float32 [1152], P('col')
- grad_value_bias: float32 [1152], P('col')
- grad_out_weight: float32 [1152, 1152], P('col', 'row')
- grad_out_bias: float32 [1152], P('col')
- grad_cross_query: float32 [1152, 1152], P('row', 'col')
- grad_cross_key: float32 [1152, 1152], P('row', 'col')
- grad_cross_value: float32 [1152, 1152], P('row', 'col')
- grad_cross_query_bias: float32 [1152], P('col')
- grad_cross_value_bias: float32 [1152], P('col')
- grad_cross_out: float32 [1152, 1152], P('col', 'row')
- grad_cross_out_bias: float32 [1152], P('col')
- grad_up_weight: float32 [1152, 4608], P('row', 'col')
- grad_up_bias: float32 [4608], P('col')
- grad_down_weight: float32 [4608, 1152], P('col', 'row')
- grad_down_bias: float32 [1152], P('col')
Inputs may be any that keep to these rules, and one draw needn't show every extreme that they name: Caption keys at positions text_length and beyond are masked; in each micro-batch one latent has all 120 text tokens and another has one.
All inputs are finite; a program needn't handle non-finite values.
Results may differ from a plain program's by a relative error of at most 0.02.
Values may be sent and summed in bfloat16 or wider, within the bound.
A program may use at most 192 MiB of HBM per device.

v0:
```python
import functools

import jax
import jax.numpy as jnp
from jax import lax
from jax.experimental import pallas as pl
from jax.experimental.pallas import tpu as pltpu
from jax.sharding import PartitionSpec as P

D = 1152
HEADS = 16
HD = 72

NORM_EPS = 1e-06
MASK_FILL = -1e30
BF = jnp.bfloat16
F32 = jnp.float32
LOG_SCALE = HD ** -0.5 * 1.4426950408889634


def dot_nn(a, b):
    return lax.dot_general(a, b, (((1,), (0,)), ((), ())), preferred_element_type=F32)


def dot_tn(a, b):
    return lax.dot_general(a, b, (((0,), (0,)), ((), ())), preferred_element_type=F32)


def dot_nt(a, b):
    return lax.dot_general(a, b, (((1,), (1,)), ((), ())), preferred_element_type=F32)


def after(value, *deps):
    return lax.optimization_barrier((value,) + deps)[0]


def row_swap(value, rows, bit):
    return lax.ppermute(value, "row", [(i, i ^ bit) for i in range(rows)])


def col_swap(value, cols, mask):
    return lax.ppermute(value, "col", [(i, i ^ mask) for i in range(cols)])


def layer_norm(resid):
    mean = jnp.mean(resid, axis=0, keepdims=True)
    centered = resid - mean
    var = jnp.mean(centered * centered, axis=0, keepdims=True)
    inv = lax.rsqrt(var + NORM_EPS)
    return centered * inv, inv


def norm_backward(grad, normed, inv, scale):
    dn = grad * (1.0 + scale)
    first = jnp.mean(dn, axis=0, keepdims=True)
    second = jnp.mean(dn * normed, axis=0, keepdims=True)
    back = (dn - first - normed * second) * inv
    return back, jnp.sum(grad, axis=1), jnp.sum(grad * normed, axis=1)


def dot_at(a, b, a_dim, b_dim):
    return lax.dot_general(a, b, (((a_dim,), (b_dim,)), ((), ())), preferred_element_type=F32)


def masked_scores(scores, len_ref):
    if len_ref is None:
        return scores
    return jnp.where(lax.broadcasted_iota(jnp.int32, scores.shape, 1) < len_ref[0], scores, MASK_FILL)


def join(refs, rows):
    return jnp.concatenate([ref[rows, :] for ref in refs], axis=1)


def put(refs, rows, value):
    start = 0
    for ref in refs:
        end = start + ref.shape[1]
        ref[rows, :] = value[:, start:end].astype(ref.dtype)
        start = end


def head_rows(h, first):
    return slice(first + HD * h, first + HD * h + HD)


def forward_kernel(n_q, n_kv, has_len, *refs):
    len_ref = refs[0] if has_len else None
    refs = refs[1:] if has_len else refs
    q_refs, kv_refs, out_refs, lse_ref = refs[:n_q], refs[n_q : n_q + n_kv], refs[n_q + n_kv : -1], refs[-1]
    feat = q_refs[0].shape[0]
    for h in range(feat // HD):
        head, value_rows = head_rows(h, 0), head_rows(h, feat)
        q, k, v = join(q_refs, head), join(kv_refs, head), join(kv_refs, value_rows)
        scores = masked_scores(dot_at(q, k, 0, 0), len_ref)
        top = jnp.max(scores, axis=1, keepdims=True)
        probs = jnp.exp2((scores - top) * LOG_SCALE)
        total = jnp.sum(probs, axis=1, keepdims=True)
        out = dot_at(probs.astype(BF), v, 1, 1) / total
        put(out_refs, head, out.T)
        lse_ref[0, :, h : h + 1] = top * LOG_SCALE + jnp.log2(total)


def backward_kernel(n_q, n_kv, has_len, *refs):
    len_ref = refs[0] if has_len else None
    refs = refs[1:] if has_len else refs
    q_refs, kv_refs, lse_ref = refs[:n_q], refs[n_q : n_q + n_kv], refs[n_q + n_kv]
    refs = refs[n_q + n_kv + 1 :]
    do_refs, dq_refs, dkv_refs = refs[:n_q], refs[n_q : 2 * n_q], refs[2 * n_q :]
    feat = q_refs[0].shape[0]
    for h in range(feat // HD):
        head, value_rows = head_rows(h, 0), head_rows(h, feat)
        q, k, v, do = join(q_refs, head), join(kv_refs, head), join(kv_refs, value_rows), join(do_refs, head)
        scores = masked_scores(dot_at(q, k, 0, 0), len_ref)
        probs = jnp.exp2(scores * LOG_SCALE - lse_ref[0, :, h : h + 1])
        put(dkv_refs, value_rows, dot_at(do, probs.astype(BF), 1, 0))
        dp = dot_at(do, v, 0, 0)
        ds = probs * (dp - jnp.sum(dp * probs, axis=1, keepdims=True)) * HD ** -0.5
        ds = ds.astype(BF)
        put(dq_refs, head, dot_at(ds, k, 1, 1).T)
        put(dkv_refs, head, dot_at(q, ds, 1, 0))


def part_spec(shape, steps):
    if len(shape) == 3:
        return pl.BlockSpec((1,) + tuple(shape[1:]), lambda z: (z, 0, 0))
    return pl.BlockSpec((shape[0] // steps, shape[1]), lambda z: (z, 0))


def whole_spec(shape):
    return pl.BlockSpec(tuple(shape), lambda z: (0,) * len(shape))


def call_parts(kernel, steps, args, arg_specs, outs, out_specs, scratch=()):
    return pl.pallas_call(
        kernel,
        grid=(steps,),
        in_specs=arg_specs,
        out_specs=out_specs,
        out_shape=outs,
        scratch_shapes=list(scratch),
        compiler_params=pltpu.CompilerParams(vmem_limit_bytes=50 * 2**20),
    )(*args)


def attend_forward(q_parts, kv_parts, length, half):
    rows, tokens = q_parts[0].shape[0], sum(q.shape[1] for q in q_parts)
    outs = [jax.ShapeDtypeStruct(q.shape, BF) for q in q_parts]
    outs.append(jax.ShapeDtypeStruct((half, tokens, rows // half // HD), F32))
    args = list(q_parts) + list(kv_parts)
    specs = [part_spec(a.shape, half) for a in args]
    if length is not None:
        args, specs = [length] + args, [pl.BlockSpec(memory_space=pltpu.SMEM)] + specs
    kernel = functools.partial(forward_kernel, len(q_parts), len(kv_parts), length is not None)
    res = call_parts(kernel, half, args, specs, outs, [part_spec(o.shape, half) for o in outs])
    return res[:-1], res[-1]


def attend_backward(q_parts, kv_parts, length, lse, do_parts, half):
    outs = [jax.ShapeDtypeStruct(a.shape, BF) for a in list(q_parts) + list(kv_parts)]
    args = list(q_parts) + list(kv_parts) + [lse] + list(do_parts)
    specs = [part_spec(a.shape, half) for a in args]
    if length is not None:
        args, specs = [length] + args, [pl.BlockSpec(memory_space=pltpu.SMEM)] + specs
    kernel = functools.partial(backward_kernel, len(q_parts), len(kv_parts), length is not None)
    res = call_parts(kernel, half, args, specs, outs, [part_spec(o.shape, half) for o in outs])
    return res[: len(q_parts)], res[len(q_parts) :]


def in_kernel(start, size, w_ref, x_ref, bias_ref, *out_refs):
    value = dot_tn(w_ref[0, :, start : start + size], x_ref[...]) + bias_ref[...]
    first = 0
    for ref in out_refs:
        ref[...] = value[first : first + ref.shape[0]].astype(ref.dtype)
        first += ref.shape[0]


def gelu_kernel(start, size, w_ref, x_ref, bias_ref, hidden_ref, slope_ref):
    v = dot_tn(w_ref[0, :, start : start + size], x_ref[...]) + bias_ref[...]
    square = v * v
    t = jnp.tanh(0.7978845608 * (v + 0.044715 * square * v))
    hidden_ref[...] = (0.5 * v * (1.0 + t)).astype(BF)
    slope_ref[...] = 0.5 * (1.0 + t) + 0.5 * v * (1.0 - t * t) * 0.7978845608 * (1.0 + 3.0 * 0.044715 * square)


def slope_kernel(start, size, w_ref, x_ref, slope_ref, grad_ref, sum_ref):
    grad = (dot_tn(w_ref[0, :, start : start + size], x_ref[...]) * slope_ref[...]).astype(BF)
    grad_ref[...] = grad
    sum_ref[...] = jnp.sum(grad.astype(F32), axis=1, keepdims=True)


def apply_in(kernel, weight, span, value, extra, outs):
    half = weight.shape[0]
    args = [weight, value, extra]
    specs = [part_spec(weight.shape, half), whole_spec(value.shape), part_spec(extra.shape, half)]
    outs = [jax.ShapeDtypeStruct((rows, cols), dtype) for rows, cols, dtype in outs]
    kernel = functools.partial(kernel, span[0], span[1])
    return call_parts(kernel, half, args, specs, outs, [part_spec(o.shape, half) for o in outs])


def out_kernel(start, w_ref, *refs):
    v_refs, out_ref, acc_ref = refs[:-2], refs[-2], refs[-1]
    z = pl.program_id(0)
    total = None
    for v_ref in v_refs:
        end = start + v_ref.shape[0]
        part = dot_nn(w_ref[0, :, start:end], v_ref[...])
        total = part if total is None else total + part
        start = end

    @pl.when(z == 0)
    def _():
        acc_ref[...] = total

    @pl.when(z > 0)
    def _():
        acc_ref[...] += total

    @pl.when(z == pl.num_programs(0) - 1)
    def _():
        out_ref[...] = acc_ref[...].astype(out_ref.dtype)


def apply_out(weight, start, values, dtype):
    half = weight.shape[0]
    tokens = values[0].shape[1]
    args = [weight] + list(values)
    out = jax.ShapeDtypeStruct((D, tokens), dtype)
    return call_parts(
        functools.partial(out_kernel, start),
        half,
        args,
        [part_spec(a.shape, half) for a in args],
        out,
        whole_spec(out.shape),
        [pltpu.VMEM((D, tokens), F32)],
    )


def outer_kernel(terms, *refs):
    out_ref = refs[-1]
    rows, chunk = out_ref.shape[0], out_ref.shape[1]
    for r in range(rows):
        block = slice(r * chunk, r * chunk + chunk)
        start, at = 0, 0
        for count in terms:
            total = None
            for i in range(count):
                part = dot_nt(refs[at + i][block, :], refs[at + count + i][...])
                total = part if total is None else total + part
            end = start + refs[at + count].shape[0]
            out_ref[r, :, start:end] = total.astype(BF)
            start, at = end, at + 2 * count


def outer_blocks(pairs, rows, half):
    chunk = D // rows
    sizes = [b[0].shape[0] // half for _, b in pairs]
    specs, args = [], []
    for a, b in pairs:
        specs += [whole_spec(p.shape) for p in a] + [part_spec(p.shape, half) for p in b]
        args += list(a) + list(b)
    out = jax.ShapeDtypeStruct((half * rows, chunk, sum(sizes)), BF)
    out_spec = pl.BlockSpec((rows, chunk, sum(sizes)), lambda z: (z, 0, 0))
    kernel = functools.partial(outer_kernel, [len(a) for a, _ in pairs])
    return call_parts(kernel, half, args, specs, out, out_spec), sizes


def shards(
    block_input,
    text_tokens,
    text_length,
    time_index,
    shift_table,
    time_table,
    query_weight,
    key_weight,
    value_weight,
    query_bias,
    value_bias,
    out_weight,
    out_bias,
    cross_query,
    cross_key,
    cross_value,
    cross_query_bias,
    cross_value_bias,
    cross_out,
    cross_out_bias,
    up_weight,
    up_bias,
    down_weight,
    down_bias,
    out_grad,
):
    rows, cols = lax.axis_size("row"), lax.axis_size("col")
    r, c = lax.axis_index("row"), lax.axis_index("col")
    half = cols // 2
    feat = block_input.shape[1]
    width = 2 * block_input.shape[2] // cols
    texts = text_tokens.shape[1]
    steps = time_table.shape[2]
    ups = up_bias.shape[0]
    core, low_z, micro = r & 1, (c >> 1) & 1, c // half
    at_home = core == low_z

    kv_masks = [1 << b for b in range(2, cols.bit_length() - 2)]
    swap_pairs = []
    for i in range(rows):
        for j in range(cols):
            swap_pairs.append(
                (i * cols + j, ((i & ~1) | ((j >> 1) & 1)) * cols + ((j & ~2) | ((i & 1) << 1)))
            )

    def place_swap(value):
        return lax.ppermute(value, ("row", "col"), swap_pairs)

    def token_blocks(value):
        return value.reshape(2, feat, half, width).transpose(0, 2, 1, 3).reshape(cols, feat, width)

    def tokens_out(value):
        blocks = place_swap(value.astype(BF)).reshape(cols, feat, width)
        blocks = lax.all_to_all(blocks, "col", 0, 0, tiled=True)
        blocks = blocks.reshape(2, half, feat, width).transpose(0, 2, 1, 3)
        return blocks.reshape(2, feat, half * width).astype(F32)

    def gather_pair(value):
        return [value, col_swap(value, cols, 1)]

    def reduce_pair(weight, start, *values):
        other = apply_out(weight, start, [v[1] for v in values], BF)
        received = col_swap(other, cols, 1)
        return apply_out(weight, start, [v[0] for v in values], F32) + received.astype(F32)

    def gather_keys(parts):
        parts = list(parts) + [row_swap(p, rows, 1) for p in parts]
        for mask in kv_masks:
            parts = parts + [col_swap(p, cols, mask) for p in parts]
        return parts

    def add_swapped(parts, swap):
        h = len(parts) // 2
        return [(a.astype(F32) + swap(b).astype(F32)).astype(BF) for a, b in zip(parts[:h], parts[h:])]

    def reduce_keys(parts):
        for mask in reversed(kv_masks):
            parts = add_swapped(parts, lambda p, mask=mask: col_swap(p, cols, mask))
        return add_swapped(parts, lambda p: row_swap(p, rows, 1))

    groups = [[i * cols + 2 * z + y for z in range(half) for i in range(rows)] for y in range(2)]

    def gather_weights(shards_w):
        flat = jnp.concatenate(shards_w, axis=1)
        full = lax.all_gather(flat, ("row", "col"), axis=0, tiled=True, axis_index_groups=groups)
        return full.reshape(half, D, flat.shape[1])

    def reduce_weights(pairs):
        blocks, sizes = outer_blocks(pairs, rows, half)
        flat = blocks.reshape(half * D, sum(sizes))
        own = lax.psum_scatter(flat, ("row", "col"), scatter_dimension=0, tiled=True, axis_index_groups=groups)
        out, start = [], 0
        for size in sizes:
            out.append(own[:, start : start + size].astype(F32))
            start += size
        return out

    first_w = gather_weights(
        [query_weight, key_weight, value_weight, out_weight.T, cross_query, cross_key, cross_value, cross_out.T]
    )
    second_w = gather_weights([up_weight, down_weight.T])

    step_ids = jnp.arange(steps, dtype=jnp.int32)
    onehot = (time_index[:, 0][:, None] == step_ids[None, :]).astype(F32)
    modulation = lax.dot_general(
        onehot,
        time_table.reshape(6 * feat, steps),
        (((1,), (1,)), ((), ())),
        precision=lax.Precision.HIGHEST,
        preferred_element_type=F32,
    ).reshape(2, 6, feat) + shift_table[None]
    same = [
        jnp.broadcast_to(b.reshape(1, -1, feat), (2, b.shape[0] // feat, feat))
        for b in (out_bias, cross_out_bias, down_bias, query_bias, value_bias, cross_query_bias, cross_value_bias, up_bias)
    ]
    lengths = jnp.broadcast_to(text_length.astype(F32)[:, :, None], (2, 1, feat))
    small = jnp.concatenate([modulation, lengths] + same, axis=1).transpose(0, 2, 1)
    small_high = lax.reduce_precision(small, 8, 7)
    small_rest = small - small_high
    small_mid = lax.reduce_precision(small_rest, 8, 7)
    small_low = small_rest - small_mid
    extra = jnp.concatenate(
        [text_tokens.transpose(0, 2, 1)] + [p.astype(BF) for p in (small_high, small_mid, small_low)], axis=2
    )
    blocks = jnp.concatenate([token_blocks(block_input), token_blocks(out_grad), jnp.repeat(extra, half, axis=0)], axis=2)
    blocks = lax.all_to_all(blocks, "col", 0, 0, tiled=True).reshape(D, -1)
    arrived = place_swap(blocks)
    small_n, head = small.shape[2], 2 * width

    def small_of(value):
        parts = [value[:, head + texts + i * small_n : head + texts + (i + 1) * small_n].astype(F32) for i in range(3)]
        return parts[0] + parts[1] + parts[2]

    model_rows = small_of(arrived)
    shift_a, scale_a, gate_a, shift_m, scale_m, gate_m, length_row, out_b, cout_b, down_b = (
        model_rows[:, i : i + 1] for i in range(10)
    )
    length = length_row[0].astype(jnp.int32)
    col_rows = small_of(arrived).reshape(cols, feat, small_n)
    col_rows = jnp.concatenate(
        [
            lax.dynamic_index_in_dim(col_rows, 2 * e + (c & 1), 0, keepdims=False)[:, 10:].T.reshape(-1, 1, feat)
            for e in range(half)
        ],
        axis=1,
    )
    q_b, v_b, cq_b, cv_b = (col_rows[i].reshape(half * feat, 1) for i in range(4))
    up_b = col_rows[4:].transpose(1, 0, 2).reshape(half * ups, 1)
    text_t = arrived[:, head : head + texts]

    resid = arrived[:, :width].astype(F32)
    cot = arrived[:, width:head].astype(F32)
    heads_w, hidden_w = half * feat, half * ups
    qkv_w, out_w, cq_w, ckv_w, cout_w = (
        first_w[:, :, i * feat : j * feat] for i, j in ((0, 3), (3, 4), (4, 5), (5, 7), (7, 8))
    )

    def columns(*parts):
        return jnp.stack([p.reshape(half, feat) for p in parts], axis=1).reshape(-1, 1)

    def heads_in(weight, value, *biases):
        sizes = [1] if len(biases) == 1 else [1, len(biases) - 1]
        outs = [(n * heads_w, value.shape[1], BF) for n in sizes]
        return apply_in(in_kernel, weight, (0, len(biases) * feat), value, columns(*biases), outs)

    none = jnp.zeros((heads_w,), F32)
    normed_a, inv_a = layer_norm(resid)
    attn_full = gather_pair((normed_a * (1.0 + scale_a) + shift_a).astype(BF))
    q_parts, kv_parts = zip(*(heads_in(qkv_w, p, q_b, none, v_b) for p in attn_full))
    kv_all = gather_keys(kv_parts)
    att, lse = attend_forward(q_parts, kv_all, None, half)
    branch_a = reduce_pair(out_w, 0, att) + out_b
    after_attn = resid + gate_a * branch_a
    cross_full = gather_pair(after_attn.astype(BF))
    cq_parts = [heads_in(cq_w, p, cq_b)[0] for p in cross_full]
    ckv = apply_in(in_kernel, ckv_w, (0, 2 * feat), text_t, columns(none, cv_b), [(2 * heads_w, texts, BF)])
    catt, clse = attend_forward(cq_parts, ckv, length, half)
    after_cross = after_attn + reduce_pair(cout_w, 0, catt) + cout_b
    normed_m, inv_m = layer_norm(after_cross)
    mlp_full = gather_pair((normed_m * (1.0 + scale_m) + shift_m).astype(BF))
    hidden_outs = [(hidden_w, width, BF), (hidden_w, width, F32)]
    hidden, slope = zip(*(apply_in(gelu_kernel, second_w, (0, ups), p, up_b, hidden_outs) for p in mlp_full))
    branch_m = reduce_pair(second_w, ups, hidden) + down_b
    block_output = tokens_out(after_cross + gate_m * branch_m)

    grad_mlp = gate_m * cot
    low_full = gather_pair(grad_mlp.astype(BF))
    g_down_b = jnp.sum(grad_mlp, axis=1)
    g_gate_m = jnp.sum(cot * branch_m, axis=1)
    pre_outs = [(hidden_w, width, BF), (hidden_w, 1, F32)]
    grad_pre, pre_sums = zip(
        *(apply_in(slope_kernel, second_w, (ups, ups), p, d, pre_outs) for p, d in zip(low_full, slope))
    )
    g_up_b = pre_sums[0] + pre_sums[1]
    back_in = reduce_pair(second_w, 0, grad_pre)
    g_up, g_down = reduce_weights([(mlp_full, grad_pre), (low_full, hidden)])
    back_m, g_shift_m, g_scale_m = norm_backward(back_in, normed_m, inv_m, scale_m)
    grad_cross = cot + back_m
    g_cout_b = jnp.sum(grad_cross, axis=1)
    low_cross = gather_pair(grad_cross.astype(BF))
    dcatt = [heads_in(cout_w, p, none)[0] for p in low_cross]
    dcq, dckv = attend_backward(cq_parts, ckv, length, clse, dcatt, half)
    grad_res = grad_cross + reduce_pair(cq_w, 0, dcq)
    g_cq, g_ckv, g_cout = reduce_weights([(cross_full, dcq), ([text_t], dckv), (low_cross, catt)])
    g_ck, g_cv = g_ckv[:, :feat], g_ckv[:, feat:]
    g_cq_b = jnp.sum(sum(p.astype(F32) for p in dcq), axis=1)
    g_cv_b = jnp.sum(dckv[0].astype(F32).reshape(half, 2, feat, texts)[:, 1], axis=2)
    g_gate_a = jnp.sum(grad_res * branch_a, axis=1)
    grad_attn = gate_a * grad_res
    g_out_b = jnp.sum(grad_attn, axis=1)
    low_attn = gather_pair(grad_attn.astype(BF))
    datt = [heads_in(out_w, p, none)[0] for p in low_attn]
    dq, dkv = attend_backward(q_parts, kv_all, None, lse, datt, half)
    dkv = reduce_keys(dkv)
    back_att = reduce_pair(qkv_w, 0, dq, dkv)
    g_q, g_kv, g_out = reduce_weights([(attn_full, dq), (attn_full, dkv), (low_attn, att)])
    g_k, g_v = g_kv[:, :feat], g_kv[:, feat:]
    g_q_b = jnp.sum(sum(p.astype(F32) for p in dq), axis=1)
    g_v_b = jnp.sum(sum(p.astype(F32) for p in dkv).reshape(half, 2, feat, width)[:, 1], axis=2)
    back_a, g_shift_a, g_scale_a = norm_backward(back_att, normed_a, inv_a, scale_a)
    grad_input = tokens_out(grad_res + back_a)
    grad_text = apply_out(ckv_w, 0, dckv, BF)
    grad_text = grad_text.astype(F32) + row_swap(grad_text, rows, 1).astype(F32)
    grad_text = jnp.where(at_home, grad_text, 0.0).astype(BF).reshape(cols, feat, texts)
    grad_text = lax.all_to_all(grad_text, "col", 0, 0, tiled=True)
    grad_text = jnp.sum(grad_text.reshape(2, half, feat, texts).astype(F32), axis=1).transpose(0, 2, 1)

    model_g = jnp.stack(
        [g_shift_a, g_scale_a, g_gate_a, g_shift_m, g_scale_m, g_gate_m, g_out_b, g_cout_b, g_down_b], axis=1
    )
    model_g = model_g.T.reshape(9, cols, feat).transpose(1, 0, 2)
    per_col = ups // feat
    col_g = jnp.concatenate(
        [g.reshape(half, 1, feat) for g in (g_q_b, g_v_b, g_cq_b, g_cv_b)] + [g_up_b.reshape(half, per_col, feat)],
        axis=1,
    )
    side = c & 1
    blocks = []
    for j in range(cols):
        blocks.append(jnp.where(side == (j & 1), col_g[j >> 1], 0.0))
    small_g = jnp.concatenate([model_g, jnp.stack(blocks)], axis=1)
    small_g = lax.all_to_all(small_g, "col", 0, 0, tiled=True)
    mod_g = small_g[:, :6].reshape(2, cols // 8, 2, 2, 6, feat).sum(axis=(1, 3))
    bias_g = small_g[:, 6:].sum(axis=0)
    step_rows = jnp.broadcast_to(time_index.astype(F32), (2, feat))
    small_g = lax.all_gather(jnp.concatenate([mod_g.reshape(24, feat), bias_g, step_rows], axis=0), "row")
    step_all = small_g[:, -2:, 0].T.reshape(2 * rows).astype(jnp.int32)
    mod_g = small_g[:, :24].reshape(rows // 2, 2, 2, 2, 6, feat).sum(axis=1)
    mod_g = mod_g.transpose(1, 0, 2, 3, 4).reshape(2 * rows, 6, feat)
    bias_g = small_g[:, 24:-2].sum(axis=0)
    g_shift = mod_g.sum(axis=0)
    onehot_all = (step_all[:, None] == step_ids[None, :]).astype(F32)
    g_time = lax.dot_general(
        mod_g.reshape(2 * rows, 6 * feat),
        onehot_all,
        (((0,), (0,)), ((), ())),
        precision=lax.Precision.HIGHEST,
        preferred_element_type=F32,
    ).reshape(6, feat, steps)
    g_out_b, g_cout_b, g_down_b, g_q_b, g_v_b, g_cq_b, g_cv_b = (bias_g[i] for i in range(7))
    g_up_b = bias_g[7:].reshape(ups)
    return (
        block_output,
        grad_input,
        grad_text,
        g_shift,
        g_time,
        g_q,
        g_k,
        g_v,
        g_q_b,
        g_v_b,
        g_out.T,
        g_out_b,
        g_cq,
        g_ck,
        g_cv,
        g_cq_b,
        g_cv_b,
        g_cout.T,
        g_cout_b,
        g_up,
        g_up_b,
        g_down.T,
        g_down_b,
    )


def solution(mesh):
    return jax.shard_map(
        shards,
        mesh=mesh,
        in_specs=(
            P(None, "col", "row"),
            P(None, "row", "col"),
            P(None, "row"),
            P(None, "row"),
            P(None, "col"),
            P(None, "col", None),
            P("row", "col"),
            P("row", "col"),
            P("row", "col"),
            P("col"),
            P("col"),
            P("col", "row"),
            P("col"),
            P("row", "col"),
            P("row", "col"),
            P("row", "col"),
            P("col"),
            P("col"),
            P("col", "row"),
            P("col"),
            P("row", "col"),
            P("col"),
            P("col", "row"),
            P("col"),
            P(None, "col", "row"),
        ),
        out_specs=(
            P(None, "col", "row"),
            P(None, "col", "row"),
            P(None, "row", "col"),
            P(None, "col"),
            P(None, "col", None),
            P("row", "col"),
            P("row", "col"),
            P("row", "col"),
            P("col"),
            P("col"),
            P("col", "row"),
            P("col"),
            P("row", "col"),
            P("row", "col"),
            P("row", "col"),
            P("col"),
            P("col"),
            P("col", "row"),
            P("col"),
            P("row", "col"),
            P("col"),
            P("col", "row"),
            P("col"),
        ),
        check_vma=False,
    )
```

profile of v0, /device:TPU:0, one launch (start us, length us, event | category | flops | bytes accessed | tf_op | source)
XLA Modules:
  0.0 700.6 jit_solution(12398900734771390997)
XLA Ops:
  31.8 78.9 %all_to_all.25 = bf16[8,144,686]{2,1,0:T(8,128)(2,1)S(1)} all-to-all(bf16[8,144,686]{2,1,0:T(8,128)(2,1)S(1)} %pad_maximum_fusion), channel_id=1, replica_groups=mesh['row'=4,'col'=8] {'col'}, dimensions={0} | all-to-all | bytes 3161088 | tf_op jit(solution)/shard_map/all_to_all | solution.py:395
  119.7 26.2 %all-gather.5.cloned.1.call-done = bf16[4608,1152]{1,0:T(8,128)(2,1)} async-done(((bf16[288,1152]{1,0:T(8,128)(2,1)}), bf16[4608,1152]{1,0:T(8,128)(2,1)}) %all-gather.5.cloned.1.call-update) | async-done | bytes 10616848 | tf_op jit(solution)/shard_map/all_gather | solution.py:354
  155.5 16.5 %collective-permute-start.2 = (bf16[1152,256]{1,0:T(8,128)(2,1)S(1)}, bf16[1152,256]{1,0:T(8,128)(2,1)S(1)}, u32[]{:S(2)}, u32[]{:S(2)}) collective-permute-start(bf16[1152,256]{1,0:T(8,128)(2,1)S(1)} %get-tuple-element.52.refs_2_), channel_id=1, source_target_pairs={{0,8},{8,0},{16,24},{24,16},{1,9},{9,1},{17,25},{25,17},{2,10},{10... | collective-permute-start | bytes 1769480 | tf_op jit(solution)/shard_map/ppermute | solution.py:38
  176.8 7.6 %fusion.37 = (bf16[4,1152,144]{2,1,0:T(8,128)(2,1)S(1)}, bf16[4,1152,144]{2,1,0:T(8,128)(2,1)}, bf16[4,1152,144]{2,1,0:T(8,128)(2,1)}) fusion(bf16[4,1152,1152]{2,1,0:T(8,128)(2,1)} %bitcast.135), kind=kLoop, calls=%fused_computation.151 | loop fusion | bytes 7962624 | tf_op jit(solution)/shard_map/slice | solution.py:424
  184.5 8.9 %shard_map.418 = (bf16[576,256]{1,0:T(8,128)(2,1)S(1)}, bf16[576,256]{1,0:T(8,128)(2,1)S(1)}, f32[4,512,2]{2,1,0:T(8,128)}) custom-call(bf16[576,256]{1,0:T(8,128)(2,1)S(1)} %get-tuple-element.50.refs_0_, bf16[576,256]{1,0:T(8,128)(2,1)S(1)} %get-tuple-element.51.refs_1_, bf16[1152,256]{1,0:T(8,128)(2,1)S(1)} %get-tuple-element.52.refs_2_, ...), custom_call_target="tpu_custom_call" | custom-call | tf_op jit(solution)/shard_map/pallas_call | solution.py:135
  197.5 13.2 %collective-permute-done.4 = bf16[1152,256]{1,0:T(8,128)(2,1)S(1)} collective-permute-done((bf16[1152,256]{1,0:T(8,128)(2,1)S(1)}, bf16[1152,256]{1,0:T(8,128)(2,1)S(1)}, u32[]{:S(2)}, u32[]{:S(2)}) %collective-permute-start.4) | collective-permute-done | bytes 589856 | tf_op jit(solution)/shard_map/ppermute | solution.py:42
  221.8 6.2 slice.306.w_ref
  251.0 6.6 collective-permute-done.6
  267.2 10.6 %collective-permute-done.7.x_ref.refs_1_ = bf16[1152,256]{1,0:T(8,128)(2,1)} collective-permute-done((bf16[1152,256]{1,0:T(8,128)(2,1)}, bf16[1152,256]{1,0:T(8,128)(2,1)}, u32[]{:S(2)}, u32[]{:S(2)}) %collective-permute-start.7) | collective-permute-done | bytes 589856 | tf_op jit(solution)/shard_map/ppermute | solution.py:42
  279.1 7.5 %shard_map.429 = (bf16[2304,256]{1,0:T(8,128)(2,1)S(1)}, f32[2304,256]{1,0:T(8,128)}) custom-call(bf16[4,1152,1152]{2,1,0:T(8,128)(2,1)} %bitcast.123, bf16[1152,256]{1,0:T(8,128)(2,1)} %collective-permute-done.7.x_ref.refs_1_, f32[2304,1]{1,0:T(8,128)S(1)} %copy-done.8), custom_call_target="tpu_custom_call" | custom-call | tf_op jit(solution)/shard_map/pallas_call | solution.py:135
  287.8 7.8 %shard_map.433 = (bf16[2304,256]{1,0:T(8,128)(2,1)S(1)}, f32[2304,1]{1,0:T(8,128)S(1)}) custom-call(bf16[4,1152,1152]{2,1,0:T(8,128)(2,1)} %bitcast.124, bf16[1152,256]{1,0:T(8,128)(2,1)} %collective-permute-done.10.x_ref.refs_5_, f32[2304,256]{1,0:T(8,128)} %get-tuple-element.62.slope_ref), custom_call_target="tpu_custom_call" | custom-call | tf_op jit(solution)/shard_map/pallas_call | solution.py:135
  296.6 6.5 shard_map.434
  304.7 7.5 %shard_map.427 = (bf16[2304,256]{1,0:T(8,128)(2,1)S(1)}, f32[2304,256]{1,0:T(8,128)}) custom-call(bf16[4,1152,1152]{2,1,0:T(8,128)(2,1)} %bitcast.126, bf16[1152,256]{1,0:T(8,128)(2,1)} %add_convert_fusion.3.x_ref.refs_0_, f32[2304,1]{1,0:T(8,128)S(1)} %copy-done.9), custom_call_target="tpu_custom_call" | custom-call | tf_op jit(solution)/shard_map/pallas_call | solution.py:135
  312.2 8.2 %shard_map.431 = (bf16[2304,256]{1,0:T(8,128)(2,1)S(1)}, f32[2304,1]{1,0:T(8,128)S(1)}) custom-call(bf16[4,1152,1152]{2,1,0:T(8,128)(2,1)} %bitcast.127, bf16[1152,256]{1,0:T(8,128)(2,1)} %fusion.7.x_ref.refs_4_, f32[2304,256]{1,0:T(8,128)} %get-tuple-element.60.slope_ref), custom_call_target="tpu_custom_call" | custom-call | tf_op jit(solution)/shard_map/pallas_call | solution.py:135
  321.4 6.5 shard_map.432
  327.9 6.2 shard_map.428
  334.2 6.3 shard_map.430
  342.5 10.6 %collective-permute-done.8 = bf16[1152,256]{1,0:T(8,128)(2,1)S(1)} collective-permute-done((bf16[1152,256]{1,0:T(8,128)(2,1)S(1)}, bf16[1152,256]{1,0:T(8,128)(2,1)S(1)}, u32[]{:S(2)}, u32[]{:S(2)}) %collective-permute-start.8) | collective-permute-done | bytes 589856 | tf_op jit(solution)/shard_map/ppermute | solution.py:42
  358.4 9.0 %collective-permute-done.12.x_ref.refs_7_ = bf16[1152,256]{1,0:T(8,128)(2,1)S(1)} collective-permute-done((bf16[1152,256]{1,0:T(8,128)(2,1)S(1)}, bf16[1152,256]{1,0:T(8,128)(2,1)S(1)}, u32[]{:S(2)}, u32[]{:S(2)}) %collective-permute-start.12) | collective-permute-done | bytes 589856 | tf_op jit(solution)/shard_map/ppermute | solution.py:42
  374.2 7.1 %shard_map.447 = bf16[16,288,576]{2,1,0:T(8,128)(2,1)} custom-call(bf16[1152,256]{1,0:T(8,128)(2,1)} %fusion.32.x_ref.refs_0_, bf16[1152,256]{1,0:T(8,128)(2,1)} %collective-permute-done.5.x_ref.refs_1_, bf16[576,256]{1,0:T(8,128)(2,1)S(1)} %get-tuple-element.65.refs_0_.refs_2_, bf16[576,256]{1,0:T(8,128)(2,1)S(1)} %get-tuple-element.66.refs_0_.refs_3_, ...), custom_call_target="tpu_custom_call" | custom-call | tf_op jit(solution)/shard_map/pallas_call | solution.py:135
  388.1 8.9 %collective-permute-done.13 = bf16[1152,256]{1,0:T(8,128)(2,1)S(1)} collective-permute-done((bf16[1152,256]{1,0:T(8,128)(2,1)S(1)}, bf16[1152,256]{1,0:T(8,128)(2,1)S(1)}, u32[]{:S(2)}, u32[]{:S(2)}) %collective-permute-start.13) | collective-permute-done | bytes 589856 | tf_op jit(solution)/shard_map/ppermute | solution.py:42
  401.2 8.1 %collective-permute-done.14.x_ref.refs_9_ = bf16[1152,256]{1,0:T(8,128)(2,1)S(1)} collective-permute-done((bf16[1152,256]{1,0:T(8,128)(2,1)S(1)}, bf16[1152,256]{1,0:T(8,128)(2,1)S(1)}, u32[]{:S(2)}, u32[]{:S(2)}) %collective-permute-start.14) | collective-permute-done | bytes 589856 | tf_op jit(solution)/shard_map/ppermute | solution.py:42
  410.6 14.3 %shard_map.442 = (bf16[576,256]{1,0:T(8,128)(2,1)S(1)}, bf16[576,256]{1,0:T(8,128)(2,1)S(1)}, bf16[1152,256]{1,0:T(8,128)(2,1)S(1)}, bf16[1152,256]{1,0:T(8,128)...) custom-call(bf16[576,256]{1,0:T(8,128)(2,1)S(1)} %copy-done.56, bf16[576,256]{1,0:T(8,128)(2,1)S(1)} %copy-done.58, ...), custom_call_target="tpu_custom_call" | custom-call | tf_op jit(solution)/shard_map/pallas_call | solution.py:135
  429.7 8.3 %shard_map.446 = bf16[16,288,576]{2,1,0:T(8,128)(2,1)} custom-call(bf16[1152,256]{1,0:T(8,128)(2,1)S(1)} %copy-done.11, bf16[1152,256]{1,0:T(8,128)(2,1)S(1)} %copy-done.15, bf16[576,256]{1,0:T(8,128)(2,1)S(1)} %get-tuple-element.68.refs_0_.refs_2_, bf16[576,256]{1,0:T(8,128)(2,1)S(1)} %get-tuple-element.71.refs_0_.refs_3_, ...), custom_call_target="tpu_custom_call" | custom-call | tf_op jit(solution)/shard_map/pallas_call | solution.py:135
  439.3 12.4 %shard_map.448 = bf16[16,288,1152]{2,1,0:T(8,128)(2,1)} custom-call(bf16[1152,256]{1,0:T(8,128)(2,1)} %add_convert_fusion.3.x_ref.refs_0_, bf16[1152,256]{1,0:T(8,128)(2,1)} %collective-permute-done.7.x_ref.refs_1_, bf16[2304,256]{1,0:T(8,128)(2,1)S(1)} %copy-done.24, bf16[2304,256]{1,0:T(8,128)(2,1)} %copy-done.21, bf16[1152,256]{1,0:T(8,128)(2,1)} %fusion.7.x_ref.refs_4_, ...), custom_call_target="tpu_custom_call" | custom-call | tf_op jit(solution)/shard_map/pallas_call | solution.py:135
  461.1 5.9 collective-permute-start.9
  488.6 7.6 %collective-permute-done.17 = bf16[1152,256]{1,0:T(8,128)(2,1)} collective-permute-done((bf16[1152,256]{1,0:T(8,128)(2,1)S(1)}, bf16[1152,256]{1,0:T(8,128)(2,1)}, u32[]{:S(2)}, u32[]{:S(2)}) %collective-permute-start.17) | collective-permute-done | bytes 589856 | tf_op jit(solution)/shard_map/ppermute | solution.py:42
  498.3 5.8 all-to-all-start.1
  506.9 6.0 collective-permute-start.18
  513.7 19.9 %all-to-all-done.1 = bf16[8,144,256]{2,1,0:T(8,128)(2,1)} async-done(((bf16[8,144,256]{2,1,0:T(8,128)(2,1)}), bf16[8,144,256]{2,1,0:T(8,128)(2,1)}, u32[]{:S(2)}, u32[]{:S(2)}) %all-to-all-start.1) | async-done | bytes 589856 | tf_op jit(solution)/shard_map/all_to_all | solution.py:323
  561.1 8.7 %all-to-all-done.2 = bf16[8,144,256]{2,1,0:T(8,128)(2,1)S(1)} async-done(((bf16[8,144,256]{2,1,0:T(8,128)(2,1)}), bf16[8,144,256]{2,1,0:T(8,128)(2,1)S(1)}, u32[]{:S(2)}, u32[]{:S(2)}) %all-to-all-start.2) | async-done | bytes 589856 | tf_op jit(solution)/shard_map/all_to_all | solution.py:323
  583.2 108.4 %reduce-scatter.8.cloned.1.call-done = bf16[288,1152]{1,0:T(8,128)(2,1)} async-done(((bf16[4608,1152]{1,0:T(8,128)(2,1)}), bf16[288,1152]{1,0:T(8,128)(2,1)}) %reduce-scatter.8.cloned.1.call-update) | async-done | bytes 663568 | tf_op jit(solution)/shard_map/reduce_scatter | solution.py:360
  (529 shorter events, 211.6 us)
Async XLA Ops:
  7.2 138.7 %all-gather.5.cloned.1.call-start = ((), (), s32[]{:S(2)}) async-start(), calls=%async_computation.8 | async-start | bytes 11280384 | tf_op jit(solution)/shard_map/all_gather | solution.py:354
  23.2 243.9 %all-gather.7.cloned.1.call-start = ((), (), s32[]{:S(2)}) async-start(), calls=%async_computation.9 | async-start | bytes 11280384 | tf_op jit(solution)/shard_map/all_gather | solution.py:354
  25.4 546.3 %reduce-scatter.12.cloned.1.call-start = ((), (), s32[]{:S(2)}) async-start(), calls=%async_computation.12 | async-start | bytes 6266880
  111.7 0.9 collective-permute-start
  116.4 34.4 %copy-start.10 = (bf16[1152,256]{1,0:T(8,128)(2,1)}, bf16[1152,256]{1,0:T(8,128)(2,1)S(1)}, u32[]{:S(2)}) copy-start(bf16[1152,256]{1,0:T(8,128)(2,1)S(1)} %fusion.9.x_ref.refs_0_.refs_4_) | copy-start | bytes 1769476
  116.4 55.7 %collective-permute-start.1 = (bf16[1152,256]{1,0:T(8,128)(2,1)S(1)}, bf16[1152,256]{1,0:T(8,128)(2,1)S(1)}, u32[]{:S(2)}, u32[]{:S(2)}) collective-permute-start(bf16[1152,256]{1,0:T(8,128)(2,1)S(1)} %fusion.9.x_ref.refs_0_.refs_4_), channel_id=1, source_target_pairs={{0,1},{1,0},{2,3},{3,2},{4,5},{5,4},{6,7},{7,6},{8,9},{9,8},{10,11... | collective-permute-start | bytes 1769480 | tf_op jit(solution)/shard_map/ppermute | solution.py:42
  155.5 28.9 %collective-permute-start.2 = (bf16[1152,256]{1,0:T(8,128)(2,1)S(1)}, bf16[1152,256]{1,0:T(8,128)(2,1)S(1)}, u32[]{:S(2)}, u32[]{:S(2)}) collective-permute-start(bf16[1152,256]{1,0:T(8,128)(2,1)S(1)} %get-tuple-element.52.refs_2_), channel_id=1, source_target_pairs={{0,8},{8,0},{16,24},{24,16},{1,9},{9,1},{17,25},{25,17},{2,10},{10... | collective-permute-start | bytes 1769480 | tf_op jit(solution)/shard_map/ppermute | solution.py:38
  176.5 7.9 %collective-permute-start.3 = (bf16[1152,256]{1,0:T(8,128)(2,1)S(1)}, bf16[1152,256]{1,0:T(8,128)(2,1)S(1)}, u32[]{:S(2)}, u32[]{:S(2)}) collective-permute-start(bf16[1152,256]{1,0:T(8,128)(2,1)S(1)} %get-tuple-element.53.refs_3_), channel_id=1, source_target_pairs={{0,8},{8,0},{16,24},{24,16},{1,9},{9,1},{17,25},{25,17},{2,10},{10... | collective-permute-start | bytes 1769480 | tf_op jit(solution)/shard_map/ppermute | solution.py:38
  195.1 15.5 %collective-permute-start.4 = (bf16[1152,256]{1,0:T(8,128)(2,1)S(1)}, bf16[1152,256]{1,0:T(8,128)(2,1)S(1)}, u32[]{:S(2)}, u32[]{:S(2)}) collective-permute-start(bf16[1152,256]{1,0:T(8,128)(2,1)S(1)} %shard_map.420), channel_id=1, source_target_pairs={{0,1},{1,0},{2,3},{3,2},{4,5},{5,4},{6,7},{7,6},{8,9},{9,8},{10,11... | collective-permute-start | bytes 1769480 | tf_op jit(solution)/shard_map/ppermute | solution.py:42
  211.9 22.7 %collective-permute-start.5 = (bf16[1152,256]{1,0:T(8,128)(2,1)}, bf16[1152,256]{1,0:T(8,128)(2,1)}, u32[]{:S(2)}, u32[]{:S(2)}) collective-permute-start(bf16[1152,256]{1,0:T(8,128)(2,1)} %fusion.32.x_ref.refs_0_), channel_id=1, source_target_pairs={{0,1},{1,0},{2,3},{3,2},{4,5},{5,4},{6,7},{7,6},{8,9},{9,8},{10,11... | collective-permute-start | bytes 1769480 | tf_op jit(solution)/shard_map/ppermute | solution.py:42
  242.9 14.8 %collective-permute-start.6 = (bf16[1152,256]{1,0:T(8,128)(2,1)}, bf16[1152,256]{1,0:T(8,128)(2,1)}, u32[]{:S(2)}, u32[]{:S(2)}) collective-permute-start(bf16[1152,256]{1,0:T(8,128)(2,1)} %shard_map.426), channel_id=1, source_target_pairs={{0,1},{1,0},{2,3},{3,2},{4,5},{5,4},{6,7},{7,6},{8,9},{9,8},{10,11... | collective-permute-start | bytes 1769480 | tf_op jit(solution)/shard_map/ppermute | solution.py:42
  261.3 16.5 %collective-permute-start.7 = (bf16[1152,256]{1,0:T(8,128)(2,1)}, bf16[1152,256]{1,0:T(8,128)(2,1)}, u32[]{:S(2)}, u32[]{:S(2)}) collective-permute-start(bf16[1152,256]{1,0:T(8,128)(2,1)} %add_convert_fusion.3.x_ref.refs_0_), channel_id=1, source_target_pairs={{0,1},{1,0},{2,3},{3,2},{4,5},{5,4},{6,7},{7,6},{8,9},{9,8},{10,11... | collective-permute-start | bytes 1769480 | tf_op jit(solution)/shard_map/ppermute | solution.py:42
  263.8 24.0 %collective-permute-start.10 = (bf16[1152,256]{1,0:T(8,128)(2,1)}, bf16[1152,256]{1,0:T(8,128)(2,1)}, u32[]{:S(2)}, u32[]{:S(2)}) collective-permute-start(bf16[1152,256]{1,0:T(8,128)(2,1)} %fusion.7.x_ref.refs_4_), channel_id=1, source_target_pairs={{0,1},{1,0},{2,3},{3,2},{4,5},{5,4},{6,7},{7,6},{8,9},{9,8},{10,11... | collective-permute-start | bytes 1769480 | tf_op jit(solution)/shard_map/ppermute | solution.py:42
  286.6 47.6 %copy-start.20 = (bf16[2304,256]{1,0:T(8,128)(2,1)}, bf16[2304,256]{1,0:T(8,128)(2,1)S(1)}, u32[]{:S(2)}) copy-start(bf16[2304,256]{1,0:T(8,128)(2,1)S(1)} %get-tuple-element.59.refs_0_.refs_7_) | copy-start | bytes 3538948
  303.1 38.1 %collective-permute-start.11 = (bf16[1152,256]{1,0:T(8,128)(2,1)S(1)}, bf16[1152,256]{1,0:T(8,128)(2,1)S(1)}, u32[]{:S(2)}, u32[]{:S(2)}) collective-permute-start(bf16[1152,256]{1,0:T(8,128)(2,1)S(1)} %shard_map.434), channel_id=1, source_target_pairs={{0,1},{1,0},{2,3},{3,2},{4,5},{5,4},{6,7},{7,6},{8,9},{9,8},{10,11... | collective-permute-start | bytes 1769480 | tf_op jit(solution)/shard_map/ppermute | solution.py:42
  340.6 12.5 %collective-permute-start.8 = (bf16[1152,256]{1,0:T(8,128)(2,1)S(1)}, bf16[1152,256]{1,0:T(8,128)(2,1)S(1)}, u32[]{:S(2)}, u32[]{:S(2)}) collective-permute-start(bf16[1152,256]{1,0:T(8,128)(2,1)S(1)} %shard_map.430), channel_id=1, source_target_pairs={{0,1},{1,0},{2,3},{3,2},{4,5},{5,4},{6,7},{7,6},{8,9},{9,8},{10,11... | collective-permute-start | bytes 1769480 | tf_op jit(solution)/shard_map/ppermute | solution.py:42
  355.7 11.7 %collective-permute-start.12 = (bf16[1152,256]{1,0:T(8,128)(2,1)S(1)}, bf16[1152,256]{1,0:T(8,128)(2,1)S(1)}, u32[]{:S(2)}, u32[]{:S(2)}) collective-permute-start(bf16[1152,256]{1,0:T(8,128)(2,1)S(1)} %convert_element_type.216.x_ref.refs_6_), channel_id=1, source_target_pairs={{0,1},{1,0},{2,3},{3,2},{4,5},{5,4},{6,7},{7,6},{8,9},{9,8},{10,11... | collective-permute-start | bytes 1769480 | tf_op jit(solution)/shard_map/ppermute | solution.py:42
  381.4 195.2 %reduce-scatter.10.cloned.1.call-start = ((), (), s32[]{:S(2)}) async-start(), calls=%async_computation.11 | async-start | bytes 6266880
  385.8 11.1 %collective-permute-start.13 = (bf16[1152,256]{1,0:T(8,128)(2,1)S(1)}, bf16[1152,256]{1,0:T(8,128)(2,1)S(1)}, u32[]{:S(2)}, u32[]{:S(2)}) collective-permute-start(bf16[1152,256]{1,0:T(8,128)(2,1)S(1)} %shard_map.439), channel_id=1, source_target_pairs={{0,1},{1,0},{2,3},{3,2},{4,5},{5,4},{6,7},{7,6},{8,9},{9,8},{10,11... | collective-permute-start | bytes 1769480 | tf_op jit(solution)/shard_map/ppermute | solution.py:42
  399.4 9.9 %collective-permute-start.14 = (bf16[1152,256]{1,0:T(8,128)(2,1)S(1)}, bf16[1152,256]{1,0:T(8,128)(2,1)S(1)}, u32[]{:S(2)}, u32[]{:S(2)}) collective-permute-start(bf16[1152,256]{1,0:T(8,128)(2,1)S(1)} %multiply_convert_fusion.x_ref.refs_8_), channel_id=1, source_target_pairs={{0,1},{1,0},{2,3},{3,2},{4,5},{5,4},{6,7},{7,6},{8,9},{9,8},{10,11... | collective-permute-start | bytes 1769480 | tf_op jit(solution)/shard_map/ppermute | solution.py:42
  424.9 2.1 collective-permute-start.15
  425.0 2.8 collective-permute-start.16
  438.0 253.6 %reduce-scatter.8.cloned.1.call-start = ((), (), s32[]{:S(2)}) async-start(), calls=%async_computation.10 | async-start | bytes 11280384 | tf_op jit(solution)/shard_map/reduce_scatter | solution.py:360
  457.2 10.3 %collective-permute-start.19 = (bf16[1152,120]{1,0:T(8,128)(2,1)}, bf16[1152,120]{1,0:T(8,128)(2,1)S(1)}, u32[]{:S(2)}, u32[]{:S(2)}) collective-permute-start(bf16[1152,120]{1,0:T(8,128)(2,1)} %shard_map.445), channel_id=1, source_target_pairs={{0,8},{8,0},{16,24},{24,16},{1,9},{9,1},{17,25},{25,17},{2,10},{10... | collective-permute-start | bytes 829448 | tf_op jit(solution)/shard_map/ppermute | solution.py:38
  461.1 37.2 %collective-permute-start.9 = (bf16[1152,256]{1,0:T(8,128)(2,1)}, bf16[1152,256]{1,0:T(8,128)(2,1)}, u32[]{:S(2)}, u32[]{:S(2)}) collective-permute-start(bf16[1152,256]{1,0:T(8,128)(2,1)} %get-tuple-element.109), channel_id=1, source_target_pairs={{0,0},{1,1},{2,8},{3,9},{4,4},{5,5},{6,12},{7,13},{8,2},{9,3},{10,... | collective-permute-start | bytes 1769480 | tf_op jit(solution)/shard_map/ppermute | solution.py:316
  469.3 28.9 %all-to-all-start.3 = ((bf16[8,144,120]{2,1,0:T(8,128)(2,1)}), bf16[8,144,120]{2,1,0:T(8,128)(2,1)S(1)}, u32[]{:S(2)}, u32[]{:S(2)}) async-start(bf16[8,144,120]{2,1,0:T(8,128)(2,1)} %bitcast.33), calls=%async_computation.3 | async-start | bytes 589824 | tf_op jit(solution)/shard_map/all_to_all | solution.py:494
  479.8 16.3 %collective-permute-start.17 = (bf16[1152,256]{1,0:T(8,128)(2,1)S(1)}, bf16[1152,256]{1,0:T(8,128)(2,1)}, u32[]{:S(2)}, u32[]{:S(2)}) collective-permute-start(bf16[1152,256]{1,0:T(8,128)(2,1)S(1)} %shard_map.444), channel_id=1, source_target_pairs={{0,1},{1,0},{2,3},{3,2},{4,5},{5,4},{6,7},{7,6},{8,9},{9,8},{10,11... | collective-permute-start | bytes 1769480 | tf_op jit(solution)/shard_map/ppermute | solution.py:42
  498.3 35.3 %all-to-all-start.1 = ((bf16[8,144,256]{2,1,0:T(8,128)(2,1)}), bf16[8,144,256]{2,1,0:T(8,128)(2,1)}, u32[]{:S(2)}, u32[]{:S(2)}) async-start(bf16[8,144,256]{2,1,0:T(8,128)(2,1)} %bitcast.27), calls=%async_computation.1 | async-start | bytes 1179648 | tf_op jit(solution)/shard_map/all_to_all | solution.py:323
  506.9 39.1 %collective-permute-start.18 = (bf16[1152,256]{1,0:T(8,128)(2,1)}, bf16[1152,256]{1,0:T(8,128)(2,1)}, u32[]{:S(2)}, u32[]{:S(2)}) collective-permute-start(bf16[1152,256]{1,0:T(8,128)(2,1)} %fusion.14), channel_id=1, source_target_pairs={{0,0},{1,1},{2,8},{3,9},{4,4},{5,5},{6,12},{7,13},{8,2},{9,3},{10,... | collective-permute-start | bytes 1769480 | tf_op jit(solution)/shard_map/ppermute | solution.py:316
  533.6 10.8 %all-to-all-start.4 = ((f32[8,1,2448]{2,1,0:T(1,128)}), f32[8,1,2448]{2,1,0:T(1,128)S(1)}, u32[]{:S(2)}, u32[]{:S(2)}) async-start(f32[8,1,2448]{2,1,0:T(1,128)} %reshape.315), calls=%async_computation.4 | async-start | bytes 163840 | tf_op jit(solution)/shard_map/all_to_all | solution.py:511
  546.0 23.8 %all-to-all-start.2 = ((bf16[8,144,256]{2,1,0:T(8,128)(2,1)}), bf16[8,144,256]{2,1,0:T(8,128)(2,1)S(1)}, u32[]{:S(2)}, u32[]{:S(2)}) async-start(bf16[8,144,256]{2,1,0:T(8,128)(2,1)} %bitcast.30), calls=%async_computation.2 | async-start | bytes 1179648 | tf_op jit(solution)/shard_map/all_to_all | solution.py:323
  581.3 112.6 %copy-start.1 = (f32[6,144,1024]{2,1,0:T(8,128)S(1)}, f32[6,144,1024]{2,1,0:T(8,128)}, u32[]{:S(2)}) copy-start(f32[6,144,1024]{2,1,0:T(8,128)} %param.30) | copy-start | bytes 10616836
  (145 other events, 987.9 us)
Sparse Core Ops, SparseCore 0:
  23.3 122.5 all-gather.4
  148.8 90.4 all-gather.6
  381.5 82.3 reduce-scatter.11
  467.6 94.6 reduce-scatter.9
  566.2 125.2 reduce-scatter.7
where the time goes:
time: 709 us; the launch traced here: 701 us
  waiting for transfers between devices  245 us (35%)
  Pallas kernels  164 us (23%)
  local copies, waits for them, and re-layouts  90.4 us (13%)
  blocking collectives  84.5 us (12%)
  starting transfers between devices  58.8 us (8%)
  other arithmetic  35.3 us (5%)
  between operations  16.8 us (2%)
    pallas_call x33, Pallas kernels, call_parts(): pl.pallas_call(kernel, grid=(steps,), in_specs=arg_specs, out_specs=out_s...  164 us
    reduce_scatter x1, waiting for transfers between devices, reduce_weights(): lax.psum_scatter(flat, ('row', 'col'), scatter_dimension=0, tiled=True, a...  108 us
    all_to_all x1, blocking collectives, shards(): blocks = lax.all_to_all(blocks, 'col', 0, 0, tiled=True).reshape(D, -1)  78.9 us
    ppermute x12, waiting for transfers between devices, col_swap(): return lax.ppermute(value, 'col', [(i, i ^ mask) for i in range(cols)])  75.8 us
    unnamed x327, local copies, waits for them, and re-layouts  38 us
    all_to_all x2, waiting for transfers between devices, tokens_out(): blocks = lax.all_to_all(blocks, 'col', 0, 0, tiled=True)  28.7 us
    all_gather x2, waiting for transfers between devices, gather_weights(): lax.all_gather(flat, ('row', 'col'), axis=0, tiled=True, axis_index_group...  26.2 us
    slice x3, local copies, waits for them, and re-layouts, shards(): first_w[:, :, i * feat:j * feat]  18.6 us
  transfers between devices with their start and end apart: 29, of which 16 were waited for; matrix products, arithmetic and copies ran while one was open for 13% of the time, Pallas kernels for 19%

commit v1 on v0

--- a/solution.py
+++ b/solution.py
@@ -167,44 +167,90 @@
     return res[: len(q_parts)], res[len(q_parts) :]
 
 
-def in_kernel(start, size, w_ref, x_ref, bias_ref, *out_refs):
-    value = dot_tn(w_ref[0, :, start : start + size], x_ref[...]) + bias_ref[...]
+class View:
+    def __init__(self, weight, block, indices, start, size):
+        self.weight, self.block, self.indices, self.start, self.size = weight, block, indices, start, size
+
+    def args(self):
+        return [self.weight] * len(self.indices)
+
+    def specs(self):
+        return [pl.BlockSpec((1, D, self.block), lambda z, i=i: (z, 0, i)) for i in self.indices]
+
+    def load(self, refs):
+        if len(refs) == 1:
+            return refs[0][0, :, self.start : self.start + self.size]
+        value = jnp.concatenate([ref[0] for ref in refs], axis=1)
+        return value[:, self.start : self.start + self.size]
+
+
+def view_of(weight, start, size):
+    lanes = weight.shape[2]
+    best = None
+    for block in range(128, lanes, 128):
+        first, last = start // block, (start + size - 1) // block
+        if (last + 1) * block > lanes and block * (last + 1) - lanes >= 128:
+            continue
+        cost = (block * (last - first + 1), last - first)
+        if last - first < 2 and (best is None or cost < best[0]):
+            best = (cost, block, list(range(first, last + 1)), start - first * block)
+    if best is None:
+        return View(weight, lanes, [0], start, size)
+    return View(weight, best[1], best[2], best[3], size)
+
+
+def store_rows(value, refs):
     first = 0
-    for ref in out_refs:
+    for ref in refs:
         ref[...] = value[first : first + ref.shape[0]].astype(ref.dtype)
         first += ref.shape[0]
 
 
-def gelu_kernel(start, size, w_ref, x_ref, bias_ref, hidden_ref, slope_ref):
-    v = dot_tn(w_ref[0, :, start : start + size], x_ref[...]) + bias_ref[...]
+def in_kernel(view, n_x, *refs):
+    n = len(view.indices)
+    w, x_refs, bias_ref, out_refs = view.load(refs[:n]), refs[n : n + n_x], refs[n + n_x], refs[n + n_x + 1 :]
+    store_rows(dot_tn(w, x_refs[0][...]) + bias_ref[...], out_refs)
+
+
+def gelu_kernel(view, n_x, *refs):
+    n = len(view.indices)
+    w, x_refs, bias_ref, out_refs = view.load(refs[:n]), refs[n : n + n_x], refs[n + n_x], refs[n + n_x + 1 :]
+    x = jnp.concatenate([ref[...] for ref in x_refs], axis=1)
+    v = dot_tn(w, x) + bias_ref[...]
     square = v * v
     t = jnp.tanh(0.7978845608 * (v + 0.044715 * square * v))
-    hidden_ref[...] = (0.5 * v * (1.0 + t)).astype(BF)
-    slope_ref[...] = 0.5 * (1.0 + t) + 0.5 * v * (1.0 - t * t) * 0.7978845608 * (1.0 + 3.0 * 0.044715 * square)
-
-
-def slope_kernel(start, size, w_ref, x_ref, slope_ref, grad_ref, sum_ref):
-    grad = (dot_tn(w_ref[0, :, start : start + size], x_ref[...]) * slope_ref[...]).astype(BF)
-    grad_ref[...] = grad
-    sum_ref[...] = jnp.sum(grad.astype(F32), axis=1, keepdims=True)
-
-
-def apply_in(kernel, weight, span, value, extra, outs):
-    half = weight.shape[0]
-    args = [weight, value, extra]
-    specs = [part_spec(weight.shape, half), whole_spec(value.shape), part_spec(extra.shape, half)]
+    hidden = 0.5 * v * (1.0 + t)
+    slope = 0.5 * (1.0 + t) + 0.5 * v * (1.0 - t * t) * 0.7978845608 * (1.0 + 3.0 * 0.044715 * square)
+    put(out_refs[:n_x], slice(None), hidden)
+    out_refs[n_x][...] = slope
+
+
+def slope_kernel(view, n_x, *refs):
+    n = len(view.indices)
+    w, x_refs, slope_ref, out_refs = view.load(refs[:n]), refs[n : n + n_x], refs[n + n_x], refs[n + n_x + 1 :]
+    x = jnp.concatenate([ref[...] for ref in x_refs], axis=1)
+    grad = (dot_tn(w, x) * slope_ref[...]).astype(BF)
+    put(out_refs[:n_x], slice(None), grad)
+    out_refs[n_x][...] = jnp.sum(grad.astype(F32), axis=1, keepdims=True)
+
+
+def apply_in(kernel, view, values, extra, outs):
+    half = view.weight.shape[0]
+    args = view.args() + list(values) + [extra]
+    specs = view.specs() + [whole_spec(v.shape) for v in values] + [part_spec(extra.shape, half)]
     outs = [jax.ShapeDtypeStruct((rows, cols), dtype) for rows, cols, dtype in outs]
-    kernel = functools.partial(kernel, span[0], span[1])
+    kernel = functools.partial(kernel, view, len(values))
     return call_parts(kernel, half, args, specs, outs, [part_spec(o.shape, half) for o in outs])
 
 
-def out_kernel(start, w_ref, *refs):
-    v_refs, out_ref, acc_ref = refs[:-2], refs[-2], refs[-1]
+def out_kernel(view, *refs):
+    n = len(view.indices)
+    w, v_refs, out_ref, acc_ref = view.load(refs[:n]), refs[n:-2], refs[-2], refs[-1]
     z = pl.program_id(0)
-    total = None
+    total, start = None, 0
     for v_ref in v_refs:
         end = start + v_ref.shape[0]
-        part = dot_nn(w_ref[0, :, start:end], v_ref[...])
+        part = dot_nn(w[:, start:end], v_ref[...])
         total = part if total is None else total + part
         start = end
 
@@ -221,20 +267,46 @@
         out_ref[...] = acc_ref[...].astype(out_ref.dtype)
 
 
-def apply_out(weight, start, values, dtype):
-    half = weight.shape[0]
+def apply_out(view, values, dtype):
+    half = view.weight.shape[0]
     tokens = values[0].shape[1]
-    args = [weight] + list(values)
     out = jax.ShapeDtypeStruct((D, tokens), dtype)
     return call_parts(
-        functools.partial(out_kernel, start),
+        functools.partial(out_kernel, view),
         half,
-        args,
-        [part_spec(a.shape, half) for a in args],
+        view.args() + list(values),
+        view.specs() + [part_spec(v.shape, half) for v in values],
         out,
         whole_spec(out.shape),
         [pltpu.VMEM((D, tokens), F32)],
     )
+
+
+def pack_kernel(*refs):
+    out_ref, start = refs[-1], 0
+    for ref in refs[:-1]:
+        end = start + ref.shape[0]
+        out_ref[:, start:end] = ref[...].T
+        start = end
+
+
+def unpack_kernel(in_ref, *out_refs):
+    start = 0
+    for ref in out_refs:
+        end = start + ref.shape[0]
+        ref[...] = in_ref[:, start:end].astype(F32).T
+        start = end
+
+
+def pack(parts):
+    out = jax.ShapeDtypeStruct((parts[0].shape[1], sum(p.shape[0] for p in parts)), BF)
+    specs = [whole_spec(p.shape) for p in parts]
+    return call_parts(pack_kernel, 1, parts, specs, out, whole_spec(out.shape))
+
+
+def unpack(value, sizes):
+    outs = [jax.ShapeDtypeStruct((n, value.shape[0]), F32) for n in sizes]
+    return call_parts(unpack_kernel, 1, [value], [whole_spec(value.shape)], outs, [whole_spec(o.shape) for o in outs])
 
 
 def outer_kernel(terms, *refs):
@@ -263,7 +335,7 @@
     out = jax.ShapeDtypeStruct((half * rows, chunk, sum(sizes)), BF)
     out_spec = pl.BlockSpec((rows, chunk, sum(sizes)), lambda z: (z, 0, 0))
     kernel = functools.partial(outer_kernel, [len(a) for a, _ in pairs])
-    return call_parts(kernel, half, args, specs, out, out_spec), sizes
+    return call_parts(kernel, half, args, specs, out, out_spec)
 
 
 def shards(
@@ -327,10 +399,15 @@
     def gather_pair(value):
         return [value, col_swap(value, cols, 1)]
 
-    def reduce_pair(weight, start, *values):
-        other = apply_out(weight, start, [v[1] for v in values], BF)
+    def reduce_pair(view, *values, cover=None):
+        other = apply_out(view, [v[1] for v in values], BF)
         received = col_swap(other, cols, 1)
-        return apply_out(weight, start, [v[0] for v in values], F32) + received.astype(F32)
+        own = [v[0] for v in values]
+        covered = None
+        if cover is not None:
+            covered = cover(other)
+            own[0] = after(own[0], covered)
+        return apply_out(view, own, F32) + received.astype(F32), covered
 
     def gather_keys(parts):
         parts = list(parts) + [row_swap(p, rows, 1) for p in parts]
@@ -349,25 +426,18 @@
 
     groups = [[i * cols + 2 * z + y for z in range(half) for i in range(rows)] for y in range(2)]
 
-    def gather_weights(shards_w):
-        flat = jnp.concatenate(shards_w, axis=1)
+    def gather_weights(flat):
         full = lax.all_gather(flat, ("row", "col"), axis=0, tiled=True, axis_index_groups=groups)
         return full.reshape(half, D, flat.shape[1])
 
-    def reduce_weights(pairs):
-        blocks, sizes = outer_blocks(pairs, rows, half)
-        flat = blocks.reshape(half * D, sum(sizes))
-        own = lax.psum_scatter(flat, ("row", "col"), scatter_dimension=0, tiled=True, axis_index_groups=groups)
-        out, start = [], 0
-        for size in sizes:
-            out.append(own[:, start : start + size].astype(F32))
-            start += size
-        return out
+    def scatter(blocks):
+        flat = blocks.reshape(half * D, blocks.shape[2])
+        return lax.psum_scatter(flat, ("row", "col"), scatter_dimension=0, tiled=True, axis_index_groups=groups)
 
     first_w = gather_weights(
-        [query_weight, key_weight, value_weight, out_weight.T, cross_query, cross_key, cross_value, cross_out.T]
-    )
-    second_w = gather_weights([up_weight, down_weight.T])
+        pack([query_weight.T, key_weight.T, value_weight.T, out_weight, cross_query.T, cross_key.T, cross_value.T, cross_out])
+    )
+    second_w = gather_weights(jnp.concatenate([up_weight, down_weight.T], axis=1))
 
     step_ids = jnp.arange(steps, dtype=jnp.int32)
     onehot = (time_index[:, 0][:, None] == step_ids[None, :]).astype(F32)
@@ -421,8 +491,9 @@
     cot = arrived[:, width:head].astype(F32)
     heads_w, hidden_w = half * feat, half * ups
     qkv_w, out_w, cq_w, ckv_w, cout_w = (
-        first_w[:, :, i * feat : j * feat] for i, j in ((0, 3), (3, 4), (4, 5), (5, 7), (7, 8))
-    )
+        view_of(first_w, i * feat, (j - i) * feat) for i, j in ((0, 3), (3, 4), (4, 5), (5, 7), (7, 8))
+    )
+    up_w, down_w = view_of(second_w, 0, ups), view_of(second_w, ups, ups)
 
     def columns(*parts):
         return jnp.stack([p.reshape(half, feat) for p in parts], axis=1).reshape(-1, 1)
@@ -430,7 +501,7 @@
     def heads_in(weight, value, *biases):
         sizes = [1] if len(biases) == 1 else [1, len(biases) - 1]
         outs = [(n * heads_w, value.shape[1], BF) for n in sizes]
-        return apply_in(in_kernel, weight, (0, len(biases) * feat), value, columns(*biases), outs)
+        return apply_in(in_kernel, weight, [value], columns(*biases), outs)
 
     none = jnp.zeros((heads_w,), F32)
     normed_a, inv_a = layer_norm(resid)
@@ -438,40 +509,38 @@
     q_parts, kv_parts = zip(*(heads_in(qkv_w, p, q_b, none, v_b) for p in attn_full))
     kv_all = gather_keys(kv_parts)
     att, lse = attend_forward(q_parts, kv_all, None, half)
-    branch_a = reduce_pair(out_w, 0, att) + out_b
+    branch_a = reduce_pair(out_w, att)[0] + out_b
     after_attn = resid + gate_a * branch_a
     cross_full = gather_pair(after_attn.astype(BF))
     cq_parts = [heads_in(cq_w, p, cq_b)[0] for p in cross_full]
-    ckv = apply_in(in_kernel, ckv_w, (0, 2 * feat), text_t, columns(none, cv_b), [(2 * heads_w, texts, BF)])
+    ckv = apply_in(in_kernel, ckv_w, [text_t], columns(none, cv_b), [(2 * heads_w, texts, BF)])
     catt, clse = attend_forward(cq_parts, ckv, length, half)
-    after_cross = after_attn + reduce_pair(cout_w, 0, catt) + cout_b
+    after_cross = after_attn + reduce_pair(cout_w, catt)[0] + cout_b
     normed_m, inv_m = layer_norm(after_cross)
     mlp_full = gather_pair((normed_m * (1.0 + scale_m) + shift_m).astype(BF))
-    hidden_outs = [(hidden_w, width, BF), (hidden_w, width, F32)]
-    hidden, slope = zip(*(apply_in(gelu_kernel, second_w, (0, ups), p, up_b, hidden_outs) for p in mlp_full))
-    branch_m = reduce_pair(second_w, ups, hidden) + down_b
+    hidden_outs = [(hidden_w, width, BF)] * 2
+    *hidden, slope = apply_in(gelu_kernel, up_w, mlp_full, up_b, hidden_outs + [(hidden_w, 2 * width, F32)])
+    branch_m = reduce_pair(down_w, hidden)[0] + down_b
     block_output = tokens_out(after_cross + gate_m * branch_m)
 
     grad_mlp = gate_m * cot
     low_full = gather_pair(grad_mlp.astype(BF))
     g_down_b = jnp.sum(grad_mlp, axis=1)
     g_gate_m = jnp.sum(cot * branch_m, axis=1)
-    pre_outs = [(hidden_w, width, BF), (hidden_w, 1, F32)]
-    grad_pre, pre_sums = zip(
-        *(apply_in(slope_kernel, second_w, (ups, ups), p, d, pre_outs) for p, d in zip(low_full, slope))
-    )
-    g_up_b = pre_sums[0] + pre_sums[1]
-    back_in = reduce_pair(second_w, 0, grad_pre)
-    g_up, g_down = reduce_weights([(mlp_full, grad_pre), (low_full, hidden)])
+    *grad_pre, g_up_b = apply_in(slope_kernel, down_w, low_full, slope, hidden_outs + [(hidden_w, 1, F32)])
+
+    def mlp_cover(other):
+        return outer_blocks([(mlp_full, grad_pre), (low_full, [after(hidden[0], other), hidden[1]])], rows, half)
+
+    back_in, mlp_blocks = reduce_pair(up_w, grad_pre, cover=mlp_cover)
+    mlp_grads = scatter(mlp_blocks)
     back_m, g_shift_m, g_scale_m = norm_backward(back_in, normed_m, inv_m, scale_m)
     grad_cross = cot + back_m
     g_cout_b = jnp.sum(grad_cross, axis=1)
     low_cross = gather_pair(grad_cross.astype(BF))
     dcatt = [heads_in(cout_w, p, none)[0] for p in low_cross]
     dcq, dckv = attend_backward(cq_parts, ckv, length, clse, dcatt, half)
-    grad_res = grad_cross + reduce_pair(cq_w, 0, dcq)
-    g_cq, g_ckv, g_cout = reduce_weights([(cross_full, dcq), ([text_t], dckv), (low_cross, catt)])
-    g_ck, g_cv = g_ckv[:, :feat], g_ckv[:, feat:]
+    grad_res = grad_cross + reduce_pair(cq_w, dcq)[0]
     g_cq_b = jnp.sum(sum(p.astype(F32) for p in dcq), axis=1)
     g_cv_b = jnp.sum(dckv[0].astype(F32).reshape(half, 2, feat, texts)[:, 1], axis=2)
     g_gate_a = jnp.sum(grad_res * branch_a, axis=1)
@@ -481,14 +550,20 @@
     datt = [heads_in(out_w, p, none)[0] for p in low_attn]
     dq, dkv = attend_backward(q_parts, kv_all, None, lse, datt, half)
     dkv = reduce_keys(dkv)
-    back_att = reduce_pair(qkv_w, 0, dq, dkv)
-    g_q, g_kv, g_out = reduce_weights([(attn_full, dq), (attn_full, dkv), (low_attn, att)])
-    g_k, g_v = g_kv[:, :feat], g_kv[:, feat:]
+
+    def attention_cover(other):
+        pairs = [(attn_full, dq), (attn_full, dkv), (low_attn, att), (cross_full, dcq), ([text_t], dckv), (low_cross, catt)]
+        return outer_blocks([(pairs[0][0], [after(dq[0], other), dq[1]])] + pairs[1:], rows, half)
+
+    back_att, att_blocks = reduce_pair(qkv_w, dq, dkv, cover=attention_cover)
+    att_grads = scatter(att_blocks)
+    g_q, g_k, g_v, g_out, g_cq, g_ck, g_cv, g_cout = unpack(att_grads, [feat] * 8)
+    g_up, g_down = mlp_grads[:, :ups].astype(F32), mlp_grads[:, ups:].astype(F32)
     g_q_b = jnp.sum(sum(p.astype(F32) for p in dq), axis=1)
     g_v_b = jnp.sum(sum(p.astype(F32) for p in dkv).reshape(half, 2, feat, width)[:, 1], axis=2)
     back_a, g_shift_a, g_scale_a = norm_backward(back_att, normed_a, inv_a, scale_a)
     grad_input = tokens_out(grad_res + back_a)
-    grad_text = apply_out(ckv_w, 0, dckv, BF)
+    grad_text = apply_out(ckv_w, dckv, BF)
     grad_text = grad_text.astype(F32) + row_swap(grad_text, rows, 1).astype(F32)
     grad_text = jnp.where(at_home, grad_text, 0.0).astype(BF).reshape(cols, feat, texts)
     grad_text = lax.all_to_all(grad_text, "col", 0, 0, tiled=True)
@@ -534,19 +609,19 @@
         grad_text,
         g_shift,
         g_time,
-        g_q,
-        g_k,
-        g_v,
+        g_q.T,
+        g_k.T,
+        g_v.T,
         g_q_b,
         g_v_b,
-        g_out.T,
+        g_out,
         g_out_b,
-        g_cq,
-        g_ck,
-        g_cv,
+        g_cq.T,
+        g_ck.T,
+        g_cv.T,
         g_cq_b,
         g_cv_b,
-        g_cout.T,
+        g_cout,
         g_cout_b,
         g_up,
         g_up_b,

time: 709 us -> 583 us (0.82)
  waiting for transfers between devices: 245 us -> 140 us
  local copies, waits for them, and re-layouts: 90.4 us -> 52.2 us
  Pallas kernels: 164 us -> 179 us
    reduce_scatter x1 -> x2, waiting for transfers between devices: 108 us -> 7.8 us  [scatter(): lax.psum_scatter(flat, ('row', 'col'), scatter_dimension=0, tiled=True, a...]
    slice x10 -> x1, local copies, waits for them, and re-layouts: 25.8 us -> 0.04 us  [the longest x3 18.6 us: shards(): first_w[:, :, i * feat:j * feat]]
    unnamed x327 -> x255, local copies, waits for them, and re-layouts: 38 us -> 22.8 us
    pallas_call x33 -> x32, Pallas kernels: 164 us -> 179 us  [call_parts(): pl.pallas_call(kernel, grid=(steps,), in_specs=arg_specs, out_specs=out_s...]
    ppermute x12, waiting for transfers between devices: 75.8 us -> 63.4 us  [col_swap(): return lax.ppermute(value, 'col', [(i, i ^ mask) for i in range(cols)])]
    all_to_all x1, waiting for transfers between devices: 3.22 us -> 13.8 us  [shards(): small_g = lax.all_to_all(small_g, 'col', 0, 0, tiled=True)]
  transfers between devices with their start and end apart: 29 -> 28, of which waited for: 16 -> 17; matrix products, arithmetic and copies ran while one was open for 13% -> 12% of each run, Pallas kernels for 19% -> 26%
where the time goes in v1:
time: 583 us; the launch traced here: 575 us
  Pallas kernels  179 us (31%)
  waiting for transfers between devices  140 us (24%)
  blocking collectives  84.4 us (14%)
  starting transfers between devices  65.1 us (11%)
  local copies, waits for them, and re-layouts  52.2 us (9%)
  other arithmetic  31.9 us (5%)
  between operations  16.4 us (3%)
    pallas_call x32, Pallas kernels, call_parts(): pl.pallas_call(kernel, grid=(steps,), in_specs=arg_specs, out_specs=out_s...  179 us
    all_to_all x1, blocking collectives, shards(): blocks = lax.all_to_all(blocks, 'col', 0, 0, tiled=True).reshape(D, -1)  78.9 us
    ppermute x12, waiting for transfers between devices, col_swap(): return lax.ppermute(value, 'col', [(i, i ^ mask) for i in range(cols)])  63.4 us
    all_to_all x2, waiting for transfers between devices, tokens_out(): blocks = lax.all_to_all(blocks, 'col', 0, 0, tiled=True)  26 us
    all_gather x2, waiting for transfers between devices, gather_weights(): lax.all_gather(flat, ('row', 'col'), axis=0, tiled=True, axis_index_group...  24 us
    unnamed x255, local copies, waits for them, and re-layouts  22.8 us
    ppermute x5, starting transfers between devices, row_swap(): return lax.ppermute(value, 'row', [(i, i ^ bit) for i in range(rows)])  18.7 us
    ppermute x12, starting transfers between devices, col_swap(): return lax.ppermute(value, 'col', [(i, i ^ mask) for i in range(cols)])  16.2 us
  transfers between devices with their start and end apart: 28, of which 17 were waited for; matrix products, arithmetic and copies ran while one was open for 12% of the time, Pallas kernels for 26%

profile of v1, /device:TPU:0, one launch (start us, length us, event | category | flops | bytes accessed | tf_op | source)
XLA Modules:
  0.0 575.0 jit_solution(4339015151695947579)
XLA Ops:
  24.8 78.9 %all_to_all.25 = bf16[8,144,686]{2,1,0:T(8,128)(2,1)S(1)} all-to-all(bf16[8,144,686]{2,1,0:T(8,128)(2,1)S(1)} %pad_maximum_fusion), channel_id=1, replica_groups=mesh['row'=4,'col'=8] {'col'}, dimensions={0} | all-to-all | bytes 3161088 | tf_op jit(solution)/shard_map/all_to_all | solution.py:465
  115.1 24.0 %all-gather.5.cloned.1.call-done = bf16[4608,1152]{1,0:T(8,128)(2,1)} async-done(((bf16[288,1152]{1,0:T(8,128)(2,1)}), bf16[4608,1152]{1,0:T(8,128)(2,1)}) %all-gather.5.cloned.1.call-update) | async-done | bytes 10616848 | tf_op jit(solution)/shard_map/all_gather | solution.py:430
  143.6 4.5 shard_map.418
  148.1 17.8 %collective-permute-start.3 = (bf16[1152,256]{1,0:T(8,128)(2,1)S(1)}, bf16[1152,256]{1,0:T(8,128)(2,1)S(1)}, u32[]{:S(2)}, u32[]{:S(2)}) collective-permute-start(bf16[1152,256]{1,0:T(8,128)(2,1)S(1)} %get-tuple-element.63.refs_3_), channel_id=1, source_target_pairs={{0,8},{8,0},{16,24},{24,16},{1,9},{9,1},{17,25},{25,17},{2,10},{10... | collective-permute-start | bytes 1769480 | tf_op jit(solution)/shard_map/ppermute | solution.py:38
  168.4 8.9 %shard_map.419 = (bf16[576,256]{1,0:T(8,128)(2,1)S(1)}, bf16[576,256]{1,0:T(8,128)(2,1)S(1)}, f32[4,512,2]{2,1,0:T(8,128)}) custom-call(bf16[576,256]{1,0:T(8,128)(2,1)S(1)} %get-tuple-element.60.refs_0_, bf16[576,256]{1,0:T(8,128)(2,1)S(1)} %get-tuple-element.61.refs_1_, bf16[1152,256]{1,0:T(8,128)(2,1)S(1)} %get-tuple-element.62.refs_2_, ...), custom_call_target="tpu_custom_call" | custom-call | tf_op jit(solution)/shard_map/pallas_call | solution.py:135
  186.6 10.3 %collective-permute-done.4 = bf16[1152,256]{1,0:T(8,128)(2,1)S(1)} collective-permute-done((bf16[1152,256]{1,0:T(8,128)(2,1)S(1)}, bf16[1152,256]{1,0:T(8,128)(2,1)S(1)}, u32[]{:S(2)}, u32[]{:S(2)}) %collective-permute-start.4) | collective-permute-done | bytes 589856 | tf_op jit(solution)/shard_map/ppermute | solution.py:42
  205.4 5.1 shard_map.424.refs_3_
  232.5 8.4 %collective-permute-done.6 = bf16[1152,256]{1,0:T(8,128)(2,1)} collective-permute-done((bf16[1152,256]{1,0:T(8,128)(2,1)S(1)}, bf16[1152,256]{1,0:T(8,128)(2,1)}, u32[]{:S(2)}, u32[]{:S(2)}) %collective-permute-start.6) | collective-permute-done | bytes 589856 | tf_op jit(solution)/shard_map/ppermute | solution.py:42
  248.9 11.2 %collective-permute-done.7.refs_2_.refs_1_ = bf16[1152,256]{1,0:T(8,128)(2,1)} collective-permute-done((bf16[1152,256]{1,0:T(8,128)(2,1)S(1)}, bf16[1152,256]{1,0:T(8,128)(2,1)}, u32[]{:S(2)}, u32[]{:S(2)}) %collective-permute-start.7) | collective-permute-done | bytes 589856 | tf_op jit(solution)/shard_map/ppermute | solution.py:42
  260.1 10.2 %shard_map.428 = (bf16[2304,256]{1,0:T(8,128)(2,1)S(1)}, bf16[2304,256]{1,0:T(8,128)(2,1)S(1)}, f32[2304,512]{1,0:T(8,128)}) custom-call(bf16[4,1152,1152]{2,1,0:T(8,128)(2,1)} %bitcast.158, bf16[1152,256]{1,0:T(8,128)(2,1)S(1)} %add_convert_fusion.3.refs_1_.refs_0_, bf16[1152,256]{1,0:T(8,128)(2,1)} %collective-permute-done.7.refs_2_.refs_1_, ...), custom_call_target="tpu_custom_call" | custom-call | tf_op jit(solution)/shard_map/pallas_call | solution.py:135
  272.3 9.8 %shard_map.431 = (bf16[2304,256]{1,0:T(8,128)(2,1)S(1)}, bf16[2304,256]{1,0:T(8,128)(2,1)S(1)}, f32[2304,1]{1,0:T(8,128)}) custom-call(bf16[4,1152,1152]{2,1,0:T(8,128)(2,1)} %bitcast.159, bf16[4,1152,1152]{2,1,0:T(8,128)(2,1)} %bitcast.160, bf16[1152,256]{1,0:T(8,128)(2,1)S(1)} %fusion.7.refs_2_.refs_4_, ...), custom_call_target="tpu_custom_call" | custom-call | tf_op jit(solution)/shard_map/pallas_call | solution.py:135
  282.1 6.0 %shard_map.432 = bf16[1152,256]{1,0:T(8,128)(2,1)S(1)} custom-call(bf16[4,1152,1152]{2,1,0:T(8,128)(2,1)} %bitcast.161, bf16[2304,256]{1,0:T(8,128)(2,1)S(1)} %get-tuple-element.72.refs_1_.refs_3_), custom_call_target="tpu_custom_call" | custom-call | tf_op jit(solution)/shard_map/pallas_call | solution.py:135
  288.1 11.9 %shard_map.433 = bf16[16,288,1152]{2,1,0:T(8,128)(2,1)} custom-call(bf16[1152,256]{1,0:T(8,128)(2,1)S(1)} %add_convert_fusion.3.refs_1_.refs_0_, bf16[1152,256]{1,0:T(8,128)(2,1)} %collective-permute-done.7.refs_2_.refs_1_, bf16[2304,256]{1,0:T(8,128)(2,1)S(1)} %get-tuple-element.74.refs_2_.refs_1_, bf16[2304,256]{1,0:T(8,128)(2,1)} %copy-done.13, ...), custom_call_target="tpu_custom_call" | custom-call | tf_op jit(solution)/shard_map/pallas_call | solution.py:135
  302.0 5.8 %shard_map.430 = bf16[1152,256]{1,0:T(8,128)(2,1)S(1)} custom-call(bf16[4,1152,1152]{2,1,0:T(8,128)(2,1)} %bitcast.162, bf16[4,1152,1152]{2,1,0:T(8,128)(2,1)} %bitcast.163, bf16[2304,256]{1,0:T(8,128)(2,1)S(1)} %copy-done.10), custom_call_target="tpu_custom_call" | custom-call | tf_op jit(solution)/shard_map/pallas_call | solution.py:135
  307.8 6.1 %shard_map.429 = f32[1152,256]{1,0:T(8,128)S(1)} custom-call(bf16[4,1152,1152]{2,1,0:T(8,128)(2,1)} %bitcast.164, bf16[4,1152,1152]{2,1,0:T(8,128)(2,1)} %bitcast.165, bf16[2304,256]{1,0:T(8,128)(2,1)S(1)} %copy-done.8), custom_call_target="tpu_custom_call" | custom-call | tf_op jit(solution)/shard_map/pallas_call | solution.py:135
  314.0 5.6 shard_map.434
  322.5 8.0 %collective-permute-done.8 = bf16[1152,256]{1,0:T(8,128)(2,1)S(1)} collective-permute-done((bf16[1152,256]{1,0:T(8,128)(2,1)S(1)}, bf16[1152,256]{1,0:T(8,128)(2,1)S(1)}, u32[]{:S(2)}, u32[]{:S(2)}) %collective-permute-start.8) | collective-permute-done | bytes 589856 | tf_op jit(solution)/shard_map/ppermute | solution.py:42
  347.2 5.3 shard_map.437
  361.5 7.7 %collective-permute-done.13 = bf16[1152,256]{1,0:T(8,128)(2,1)S(1)} collective-permute-done((bf16[1152,256]{1,0:T(8,128)(2,1)S(1)}, bf16[1152,256]{1,0:T(8,128)(2,1)S(1)}, u32[]{:S(2)}, u32[]{:S(2)}) %collective-permute-start.13) | collective-permute-done | bytes 589856 | tf_op jit(solution)/shard_map/ppermute | solution.py:42
  385.0 14.1 %shard_map.442 = (bf16[576,256]{1,0:T(8,128)(2,1)S(1)}, bf16[576,256]{1,0:T(8,128)(2,1)S(1)}, bf16[1152,256]{1,0:T(8,128)(2,1)S(1)}, bf16[1152,256]{1,0:T(8,128)...) custom-call(bf16[576,256]{1,0:T(8,128)(2,1)S(1)} %copy-done.31, bf16[576,256]{1,0:T(8,128)(2,1)S(1)} %copy-done.33, ...), custom_call_target="tpu_custom_call" | custom-call | tf_op jit(solution)/shard_map/pallas_call | solution.py:135
  403.5 6.1 %shard_map.443 = bf16[1152,256]{1,0:T(8,128)(2,1)} custom-call(bf16[4,1152,1152]{2,1,0:T(8,128)(2,1)} %bitcast.155, bf16[576,256]{1,0:T(8,128)(2,1)S(1)} %get-tuple-element.80.refs_1_.refs_3_, bf16[1152,256]{1,0:T(8,128)(2,1)S(1)} %get-tuple-element.123.refs_2_.refs_7_), custom_call_target="tpu_custom_call" | custom-call | tf_op jit(solution)/shard_map/pallas_call | solution.py:135
  409.7 13.3 %shard_map.444 = bf16[16,288,1152]{2,1,0:T(8,128)(2,1)} custom-call(bf16[1152,256]{1,0:T(8,128)(2,1)S(1)} %fusion.9.refs_1_.refs_0_.refs_4_, bf16[1152,256]{1,0:T(8,128)(2,1)S(1)} %collective-permute-done.1.refs_1_.refs_5_, bf16[576,256]{1,0:T(8,128)(2,1)S(1)} %get-tuple-element.87.refs_2_.refs_1_, bf16[576,256]{1,0:T(8,128)(2,1)S(1)} %get-tuple-element.80.refs_1_.refs_3_, ...), custom_call_target="tpu_custom_call" | custom-call | tf_op jit(solution)/shard_map/pallas_call | solution.py:135
  431.2 6.0 %collective-permute-start.9 = (bf16[1152,256]{1,0:T(8,128)(2,1)}, bf16[1152,256]{1,0:T(8,128)(2,1)}, u32[]{:S(2)}, u32[]{:S(2)}) collective-permute-start(bf16[1152,256]{1,0:T(8,128)(2,1)} %get-tuple-element.126), channel_id=1, source_target_pairs={{0,0},{1,1},{2,8},{3,9},{4,4},{5,5},{6,12},{7,13},{8,2},{9,3},{10,... | collective-permute-start | bytes 1769480 | tf_op jit(solution)/shard_map/ppermute | solution.py:388
  447.6 5.3 shard_map.445
  452.9 9.2 %collective-permute-done.17 = bf16[1152,256]{1,0:T(8,128)(2,1)S(1)} collective-permute-done((bf16[1152,256]{1,0:T(8,128)(2,1)}, bf16[1152,256]{1,0:T(8,128)(2,1)S(1)}, u32[]{:S(2)}, u32[]{:S(2)}) %collective-permute-start.17) | collective-permute-done | bytes 589856 | tf_op jit(solution)/shard_map/ppermute | solution.py:42
  464.2 4.6 all-to-all-start.1
  480.4 5.9 %collective-permute-start.18 = (bf16[1152,256]{1,0:T(8,128)(2,1)}, bf16[1152,256]{1,0:T(8,128)(2,1)}, u32[]{:S(2)}, u32[]{:S(2)}) collective-permute-start(bf16[1152,256]{1,0:T(8,128)(2,1)} %fusion.14), channel_id=1, source_target_pairs={{0,0},{1,1},{2,8},{3,9},{4,4},{5,5},{6,12},{7,13},{8,2},{9,3},{10,... | collective-permute-start | bytes 1769480 | tf_op jit(solution)/shard_map/ppermute | solution.py:388
  487.2 12.9 %all-to-all-done.1 = bf16[8,144,256]{2,1,0:T(8,128)(2,1)S(1)} async-done(((bf16[8,144,256]{2,1,0:T(8,128)(2,1)}), bf16[8,144,256]{2,1,0:T(8,128)(2,1)S(1)}, u32[]{:S(2)}, u32[]{:S(2)}) %all-to-all-start.1) | async-done | bytes 589856 | tf_op jit(solution)/shard_map/all_to_all | solution.py:395
  507.6 13.8 %all-to-all-done.4 = f32[8,1,2448]{2,1,0:T(1,128)S(1)} async-done(((f32[8,1,2448]{2,1,0:T(1,128)}), f32[8,1,2448]{2,1,0:T(1,128)S(1)}, u32[]{:S(2)}, u32[]{:S(2)}) %all-to-all-start.4) | async-done | bytes 78368 | tf_op jit(solution)/shard_map/all_to_all | solution.py:586
  526.6 5.5 all-gather.1
  537.9 13.0 %all-to-all-done.2 = bf16[8,144,256]{2,1,0:T(8,128)(2,1)S(1)} async-done(((bf16[8,144,256]{2,1,0:T(8,128)(2,1)}), bf16[8,144,256]{2,1,0:T(8,128)(2,1)S(1)}, u32[]{:S(2)}, u32[]{:S(2)}) %all-to-all-start.2) | async-done | bytes 589856 | tf_op jit(solution)/shard_map/all_to_all | solution.py:395
  557.6 7.8 %reduce-scatter.3.cloned.1.call-done.in_ref = bf16[288,1152]{1,0:T(8,128)(2,1)} async-done(((bf16[4608,1152]{1,0:T(8,128)(2,1)}), bf16[288,1152]{1,0:T(8,128)(2,1)}) %reduce-scatter.3.cloned.1.call-update) | async-done | bytes 663568 | tf_op jit(solution)/shard_map/reduce_scatter | solution.py:435
  (440 shorter events, 195.5 us)
Async XLA Ops:
  7.2 131.8 %all-gather.5.cloned.1.call-start = ((), (), s32[]{:S(2)}) async-start(), calls=%async_computation.7 | async-start | bytes 11280384 | tf_op jit(solution)/shard_map/all_gather | solution.py:430
  16.2 232.7 %all-gather.7.cloned.1.call-start = ((), (), s32[]{:S(2)}) async-start(), calls=%async_computation.8 | async-start | bytes 11280384 | tf_op jit(solution)/shard_map/all_gather | solution.py:430
  18.4 536.8 %reduce-scatter.5.cloned.1.call-start = ((), (), s32[]{:S(2)}) async-start(), calls=%async_computation.10 | async-start | bytes 11280384 | tf_op jit(solution)/shard_map/reduce_scatter | solution.py:435
  105.8 2.1 collective-permute-start
  109.6 87.3 %copy-start.54 = (bf16[1152,256]{1,0:T(8,128)(2,1)}, bf16[1152,256]{1,0:T(8,128)(2,1)S(1)}, u32[]{:S(2)}) copy-start(bf16[1152,256]{1,0:T(8,128)(2,1)S(1)} %copy.147) | copy-start | bytes 1769476
  111.7 31.8 %collective-permute-start.1 = (bf16[1152,256]{1,0:T(8,128)(2,1)S(1)}, bf16[1152,256]{1,0:T(8,128)(2,1)S(1)}, u32[]{:S(2)}, u32[]{:S(2)}) collective-permute-start(bf16[1152,256]{1,0:T(8,128)(2,1)S(1)} %fusion.9.refs_1_.refs_0_.refs_4_), channel_id=1, source_target_pairs={{0,1},{1,0},{2,3},{3,2},{4,5},{5,4},{6,7},{7,6},{8,9},{9,8},{10,11... | collective-permute-start | bytes 1769480 | tf_op jit(solution)/shard_map/ppermute | solution.py:42
  113.3 30.2 %copy-start.81 = (f32[8,1,144]{2,0,1:T(8,128)}, f32[8,1,144]{2,0,1:T(8,128)S(1)}, u32[]{:S(2)}) copy-start(f32[8,1,144]{2,0,1:T(8,128)S(1)} %slice_bitcast_fusion.2) | copy-start | bytes 13828
  113.3 30.2 %copy-start.83 = (f32[8,1,144]{2,0,1:T(8,128)}, f32[8,1,144]{2,0,1:T(8,128)S(1)}, u32[]{:S(2)}) copy-start(f32[8,1,144]{2,0,1:T(8,128)S(1)} %slice_bitcast_fusion.3) | copy-start | bytes 13828
  113.4 30.1 %copy-start.85 = (f32[8,1,144]{2,0,1:T(8,128)}, f32[8,1,144]{2,0,1:T(8,128)S(1)}, u32[]{:S(2)}) copy-start(f32[8,1,144]{2,0,1:T(8,128)S(1)} %slice_bitcast_fusion) | copy-start | bytes 13828
  148.1 19.4 %collective-permute-start.3 = (bf16[1152,256]{1,0:T(8,128)(2,1)S(1)}, bf16[1152,256]{1,0:T(8,128)(2,1)S(1)}, u32[]{:S(2)}, u32[]{:S(2)}) collective-permute-start(bf16[1152,256]{1,0:T(8,128)(2,1)S(1)} %get-tuple-element.63.refs_3_), channel_id=1, source_target_pairs={{0,8},{8,0},{16,24},{24,16},{1,9},{9,1},{17,25},{25,17},{2,10},{10... | collective-permute-start | bytes 1769480 | tf_op jit(solution)/shard_map/ppermute | solution.py:38
  165.9 2.5 collective-permute-start.2
  181.2 15.7 %collective-permute-start.4 = (bf16[1152,256]{1,0:T(8,128)(2,1)S(1)}, bf16[1152,256]{1,0:T(8,128)(2,1)S(1)}, u32[]{:S(2)}, u32[]{:S(2)}) collective-permute-start(bf16[1152,256]{1,0:T(8,128)(2,1)S(1)} %shard_map.421), channel_id=1, source_target_pairs={{0,1},{1,0},{2,3},{3,2},{4,5},{5,4},{6,7},{7,6},{8,9},{9,8},{10,11... | collective-permute-start | bytes 1769480 | tf_op jit(solution)/shard_map/ppermute | solution.py:42
  197.7 16.9 %collective-permute-start.5 = (bf16[1152,256]{1,0:T(8,128)(2,1)S(1)}, bf16[1152,256]{1,0:T(8,128)(2,1)}, u32[]{:S(2)}, u32[]{:S(2)}) collective-permute-start(bf16[1152,256]{1,0:T(8,128)(2,1)S(1)} %fusion.32.refs_1_.refs_12_), channel_id=1, source_target_pairs={{0,1},{1,0},{2,3},{3,2},{4,5},{5,4},{6,7},{7,6},{8,9},{9,8},{10,11... | collective-permute-start | bytes 1769480 | tf_op jit(solution)/shard_map/ppermute | solution.py:42
  226.1 14.8 %collective-permute-start.6 = (bf16[1152,256]{1,0:T(8,128)(2,1)S(1)}, bf16[1152,256]{1,0:T(8,128)(2,1)}, u32[]{:S(2)}, u32[]{:S(2)}) collective-permute-start(bf16[1152,256]{1,0:T(8,128)(2,1)S(1)} %shard_map.427), channel_id=1, source_target_pairs={{0,1},{1,0},{2,3},{3,2},{4,5},{5,4},{6,7},{7,6},{8,9},{9,8},{10,11... | collective-permute-start | bytes 1769480 | tf_op jit(solution)/shard_map/ppermute | solution.py:42
  243.7 16.4 %collective-permute-start.7 = (bf16[1152,256]{1,0:T(8,128)(2,1)S(1)}, bf16[1152,256]{1,0:T(8,128)(2,1)}, u32[]{:S(2)}, u32[]{:S(2)}) collective-permute-start(bf16[1152,256]{1,0:T(8,128)(2,1)S(1)} %add_convert_fusion.3.refs_1_.refs_0_), channel_id=1, source_target_pairs={{0,1},{1,0},{2,3},{3,2},{4,5},{5,4},{6,7},{7,6},{8,9},{9,8},{10,11... | collective-permute-start | bytes 1769480 | tf_op jit(solution)/shard_map/ppermute | solution.py:42
  244.5 27.8 %collective-permute-start.10 = (bf16[1152,256]{1,0:T(8,128)(2,1)S(1)}, bf16[1152,256]{1,0:T(8,128)(2,1)}, u32[]{:S(2)}, u32[]{:S(2)}) collective-permute-start(bf16[1152,256]{1,0:T(8,128)(2,1)S(1)} %fusion.7.refs_2_.refs_4_), channel_id=1, source_target_pairs={{0,1},{1,0},{2,3},{3,2},{4,5},{5,4},{6,7},{7,6},{8,9},{9,8},{10,11... | collective-permute-start | bytes 1769480 | tf_op jit(solution)/shard_map/ppermute | solution.py:42
  300.1 265.3 %reduce-scatter.3.cloned.1.call-start = ((), (), s32[]{:S(2)}) async-start(), calls=%async_computation.9 | async-start | bytes 11280384 | tf_op jit(solution)/shard_map/reduce_scatter | solution.py:435
  300.2 21.0 %collective-permute-start.11 = (bf16[1152,256]{1,0:T(8,128)(2,1)}, bf16[1152,256]{1,0:T(8,128)(2,1)S(1)}, u32[]{:S(2)}, u32[]{:S(2)}) collective-permute-start(bf16[1152,256]{1,0:T(8,128)(2,1)} %copy-done.45), channel_id=1, source_target_pairs={{0,1},{1,0},{2,3},{3,2},{4,5},{5,4},{6,7},{7,6},{8,9},{9,8},{10,11... | collective-permute-start | bytes 1769480 | tf_op jit(solution)/shard_map/ppermute | solution.py:42
  319.6 10.8 %collective-permute-start.8 = (bf16[1152,256]{1,0:T(8,128)(2,1)S(1)}, bf16[1152,256]{1,0:T(8,128)(2,1)S(1)}, u32[]{:S(2)}, u32[]{:S(2)}) collective-permute-start(bf16[1152,256]{1,0:T(8,128)(2,1)S(1)} %shard_map.430), channel_id=1, source_target_pairs={{0,1},{1,0},{2,3},{3,2},{4,5},{5,4},{6,7},{7,6},{8,9},{9,8},{10,11... | collective-permute-start | bytes 1769480 | tf_op jit(solution)/shard_map/ppermute | solution.py:42
  333.1 9.9 %collective-permute-start.12 = (bf16[1152,256]{1,0:T(8,128)(2,1)S(1)}, bf16[1152,256]{1,0:T(8,128)(2,1)S(1)}, u32[]{:S(2)}, u32[]{:S(2)}) collective-permute-start(bf16[1152,256]{1,0:T(8,128)(2,1)S(1)} %convert_element_type.202.refs_2_.refs_18_), channel_id=1, source_target_pairs={{0,1},{1,0},{2,3},{3,2},{4,5},{5,4},{6,7},{7,6},{8,9},{9,8},{10,11... | collective-permute-start | bytes 1769480 | tf_op jit(solution)/shard_map/ppermute | solution.py:42
  356.2 13.0 %collective-permute-start.13 = (bf16[1152,256]{1,0:T(8,128)(2,1)S(1)}, bf16[1152,256]{1,0:T(8,128)(2,1)S(1)}, u32[]{:S(2)}, u32[]{:S(2)}) collective-permute-start(bf16[1152,256]{1,0:T(8,128)(2,1)S(1)} %shard_map.439), channel_id=1, source_target_pairs={{0,1},{1,0},{2,3},{3,2},{4,5},{5,4},{6,7},{7,6},{8,9},{9,8},{10,11... | collective-permute-start | bytes 1769480 | tf_op jit(solution)/shard_map/ppermute | solution.py:42
  370.9 9.9 %collective-permute-start.14 = (bf16[1152,256]{1,0:T(8,128)(2,1)S(1)}, bf16[1152,256]{1,0:T(8,128)(2,1)S(1)}, u32[]{:S(2)}, u32[]{:S(2)}) collective-permute-start(bf16[1152,256]{1,0:T(8,128)(2,1)S(1)} %multiply_convert_fusion.refs_2_.refs_8_), channel_id=1, source_target_pairs={{0,1},{1,0},{2,3},{3,2},{4,5},{5,4},{6,7},{7,6},{8,9},{9,8},{10,11... | collective-permute-start | bytes 1769480 | tf_op jit(solution)/shard_map/ppermute | solution.py:42
  399.1 2.1 collective-permute-start.15
  399.1 2.8 collective-permute-start.16
  427.5 10.1 %collective-permute-start.19 = (bf16[1152,120]{1,0:T(8,128)(2,1)S(1)}, bf16[1152,120]{1,0:T(8,128)(2,1)S(1)}, u32[]{:S(2)}, u32[]{:S(2)}) collective-permute-start(bf16[1152,120]{1,0:T(8,128)(2,1)S(1)} %shard_map.446), channel_id=1, source_target_pairs={{0,8},{8,0},{16,24},{24,16},{1,9},{9,1},{17,25},{25,17},{2,10},{10... | collective-permute-start | bytes 829448 | tf_op jit(solution)/shard_map/ppermute | solution.py:38
  431.2 33.0 %collective-permute-start.9 = (bf16[1152,256]{1,0:T(8,128)(2,1)}, bf16[1152,256]{1,0:T(8,128)(2,1)}, u32[]{:S(2)}, u32[]{:S(2)}) collective-permute-start(bf16[1152,256]{1,0:T(8,128)(2,1)} %get-tuple-element.126), channel_id=1, source_target_pairs={{0,0},{1,1},{2,8},{3,9},{4,4},{5,5},{6,12},{7,13},{8,2},{9,3},{10,... | collective-permute-start | bytes 1769480 | tf_op jit(solution)/shard_map/ppermute | solution.py:388
  438.5 25.8 %all-to-all-start.3 = ((bf16[8,144,120]{2,1,0:T(8,128)(2,1)}), bf16[8,144,120]{2,1,0:T(8,128)(2,1)}, u32[]{:S(2)}, u32[]{:S(2)}) async-start(bf16[8,144,120]{2,1,0:T(8,128)(2,1)} %bitcast.37), calls=%async_computation.3 | async-start | bytes 589824 | tf_op jit(solution)/shard_map/all_to_all | solution.py:569
  444.1 17.9 %collective-permute-start.17 = (bf16[1152,256]{1,0:T(8,128)(2,1)}, bf16[1152,256]{1,0:T(8,128)(2,1)S(1)}, u32[]{:S(2)}, u32[]{:S(2)}) collective-permute-start(bf16[1152,256]{1,0:T(8,128)(2,1)} %shard_map.443), channel_id=1, source_target_pairs={{0,1},{1,0},{2,3},{3,2},{4,5},{5,4},{6,7},{7,6},{8,9},{9,8},{10,11... | collective-permute-start | bytes 1769480 | tf_op jit(solution)/shard_map/ppermute | solution.py:42
  464.2 35.9 %all-to-all-start.1 = ((bf16[8,144,256]{2,1,0:T(8,128)(2,1)}), bf16[8,144,256]{2,1,0:T(8,128)(2,1)S(1)}, u32[]{:S(2)}, u32[]{:S(2)}) async-start(bf16[8,144,256]{2,1,0:T(8,128)(2,1)} %bitcast.31), calls=%async_computation.1 | async-start | bytes 1179648 | tf_op jit(solution)/shard_map/all_to_all | solution.py:395
  480.4 42.5 %collective-permute-start.18 = (bf16[1152,256]{1,0:T(8,128)(2,1)}, bf16[1152,256]{1,0:T(8,128)(2,1)}, u32[]{:S(2)}, u32[]{:S(2)}) collective-permute-start(bf16[1152,256]{1,0:T(8,128)(2,1)} %fusion.14), channel_id=1, source_target_pairs={{0,0},{1,1},{2,8},{3,9},{4,4},{5,5},{6,12},{7,13},{8,2},{9,3},{10,... | collective-permute-start | bytes 1769480 | tf_op jit(solution)/shard_map/ppermute | solution.py:388
  500.2 21.3 %all-to-all-start.4 = ((f32[8,1,2448]{2,1,0:T(1,128)}), f32[8,1,2448]{2,1,0:T(1,128)S(1)}, u32[]{:S(2)}, u32[]{:S(2)}) async-start(f32[8,1,2448]{2,1,0:T(1,128)} %reshape.307), calls=%async_computation.4 | async-start | bytes 163840 | tf_op jit(solution)/shard_map/all_to_all | solution.py:586
  523.0 27.9 %all-to-all-start.2 = ((bf16[8,144,256]{2,1,0:T(8,128)(2,1)}), bf16[8,144,256]{2,1,0:T(8,128)(2,1)S(1)}, u32[]{:S(2)}, u32[]{:S(2)}) async-start(bf16[8,144,256]{2,1,0:T(8,128)(2,1)} %bitcast.34), calls=%async_computation.2 | async-start | bytes 1179648 | tf_op jit(solution)/shard_map/all_to_all | solution.py:395
  (116 other events, 775.1 us)
Sparse Core Ops, SparseCore 0:
  16.3 122.7 all-gather.4
  141.9 89.7 all-gather.6
  300.2 120.2 reduce-scatter.4
  424.4 140.9 reduce-scatter.2

commit v2 on v1

--- a/solution.py
+++ b/solution.py
@@ -377,15 +377,31 @@
     at_home = core == low_z
 
     kv_masks = [1 << b for b in range(2, cols.bit_length() - 2)]
-    swap_pairs = []
-    for i in range(rows):
-        for j in range(cols):
-            swap_pairs.append(
-                (i * cols + j, ((i & ~1) | ((j >> 1) & 1)) * cols + ((j & ~2) | ((i & 1) << 1)))
-            )
+    def home_of(i, j):
+        return (i & ~1) | ((j >> 1) & 1), (j & ~2) | ((i & 1) << 1)
+
+    home_r, home_c = home_of(r, c)
 
     def place_swap(value):
-        return lax.ppermute(value, ("row", "col"), swap_pairs)
+        pairs = []
+        for i in range(rows):
+            for j in range(cols):
+                to_r, to_c = home_of(i, j)
+                pairs.append((i * cols + j, to_r * cols + to_c))
+        return lax.ppermute(value, ("row", "col"), pairs)
+
+    def send_tokens(blocks):
+        full = jnp.zeros_like(blocks)
+        for e in range(cols):
+            pairs = []
+            for i in range(rows):
+                for j in range(cols):
+                    to_r, to_c = home_of(i, j ^ e)
+                    pairs.append((i * cols + j, to_r * cols + to_c))
+            part = lax.dynamic_slice_in_dim(blocks, c ^ e, 1, 0)
+            part = lax.ppermute(part, ("row", "col"), pairs)
+            full = lax.dynamic_update_slice_in_dim(full, part, home_c ^ e, 0)
+        return full.reshape(D, blocks.shape[2])
 
     def token_blocks(value):
         return value.reshape(2, feat, half, width).transpose(0, 2, 1, 3).reshape(cols, feat, width)
@@ -461,10 +477,9 @@
     extra = jnp.concatenate(
         [text_tokens.transpose(0, 2, 1)] + [p.astype(BF) for p in (small_high, small_mid, small_low)], axis=2
     )
-    blocks = jnp.concatenate([token_blocks(block_input), token_blocks(out_grad), jnp.repeat(extra, half, axis=0)], axis=2)
-    blocks = lax.all_to_all(blocks, "col", 0, 0, tiled=True).reshape(D, -1)
-    arrived = place_swap(blocks)
-    small_n, head = small.shape[2], 2 * width
+    arrived = send_tokens(jnp.concatenate([token_blocks(block_input), jnp.repeat(extra, half, axis=0)], axis=2))
+    cot_low = send_tokens(token_blocks(after(out_grad, arrived)))
+    small_n, head = small.shape[2], width
 
     def small_of(value):
         parts = [value[:, head + texts + i * small_n : head + texts + (i + 1) * small_n].astype(F32) for i in range(3)]
@@ -488,7 +503,7 @@
     text_t = arrived[:, head : head + texts]
 
     resid = arrived[:, :width].astype(F32)
-    cot = arrived[:, width:head].astype(F32)
+    cot = cot_low.astype(F32)
     heads_w, hidden_w = half * feat, half * ups
     qkv_w, out_w, cq_w, ckv_w, cout_w = (
         view_of(first_w, i * feat, (j - i) * feat) for i, j in ((0, 3), (3, 4), (4, 5), (5, 7), (7, 8))

time: 583 us -> 579 us (level)
  blocking collectives: 84.4 us -> 5.65 us
  waiting for transfers between devices: 140 us -> 191 us
  starting transfers between devices: 65.1 us -> 85.2 us
    all_to_all x1 -> x0, blocking collectives: 78.9 us -> none  [shards(): blocks = lax.all_to_all(blocks, 'col', 0, 0, tiled=True).reshape(D, -1)]
    ppermute x3 -> x18, starting transfers between devices: 14 us -> 50.8 us  [the longest x16 38.5 us: send_tokens(): part = lax.ppermute(part, ('row', 'col'), pairs)]
    ppermute x3 -> x18, waiting for transfers between devices: 0.01 us -> 31.5 us  [the longest x16 31.5 us: send_tokens(): part = lax.ppermute(part, ('row', 'col'), pairs)]
    all_gather x2, waiting for transfers between devices: 24 us -> 47.5 us  [gather_weights(): lax.all_gather(flat, ('row', 'col'), axis=0, tiled=True, axis_index_group...]
    ppermute x5, starting transfers between devices: 18.7 us -> 1.46 us  [row_swap(): return lax.ppermute(value, 'row', [(i, i ^ bit) for i in range(rows)])]
    all_to_all x1, waiting for transfers between devices: 13.8 us -> 6.89 us  [shards(): small_g = lax.all_to_all(small_g, 'col', 0, 0, tiled=True)]
    ppermute x12, waiting for transfers between devices: 63.4 us -> 69.3 us  [col_swap(): return lax.ppermute(value, 'col', [(i, i ^ mask) for i in range(cols)])]
    unnamed x255 -> x254, local copies, waits for them, and re-layouts: 22.8 us -> 18.6 us
  transfers between devices with their start and end apart: 28 -> 43, of which waited for: 17 -> 25; matrix products, arithmetic and copies ran while one was open for 12% -> 13% of each run, Pallas kernels for 26% -> 26%
where the time goes in v2:
time: 579 us; the launch traced here: 572 us
  waiting for transfers between devices  191 us (33%)
  Pallas kernels  179 us (31%)
  starting transfers between devices  85.2 us (15%)
  local copies, waits for them, and re-layouts  52.1 us (9%)
  other arithmetic  35.7 us (6%)
  between operations  16.8 us (3%)
  matrix products  5.79 us (1%)
    pallas_call x32, Pallas kernels, call_parts(): pl.pallas_call(kernel, grid=(steps,), in_specs=arg_specs, out_specs=out_s...  179 us
    ppermute x12, waiting for transfers between devices, col_swap(): return lax.ppermute(value, 'col', [(i, i ^ mask) for i in range(cols)])  69.3 us
    all_gather x2, waiting for transfers between devices, gather_weights(): lax.all_gather(flat, ('row', 'col'), axis=0, tiled=True, axis_index_group...  47.5 us
    ppermute x16, starting transfers between devices, send_tokens(): part = lax.ppermute(part, ('row', 'col'), pairs)  38.5 us
    ppermute x16, waiting for transfers between devices, send_tokens(): part = lax.ppermute(part, ('row', 'col'), pairs)  31.5 us
    all_to_all x2, waiting for transfers between devices, tokens_out(): blocks = lax.all_to_all(blocks, 'col', 0, 0, tiled=True)  24.7 us
    unnamed x254, local copies, waits for them, and re-layouts  18.6 us
    ppermute x12, starting transfers between devices, col_swap(): return lax.ppermute(value, 'col', [(i, i ^ mask) for i in range(cols)])  16.4 us
  transfers between devices with their start and end apart: 43, of which 25 were waited for; matrix products, arithmetic and copies ran while one was open for 13% of the time, Pallas kernels for 26%

profile of v2, /device:TPU:0, one launch (start us, length us, event | category | flops | bytes accessed | tf_op | source)
XLA Modules:
  0.0 571.7 jit_solution(5561733260122056425)
XLA Ops:
  34.2 13.9 %collective-permute-start.6 = (bf16[1,144,430]{2,1,0:T(8,128)(2,1)S(1)}, bf16[1,144,430]{2,1,0:T(8,128)(2,1)S(1)}, u32[]{:S(2)}, u32[]{:S(2)}) collective-permute-start(bf16[1,144,430]{2,1,0:T(8,128)(2,1)S(1)} %get-tuple-element.136), channel_id=1, source_target_pairs={{0,12},{1,13},{2,4},{3,5},{4,8},{5,9},{6,0},{7,1},{8,14},{9,15},{1... | collective-permute-start | bytes 371528 | tf_op jit(solution)/shard_map/ppermute | solution.py:402
  61.7 9.1 %collective-permute-done.6 = bf16[1,144,430]{2,1,0:T(8,128)(2,1)S(1)} collective-permute-done((bf16[1,144,430]{2,1,0:T(8,128)(2,1)S(1)}, bf16[1,144,430]{2,1,0:T(8,128)(2,1)S(1)}, u32[]{:S(2)}, u32[]{:S(2)}) %collective-permute-start.6) | collective-permute-done | bytes 123872 | tf_op jit(solution)/shard_map/ppermute | solution.py:402
  80.3 47.5 %all-gather.5.cloned.1.call-done = bf16[4608,1152]{1,0:T(8,128)(2,1)} async-done(((bf16[288,1152]{1,0:T(8,128)(2,1)}), bf16[4608,1152]{1,0:T(8,128)(2,1)}) %all-gather.5.cloned.1.call-update) | async-done | bytes 10616848 | tf_op jit(solution)/shard_map/all_gather | solution.py:446
  139.6 8.9 %shard_map.419 = (bf16[576,256]{1,0:T(8,128)(2,1)S(1)}, bf16[576,256]{1,0:T(8,128)(2,1)S(1)}, f32[4,512,2]{2,1,0:T(8,128)}) custom-call(bf16[576,256]{1,0:T(8,128)(2,1)S(1)} %get-tuple-element.61.refs_0_, bf16[576,256]{1,0:T(8,128)(2,1)S(1)} %get-tuple-element.62.refs_1_, bf16[1152,256]{1,0:T(8,128)(2,1)S(1)} %get-tuple-element.63.refs_2_, ...), custom_call_target="tpu_custom_call" | custom-call | tf_op jit(solution)/shard_map/pallas_call | solution.py:135
  157.8 10.2 %collective-permute-done.11 = bf16[1152,256]{1,0:T(8,128)(2,1)S(1)} collective-permute-done((bf16[1152,256]{1,0:T(8,128)(2,1)S(1)}, bf16[1152,256]{1,0:T(8,128)(2,1)S(1)}, u32[]{:S(2)}, u32[]{:S(2)}) %collective-permute-start.11) | collective-permute-done | bytes 589856 | tf_op jit(solution)/shard_map/ppermute | solution.py:42
  188.4 5.2 shard_map.424.refs_3_
  211.3 8.5 %collective-permute-done.24 = bf16[1,144,256]{2,1,0:T(8,128)(2,1)S(1)} collective-permute-done((bf16[1,144,256]{2,1,0:T(8,128)(2,1)S(1)}, bf16[1,144,256]{2,1,0:T(8,128)(2,1)S(1)}, u32[]{:S(2)}, u32[]{:S(2)}) %collective-permute-start.24) | collective-permute-done | bytes 73760 | tf_op jit(solution)/shard_map/ppermute | solution.py:402
  233.4 10.1 %collective-permute-done.14.refs_2_.refs_1_ = bf16[1152,256]{1,0:T(8,128)(2,1)} collective-permute-done((bf16[1152,256]{1,0:T(8,128)(2,1)S(1)}, bf16[1152,256]{1,0:T(8,128)(2,1)}, u32[]{:S(2)}, u32[]{:S(2)}) %collective-permute-start.14) | collective-permute-done | bytes 589856 | tf_op jit(solution)/shard_map/ppermute | solution.py:42
  243.5 9.7 %shard_map.428 = (bf16[2304,256]{1,0:T(8,128)(2,1)S(1)}, bf16[2304,256]{1,0:T(8,128)(2,1)S(1)}, f32[2304,512]{1,0:T(8,128)}) custom-call(bf16[4,1152,1152]{2,1,0:T(8,128)(2,1)} %bitcast.162, bf16[1152,256]{1,0:T(8,128)(2,1)S(1)} %add_convert_fusion.3.refs_1_.refs_0_, bf16[1152,256]{1,0:T(8,128)(2,1)} %collective-permute-done.14.refs_2_.refs_1_, ...), custom_call_target="tpu_custom_call" | custom-call | tf_op jit(solution)/shard_map/pallas_call | solution.py:135
  256.1 9.8 %shard_map.431 = (bf16[2304,256]{1,0:T(8,128)(2,1)S(1)}, bf16[2304,256]{1,0:T(8,128)(2,1)S(1)}, f32[2304,1]{1,0:T(8,128)}) custom-call(bf16[4,1152,1152]{2,1,0:T(8,128)(2,1)} %bitcast.163, bf16[4,1152,1152]{2,1,0:T(8,128)(2,1)} %bitcast.164, bf16[1152,256]{1,0:T(8,128)(2,1)S(1)} %fusion.16.refs_2_.refs_4_, ...), custom_call_target="tpu_custom_call" | custom-call | tf_op jit(solution)/shard_map/pallas_call | solution.py:135
  265.9 6.0 %shard_map.432 = bf16[1152,256]{1,0:T(8,128)(2,1)S(1)} custom-call(bf16[4,1152,1152]{2,1,0:T(8,128)(2,1)} %bitcast.165, bf16[2304,256]{1,0:T(8,128)(2,1)S(1)} %get-tuple-element.74.refs_1_.refs_3_), custom_call_target="tpu_custom_call" | custom-call | tf_op jit(solution)/shard_map/pallas_call | solution.py:135
  272.0 11.9 %shard_map.433 = bf16[16,288,1152]{2,1,0:T(8,128)(2,1)} custom-call(bf16[1152,256]{1,0:T(8,128)(2,1)S(1)} %add_convert_fusion.3.refs_1_.refs_0_, bf16[1152,256]{1,0:T(8,128)(2,1)} %collective-permute-done.14.refs_2_.refs_1_, bf16[2304,256]{1,0:T(8,128)(2,1)S(1)} %get-tuple-element.76.refs_2_.refs_1_, bf16[2304,256]{1,0:T(8,128)(2,1)} %copy-done.13, ...), custom_call_target="tpu_custom_call" | custom-call | tf_op jit(solution)/shard_map/pallas_call | solution.py:135
  285.6 5.7 %shard_map.430 = bf16[1152,256]{1,0:T(8,128)(2,1)S(1)} custom-call(bf16[4,1152,1152]{2,1,0:T(8,128)(2,1)} %bitcast.166, bf16[4,1152,1152]{2,1,0:T(8,128)(2,1)} %bitcast.167, bf16[2304,256]{1,0:T(8,128)(2,1)S(1)} %copy-done.10), custom_call_target="tpu_custom_call" | custom-call | tf_op jit(solution)/shard_map/pallas_call | solution.py:135
  291.3 6.1 %shard_map.429 = f32[1152,256]{1,0:T(8,128)S(1)} custom-call(bf16[4,1152,1152]{2,1,0:T(8,128)(2,1)} %bitcast.168, bf16[4,1152,1152]{2,1,0:T(8,128)(2,1)} %bitcast.169, bf16[2304,256]{1,0:T(8,128)(2,1)S(1)} %copy-done.8), custom_call_target="tpu_custom_call" | custom-call | tf_op jit(solution)/shard_map/pallas_call | solution.py:135
  297.5 5.6 shard_map.434
  306.6 12.3 %collective-permute-done.15 = bf16[1152,256]{1,0:T(8,128)(2,1)S(1)} collective-permute-done((bf16[1152,256]{1,0:T(8,128)(2,1)S(1)}, bf16[1152,256]{1,0:T(8,128)(2,1)S(1)}, u32[]{:S(2)}, u32[]{:S(2)}) %collective-permute-start.15) | collective-permute-done | bytes 589856 | tf_op jit(solution)/shard_map/ppermute | solution.py:42
  327.9 9.7 %collective-permute-done.27.refs_2_.refs_19_ = bf16[1152,256]{1,0:T(8,128)(2,1)S(1)} collective-permute-done((bf16[1152,256]{1,0:T(8,128)(2,1)S(1)}, bf16[1152,256]{1,0:T(8,128)(2,1)S(1)}, u32[]{:S(2)}, u32[]{:S(2)}) %collective-permute-start.27) | collective-permute-done | bytes 589856 | tf_op jit(solution)/shard_map/ppermute | solution.py:42
  341.7 5.3 shard_map.437
  356.3 9.4 %collective-permute-done.28 = bf16[1152,256]{1,0:T(8,128)(2,1)S(1)} collective-permute-done((bf16[1152,256]{1,0:T(8,128)(2,1)S(1)}, bf16[1152,256]{1,0:T(8,128)(2,1)S(1)}, u32[]{:S(2)}, u32[]{:S(2)}) %collective-permute-start.28) | collective-permute-done | bytes 589856 | tf_op jit(solution)/shard_map/ppermute | solution.py:42
  372.8 8.7 %collective-permute-done.29.refs_2_.refs_9_ = bf16[1152,256]{1,0:T(8,128)(2,1)S(1)} collective-permute-done((bf16[1152,256]{1,0:T(8,128)(2,1)S(1)}, bf16[1152,256]{1,0:T(8,128)(2,1)S(1)}, u32[]{:S(2)}, u32[]{:S(2)}) %collective-permute-start.29) | collective-permute-done | bytes 589856 | tf_op jit(solution)/shard_map/ppermute | solution.py:42
  385.6 14.1 %shard_map.442 = (bf16[576,256]{1,0:T(8,128)(2,1)S(1)}, bf16[576,256]{1,0:T(8,128)(2,1)S(1)}, bf16[1152,256]{1,0:T(8,128)(2,1)S(1)}, bf16[1152,256]{1,0:T(8,128)...) custom-call(bf16[576,256]{1,0:T(8,128)(2,1)S(1)} %copy-done.31, bf16[576,256]{1,0:T(8,128)(2,1)S(1)} %copy-done.33, ...), custom_call_target="tpu_custom_call" | custom-call | tf_op jit(solution)/shard_map/pallas_call | solution.py:135
  404.2 6.1 %shard_map.443 = bf16[1152,256]{1,0:T(8,128)(2,1)} custom-call(bf16[4,1152,1152]{2,1,0:T(8,128)(2,1)} %bitcast.159, bf16[576,256]{1,0:T(8,128)(2,1)S(1)} %get-tuple-element.82.refs_1_.refs_3_, bf16[1152,256]{1,0:T(8,128)(2,1)S(1)} %get-tuple-element.123.refs_2_.refs_7_), custom_call_target="tpu_custom_call" | custom-call | tf_op jit(solution)/shard_map/pallas_call | solution.py:135
  410.4 13.2 %shard_map.444 = bf16[16,288,1152]{2,1,0:T(8,128)(2,1)} custom-call(bf16[1152,256]{1,0:T(8,128)(2,1)S(1)} %fusion.7.refs_1_.refs_0_.refs_4_, bf16[1152,256]{1,0:T(8,128)(2,1)S(1)} %collective-permute-done.8.refs_1_.refs_5_, bf16[576,256]{1,0:T(8,128)(2,1)S(1)} %get-tuple-element.89.refs_2_.refs_1_, bf16[576,256]{1,0:T(8,128)(2,1)S(1)} %get-tuple-element.82.refs_1_.refs_3_, ...), custom_call_target="tpu_custom_call" | custom-call | tf_op jit(solution)/shard_map/pallas_call | solution.py:135
  437.3 6.0 %collective-permute-start.16 = (bf16[1152,256]{1,0:T(8,128)(2,1)}, bf16[1152,256]{1,0:T(8,128)(2,1)}, u32[]{:S(2)}, u32[]{:S(2)}) collective-permute-start(bf16[1152,256]{1,0:T(8,128)(2,1)} %get-tuple-element.127), channel_id=1, source_target_pairs={{0,0},{1,1},{2,8},{3,9},{4,4},{5,5},{6,12},{7,13},{8,2},{9,3},{10,... | collective-permute-start | bytes 1769480 | tf_op jit(solution)/shard_map/ppermute | solution.py:391
  454.6 5.6 shard_map.445
  460.8 5.7 collective-permute-done.32
  485.4 6.2 %collective-permute-start.33 = (bf16[1152,256]{1,0:T(8,128)(2,1)}, bf16[1152,256]{1,0:T(8,128)(2,1)}, u32[]{:S(2)}, u32[]{:S(2)}) collective-permute-start(bf16[1152,256]{1,0:T(8,128)(2,1)} %fusion.12), channel_id=1, source_target_pairs={{0,0},{1,1},{2,8},{3,9},{4,4},{5,5},{6,12},{7,13},{8,2},{9,3},{10,... | collective-permute-start | bytes 1769480 | tf_op jit(solution)/shard_map/ppermute | solution.py:391
  492.4 12.0 %all-to-all-done = bf16[8,144,256]{2,1,0:T(8,128)(2,1)} async-done(((bf16[8,144,256]{2,1,0:T(8,128)(2,1)}), bf16[8,144,256]{2,1,0:T(8,128)(2,1)}, u32[]{:S(2)}, u32[]{:S(2)}) %all-to-all-start) | async-done | bytes 589856 | tf_op jit(solution)/shard_map/all_to_all | solution.py:411
  512.6 6.9 %all-to-all-done.3 = f32[8,1,2448]{2,1,0:T(1,128)S(1)} async-done(((f32[8,1,2448]{2,1,0:T(1,128)}), f32[8,1,2448]{2,1,0:T(1,128)S(1)}, u32[]{:S(2)}, u32[]{:S(2)}) %all-to-all-start.3) | async-done | bytes 78368 | tf_op jit(solution)/shard_map/all_to_all | solution.py:601
  524.7 5.7 all-gather.1
  536.1 12.8 %all-to-all-done.1 = bf16[8,144,256]{2,1,0:T(8,128)(2,1)S(1)} async-done(((bf16[8,144,256]{2,1,0:T(8,128)(2,1)}), bf16[8,144,256]{2,1,0:T(8,128)(2,1)S(1)}, u32[]{:S(2)}, u32[]{:S(2)}) %all-to-all-start.1) | async-done | bytes 589856 | tf_op jit(solution)/shard_map/all_to_all | solution.py:411
  555.5 6.6 %reduce-scatter.3.cloned.1.call-done.in_ref = bf16[288,1152]{1,0:T(8,128)(2,1)} async-done(((bf16[4608,1152]{1,0:T(8,128)(2,1)}), bf16[288,1152]{1,0:T(8,128)(2,1)}) %reduce-scatter.3.cloned.1.call-update) | async-done | bytes 663568 | tf_op jit(solution)/shard_map/reduce_scatter | solution.py:451
  (484 shorter events, 240.4 us)
Async XLA Ops:
  7.2 120.6 %all-gather.5.cloned.1.call-start = ((), (), s32[]{:S(2)}) async-start(), calls=%async_computation.6 | async-start | bytes 11280384 | tf_op jit(solution)/shard_map/all_gather | solution.py:446
  16.2 217.2 %all-gather.7.cloned.1.call-start = ((), (), s32[]{:S(2)}) async-start(), calls=%async_computation.7 | async-start | bytes 11280384 | tf_op jit(solution)/shard_map/all_gather | solution.py:446
  18.4 534.7 %reduce-scatter.5.cloned.1.call-start = ((), (), s32[]{:S(2)}) async-start(), calls=%async_computation.9 | async-start | bytes 11280384 | tf_op jit(solution)/shard_map/reduce_scatter | solution.py:451
  27.5 25.1 %collective-permute-start.2 = (bf16[1,144,430]{2,1,0:T(8,128)(2,1)S(1)}, bf16[1,144,430]{2,1,0:T(8,128)(2,1)S(1)}, u32[]{:S(2)}, u32[]{:S(2)}) collective-permute-start(bf16[1,144,430]{2,1,0:T(8,128)(2,1)S(1)} %get-tuple-element.133), channel_id=1, source_target_pairs={{0,8},{1,9},{2,0},{3,1},{4,12},{5,13},{6,4},{7,5},{8,10},{9,11},{1... | collective-permute-start | bytes 371528 | tf_op jit(solution)/shard_map/ppermute | solution.py:402
  29.9 29.0 %collective-permute-start.3 = (bf16[1,144,430]{2,1,0:T(8,128)(2,1)S(1)}, bf16[1,144,430]{2,1,0:T(8,128)(2,1)S(1)}, u32[]{:S(2)}, u32[]{:S(2)}) collective-permute-start(bf16[1,144,430]{2,1,0:T(8,128)(2,1)S(1)} %get-tuple-element.134), channel_id=1, source_target_pairs={{0,9},{1,8},{2,1},{3,0},{4,13},{5,12},{6,5},{7,4},{8,11},{9,10},{1... | collective-permute-start | bytes 371528 | tf_op jit(solution)/shard_map/ppermute | solution.py:402
  30.2 28.7 %collective-permute-start.4 = (bf16[1,144,430]{2,1,0:T(8,128)(2,1)S(1)}, bf16[1,144,430]{2,1,0:T(8,128)(2,1)S(1)}, u32[]{:S(2)}, u32[]{:S(2)}) collective-permute-start(bf16[1,144,430]{2,1,0:T(8,128)(2,1)S(1)} %get-tuple-element.135), channel_id=1, source_target_pairs={{0,4},{1,5},{2,12},{3,13},{4,0},{5,1},{6,8},{7,9},{8,6},{9,7},{10,... | collective-permute-start | bytes 371528 | tf_op jit(solution)/shard_map/ppermute | solution.py:402
  33.0 28.7 %collective-permute-start.5 = (bf16[1,144,430]{2,1,0:T(8,128)(2,1)S(1)}, bf16[1,144,430]{2,1,0:T(8,128)(2,1)S(1)}, u32[]{:S(2)}, u32[]{:S(2)}) collective-permute-start(bf16[1,144,430]{2,1,0:T(8,128)(2,1)S(1)} %get-tuple-element.137), channel_id=1, source_target_pairs={{0,5},{1,4},{2,13},{3,12},{4,1},{5,0},{6,9},{7,8},{8,7},{9,6},{10,... | collective-permute-start | bytes 371528 | tf_op jit(solution)/shard_map/ppermute | solution.py:402
  34.2 36.6 %collective-permute-start.6 = (bf16[1,144,430]{2,1,0:T(8,128)(2,1)S(1)}, bf16[1,144,430]{2,1,0:T(8,128)(2,1)S(1)}, u32[]{:S(2)}, u32[]{:S(2)}) collective-permute-start(bf16[1,144,430]{2,1,0:T(8,128)(2,1)S(1)} %get-tuple-element.136), channel_id=1, source_target_pairs={{0,12},{1,13},{2,4},{3,5},{4,8},{5,9},{6,0},{7,1},{8,14},{9,15},{1... | collective-permute-start | bytes 371528 | tf_op jit(solution)/shard_map/ppermute | solution.py:402
  52.6 20.7 %collective-permute-start.7 = (bf16[1,144,430]{2,1,0:T(8,128)(2,1)S(1)}, bf16[1,144,430]{2,1,0:T(8,128)(2,1)S(1)}, u32[]{:S(2)}, u32[]{:S(2)}) collective-permute-start(bf16[1,144,430]{2,1,0:T(8,128)(2,1)S(1)} %get-tuple-element.130), channel_id=1, source_target_pairs={{0,13},{1,12},{2,5},{3,4},{4,9},{5,8},{6,1},{7,0},{8,15},{9,14},{1... | collective-permute-start | bytes 371528 | tf_op jit(solution)/shard_map/ppermute | solution.py:402
  77.8 54.3 %collective-permute-start.8 = (bf16[1152,256]{1,0:T(8,128)(2,1)S(1)}, bf16[1152,256]{1,0:T(8,128)(2,1)S(1)}, u32[]{:S(2)}, u32[]{:S(2)}) collective-permute-start(bf16[1152,256]{1,0:T(8,128)(2,1)S(1)} %fusion.7.refs_1_.refs_0_.refs_4_), channel_id=1, source_target_pairs={{0,1},{1,0},{2,3},{3,2},{4,5},{5,4},{6,7},{7,6},{8,9},{9,8},{10,11... | collective-permute-start | bytes 1769480 | tf_op jit(solution)/shard_map/ppermute | solution.py:42
  152.5 15.5 %collective-permute-start.11 = (bf16[1152,256]{1,0:T(8,128)(2,1)S(1)}, bf16[1152,256]{1,0:T(8,128)(2,1)S(1)}, u32[]{:S(2)}, u32[]{:S(2)}) collective-permute-start(bf16[1152,256]{1,0:T(8,128)(2,1)S(1)} %shard_map.421), channel_id=1, source_target_pairs={{0,1},{1,0},{2,3},{3,2},{4,5},{5,4},{6,7},{7,6},{8,9},{9,8},{10,11... | collective-permute-start | bytes 1769480 | tf_op jit(solution)/shard_map/ppermute | solution.py:42
  168.8 28.7 %collective-permute-start.12 = (bf16[1152,256]{1,0:T(8,128)(2,1)S(1)}, bf16[1152,256]{1,0:T(8,128)(2,1)}, u32[]{:S(2)}, u32[]{:S(2)}) collective-permute-start(bf16[1152,256]{1,0:T(8,128)(2,1)S(1)} %fusion.42.refs_1_.refs_12_), channel_id=1, source_target_pairs={{0,1},{1,0},{2,3},{3,2},{4,5},{5,4},{6,7},{7,6},{8,9},{9,8},{10,11... | collective-permute-start | bytes 1769480 | tf_op jit(solution)/shard_map/ppermute | solution.py:42
  178.1 31.7 %collective-permute-start.19 = (bf16[1,144,256]{2,1,0:T(8,128)(2,1)}, bf16[1,144,256]{2,1,0:T(8,128)(2,1)S(1)}, u32[]{:S(2)}, u32[]{:S(2)}) collective-permute-start(bf16[1,144,256]{2,1,0:T(8,128)(2,1)} %get-tuple-element.145), channel_id=1, source_target_pairs={{0,8},{1,9},{2,0},{3,1},{4,12},{5,13},{6,4},{7,5},{8,10},{9,11},{1... | collective-permute-start | bytes 221192 | tf_op jit(solution)/shard_map/ppermute | solution.py:402
  178.4 32.1 %collective-permute-start.20 = (bf16[1,144,256]{2,1,0:T(8,128)(2,1)}, bf16[1,144,256]{2,1,0:T(8,128)(2,1)S(1)}, u32[]{:S(2)}, u32[]{:S(2)}) collective-permute-start(bf16[1,144,256]{2,1,0:T(8,128)(2,1)} %get-tuple-element.144), channel_id=1, source_target_pairs={{0,9},{1,8},{2,1},{3,0},{4,13},{5,12},{6,5},{7,4},{8,11},{9,10},{1... | collective-permute-start | bytes 221192 | tf_op jit(solution)/shard_map/ppermute | solution.py:402
  179.2 32.0 %collective-permute-start.21 = (bf16[1,144,256]{2,1,0:T(8,128)(2,1)}, bf16[1,144,256]{2,1,0:T(8,128)(2,1)S(1)}, u32[]{:S(2)}, u32[]{:S(2)}) collective-permute-start(bf16[1,144,256]{2,1,0:T(8,128)(2,1)} %get-tuple-element.143), channel_id=1, source_target_pairs={{0,4},{1,5},{2,12},{3,13},{4,0},{5,1},{6,8},{7,9},{8,6},{9,7},{10,... | collective-permute-start | bytes 221192 | tf_op jit(solution)/shard_map/ppermute | solution.py:402
  184.3 26.9 %collective-permute-start.22 = (bf16[1,144,256]{2,1,0:T(8,128)(2,1)}, bf16[1,144,256]{2,1,0:T(8,128)(2,1)S(1)}, u32[]{:S(2)}, u32[]{:S(2)}) collective-permute-start(bf16[1,144,256]{2,1,0:T(8,128)(2,1)} %get-tuple-element.142), channel_id=1, source_target_pairs={{0,5},{1,4},{2,13},{3,12},{4,1},{5,0},{6,9},{7,8},{8,7},{9,6},{10,... | collective-permute-start | bytes 221192 | tf_op jit(solution)/shard_map/ppermute | solution.py:402
  209.8 16.3 %collective-permute-start.13 = (bf16[1152,256]{1,0:T(8,128)(2,1)S(1)}, bf16[1152,256]{1,0:T(8,128)(2,1)S(1)}, u32[]{:S(2)}, u32[]{:S(2)}) collective-permute-start(bf16[1152,256]{1,0:T(8,128)(2,1)S(1)} %shard_map.427), channel_id=1, source_target_pairs={{0,1},{1,0},{2,3},{3,2},{4,5},{5,4},{6,7},{7,6},{8,9},{9,8},{10,11... | collective-permute-start | bytes 1769480 | tf_op jit(solution)/shard_map/ppermute | solution.py:42
  228.2 15.3 %collective-permute-start.14 = (bf16[1152,256]{1,0:T(8,128)(2,1)S(1)}, bf16[1152,256]{1,0:T(8,128)(2,1)}, u32[]{:S(2)}, u32[]{:S(2)}) collective-permute-start(bf16[1152,256]{1,0:T(8,128)(2,1)S(1)} %add_convert_fusion.3.refs_1_.refs_0_), channel_id=1, source_target_pairs={{0,1},{1,0},{2,3},{3,2},{4,5},{5,4},{6,7},{7,6},{8,9},{9,8},{10,11... | collective-permute-start | bytes 1769480 | tf_op jit(solution)/shard_map/ppermute | solution.py:42
  228.9 27.3 %collective-permute-start.25 = (bf16[1152,256]{1,0:T(8,128)(2,1)S(1)}, bf16[1152,256]{1,0:T(8,128)(2,1)}, u32[]{:S(2)}, u32[]{:S(2)}) collective-permute-start(bf16[1152,256]{1,0:T(8,128)(2,1)S(1)} %fusion.16.refs_2_.refs_4_), channel_id=1, source_target_pairs={{0,1},{1,0},{2,3},{3,2},{4,5},{5,4},{6,7},{7,6},{8,9},{9,8},{10,11... | collective-permute-start | bytes 1769480 | tf_op jit(solution)/shard_map/ppermute | solution.py:42
  283.9 278.2 %reduce-scatter.3.cloned.1.call-start = ((), (), s32[]{:S(2)}) async-start(), calls=%async_computation.8 | async-start | bytes 11280384 | tf_op jit(solution)/shard_map/reduce_scatter | solution.py:451
  284.2 21.1 %collective-permute-start.26 = (bf16[1152,256]{1,0:T(8,128)(2,1)}, bf16[1152,256]{1,0:T(8,128)(2,1)S(1)}, u32[]{:S(2)}, u32[]{:S(2)}) collective-permute-start(bf16[1152,256]{1,0:T(8,128)(2,1)} %copy-done.45), channel_id=1, source_target_pairs={{0,1},{1,0},{2,3},{3,2},{4,5},{5,4},{6,7},{7,6},{8,9},{9,8},{10,11... | collective-permute-start | bytes 1769480 | tf_op jit(solution)/shard_map/ppermute | solution.py:42
  303.1 15.7 %collective-permute-start.15 = (bf16[1152,256]{1,0:T(8,128)(2,1)S(1)}, bf16[1152,256]{1,0:T(8,128)(2,1)S(1)}, u32[]{:S(2)}, u32[]{:S(2)}) collective-permute-start(bf16[1152,256]{1,0:T(8,128)(2,1)S(1)} %shard_map.430), channel_id=1, source_target_pairs={{0,1},{1,0},{2,3},{3,2},{4,5},{5,4},{6,7},{7,6},{8,9},{9,8},{10,11... | collective-permute-start | bytes 1769480 | tf_op jit(solution)/shard_map/ppermute | solution.py:42
  321.4 16.2 %collective-permute-start.27 = (bf16[1152,256]{1,0:T(8,128)(2,1)S(1)}, bf16[1152,256]{1,0:T(8,128)(2,1)S(1)}, u32[]{:S(2)}, u32[]{:S(2)}) collective-permute-start(bf16[1152,256]{1,0:T(8,128)(2,1)S(1)} %convert_element_type.209.refs_2_.refs_18_), channel_id=1, source_target_pairs={{0,1},{1,0},{2,3},{3,2},{4,5},{5,4},{6,7},{7,6},{8,9},{9,8},{10,11... | collective-permute-start | bytes 1769480 | tf_op jit(solution)/shard_map/ppermute | solution.py:42
  350.7 15.0 %collective-permute-start.28 = (bf16[1152,256]{1,0:T(8,128)(2,1)S(1)}, bf16[1152,256]{1,0:T(8,128)(2,1)S(1)}, u32[]{:S(2)}, u32[]{:S(2)}) collective-permute-start(bf16[1152,256]{1,0:T(8,128)(2,1)S(1)} %shard_map.439), channel_id=1, source_target_pairs={{0,1},{1,0},{2,3},{3,2},{4,5},{5,4},{6,7},{7,6},{8,9},{9,8},{10,11... | collective-permute-start | bytes 1769480 | tf_op jit(solution)/shard_map/ppermute | solution.py:42
  429.4 14.3 %collective-permute-start.34 = (bf16[1152,120]{1,0:T(8,128)(2,1)S(1)}, bf16[1152,120]{1,0:T(8,128)(2,1)}, u32[]{:S(2)}, u32[]{:S(2)}) collective-permute-start(bf16[1152,120]{1,0:T(8,128)(2,1)S(1)} %shard_map.446), channel_id=1, source_target_pairs={{0,8},{8,0},{16,24},{24,16},{1,9},{9,1},{17,25},{25,17},{2,10},{10... | collective-permute-start | bytes 829448 | tf_op jit(solution)/shard_map/ppermute | solution.py:38
  437.3 31.4 %collective-permute-start.16 = (bf16[1152,256]{1,0:T(8,128)(2,1)}, bf16[1152,256]{1,0:T(8,128)(2,1)}, u32[]{:S(2)}, u32[]{:S(2)}) collective-permute-start(bf16[1152,256]{1,0:T(8,128)(2,1)} %get-tuple-element.127), channel_id=1, source_target_pairs={{0,0},{1,1},{2,8},{3,9},{4,4},{5,5},{6,12},{7,13},{8,2},{9,3},{10,... | collective-permute-start | bytes 1769480 | tf_op jit(solution)/shard_map/ppermute | solution.py:391
  445.5 23.2 %all-to-all-start.2 = ((bf16[8,144,120]{2,1,0:T(8,128)(2,1)}), bf16[8,144,120]{2,1,0:T(8,128)(2,1)}, u32[]{:S(2)}, u32[]{:S(2)}) async-start(bf16[8,144,120]{2,1,0:T(8,128)(2,1)} %bitcast.43), calls=%async_computation.2 | async-start | bytes 589824 | tf_op jit(solution)/shard_map/all_to_all | solution.py:584
  451.2 15.3 %collective-permute-start.32 = (bf16[1152,256]{1,0:T(8,128)(2,1)}, bf16[1152,256]{1,0:T(8,128)(2,1)S(1)}, u32[]{:S(2)}, u32[]{:S(2)}) collective-permute-start(bf16[1152,256]{1,0:T(8,128)(2,1)} %shard_map.443), channel_id=1, source_target_pairs={{0,1},{1,0},{2,3},{3,2},{4,5},{5,4},{6,7},{7,6},{8,9},{9,8},{10,11... | collective-permute-start | bytes 1769480 | tf_op jit(solution)/shard_map/ppermute | solution.py:42
  468.7 35.7 %all-to-all-start = ((bf16[8,144,256]{2,1,0:T(8,128)(2,1)}), bf16[8,144,256]{2,1,0:T(8,128)(2,1)}, u32[]{:S(2)}, u32[]{:S(2)}) async-start(bf16[8,144,256]{2,1,0:T(8,128)(2,1)} %bitcast.35), calls=%async_computation | async-start | bytes 1179648 | tf_op jit(solution)/shard_map/all_to_all | solution.py:411
  485.4 35.7 %collective-permute-start.33 = (bf16[1152,256]{1,0:T(8,128)(2,1)}, bf16[1152,256]{1,0:T(8,128)(2,1)}, u32[]{:S(2)}, u32[]{:S(2)}) collective-permute-start(bf16[1152,256]{1,0:T(8,128)(2,1)} %fusion.12), channel_id=1, source_target_pairs={{0,0},{1,1},{2,8},{3,9},{4,4},{5,5},{6,12},{7,13},{8,2},{9,3},{10,... | collective-permute-start | bytes 1769480 | tf_op jit(solution)/shard_map/ppermute | solution.py:391
  504.4 15.1 %all-to-all-start.3 = ((f32[8,1,2448]{2,1,0:T(1,128)}), f32[8,1,2448]{2,1,0:T(1,128)S(1)}, u32[]{:S(2)}, u32[]{:S(2)}) async-start(f32[8,1,2448]{2,1,0:T(1,128)} %reshape.319), calls=%async_computation.3 | async-start | bytes 163840 | tf_op jit(solution)/shard_map/all_to_all | solution.py:601
  521.0 27.8 %all-to-all-start.1 = ((bf16[8,144,256]{2,1,0:T(8,128)(2,1)}), bf16[8,144,256]{2,1,0:T(8,128)(2,1)S(1)}, u32[]{:S(2)}, u32[]{:S(2)}) async-start(bf16[8,144,256]{2,1,0:T(8,128)(2,1)} %bitcast.40), calls=%async_computation.1 | async-start | bytes 1179648 | tf_op jit(solution)/shard_map/all_to_all | solution.py:411
  (130 other events, 1068.6 us)
Sparse Core Ops, SparseCore 0:
  16.3 111.4 all-gather.4
  130.7 96.9 all-gather.6
  284.1 120.1 reduce-scatter.4
  423.7 138.3 reduce-scatter.2

commit v3 on v2

--- a/solution.py
+++ b/solution.py
@@ -336,6 +336,39 @@
     out_spec = pl.BlockSpec((rows, chunk, sum(sizes)), lambda z: (z, 0, 0))
     kernel = functools.partial(outer_kernel, [len(a) for a, _ in pairs])
     return call_parts(kernel, half, args, specs, out, out_spec)
+
+
+def tree_kernel(terms, order_ref, *refs):
+    out_ref, start, at = refs[-1], 0, 0
+    for count in terms:
+        total = None
+        for i in range(count):
+            part = dot_nt(refs[at + i][...], refs[at + count + i][...])
+            total = part if total is None else total + part
+        end = start + refs[at + count].shape[0]
+        out_ref[0, 0, :, start:end] = total.astype(BF)
+        start, at = end, at + 2 * count
+
+
+def tree_blocks(pairs, rows, half, row_order, col_order):
+    chunk = D // rows
+    sizes = [b[0].shape[0] // half for _, b in pairs]
+    specs, args = [], []
+    for (a, b), n in zip(pairs, sizes):
+        specs += [pl.BlockSpec((chunk, p.shape[1]), lambda i, e, order: (order[i], 0)) for p in a]
+        specs += [pl.BlockSpec((n, p.shape[1]), lambda i, e, order: (order[rows + e], 0)) for p in b]
+        args += list(a) + list(b)
+    return pl.pallas_call(
+        functools.partial(tree_kernel, [len(a) for a, _ in pairs]),
+        grid_spec=pltpu.PrefetchScalarGridSpec(
+            num_scalar_prefetch=1,
+            grid=(rows, half),
+            in_specs=specs,
+            out_specs=pl.BlockSpec((1, 1, chunk, sum(sizes)), lambda i, e, order: (i, e, 0, 0)),
+        ),
+        out_shape=jax.ShapeDtypeStruct((rows, half, chunk, sum(sizes)), BF),
+        compiler_params=pltpu.CompilerParams(vmem_limit_bytes=50 * 2**20),
+    )(jnp.stack(row_order + col_order), *args)
 
 
 def shards(
@@ -407,7 +440,7 @@
         return value.reshape(2, feat, half, width).transpose(0, 2, 1, 3).reshape(cols, feat, width)
 
     def tokens_out(value):
-        blocks = place_swap(value.astype(BF)).reshape(cols, feat, width)
+        blocks = place_swap(value).reshape(cols, feat, width)
         blocks = lax.all_to_all(blocks, "col", 0, 0, tiled=True)
         blocks = blocks.reshape(2, half, feat, width).transpose(0, 2, 1, 3)
         return blocks.reshape(2, feat, half * width).astype(F32)
@@ -449,6 +482,25 @@
     def scatter(blocks):
         flat = blocks.reshape(half * D, blocks.shape[2])
         return lax.psum_scatter(flat, ("row", "col"), scatter_dimension=0, tiled=True, axis_index_groups=groups)
+
+    row_bits = rows.bit_length() - 1
+    order = [0]
+    for b in range(row_bits):
+        order = [i for j in order for i in (j, j | (1 << (row_bits - 1 - b)))]
+    order = sorted(order, key=lambda i: int(format(i, f"0{row_bits}b")[::-1], 2))
+
+    def tree_outer(pairs):
+        return tree_blocks(pairs, rows, half, [r ^ i for i in order], [(c >> 1) ^ e for e in range(half)])
+
+    def tree_reduce(blocks):
+        for b in range(row_bits):
+            h = blocks.shape[0] // 2
+            received = row_swap(blocks[h:], rows, 1 << b)
+            blocks = (blocks[:h].astype(F32) + received.astype(F32)).astype(BF)
+        total = blocks[0, 0].astype(F32)
+        for e in range(1, half):
+            total = total + col_swap(blocks[0, e], cols, e << 1).astype(F32)
+        return total
 
     first_w = gather_weights(
         pack([query_weight.T, key_weight.T, value_weight.T, out_weight, cross_query.T, cross_key.T, cross_value.T, cross_out])
@@ -477,9 +529,10 @@
     extra = jnp.concatenate(
         [text_tokens.transpose(0, 2, 1)] + [p.astype(BF) for p in (small_high, small_mid, small_low)], axis=2
     )
-    arrived = send_tokens(jnp.concatenate([token_blocks(block_input), jnp.repeat(extra, half, axis=0)], axis=2))
-    cot_low = send_tokens(token_blocks(after(out_grad, arrived)))
-    small_n, head = small.shape[2], width
+    arrived = send_tokens(
+        jnp.concatenate([token_blocks(block_input), token_blocks(out_grad), jnp.repeat(extra, half, axis=0)], axis=2)
+    )
+    small_n, head = small.shape[2], 2 * width
 
     def small_of(value):
         parts = [value[:, head + texts + i * small_n : head + texts + (i + 1) * small_n].astype(F32) for i in range(3)]
@@ -503,7 +556,7 @@
     text_t = arrived[:, head : head + texts]
 
     resid = arrived[:, :width].astype(F32)
-    cot = cot_low.astype(F32)
+    cot = arrived[:, width:head].astype(F32)
     heads_w, hidden_w = half * feat, half * ups
     qkv_w, out_w, cq_w, ckv_w, cout_w = (
         view_of(first_w, i * feat, (j - i) * feat) for i, j in ((0, 3), (3, 4), (4, 5), (5, 7), (7, 8))
@@ -536,7 +589,7 @@
     hidden_outs = [(hidden_w, width, BF)] * 2
     *hidden, slope = apply_in(gelu_kernel, up_w, mlp_full, up_b, hidden_outs + [(hidden_w, 2 * width, F32)])
     branch_m = reduce_pair(down_w, hidden)[0] + down_b
-    block_output = tokens_out(after_cross + gate_m * branch_m)
+    block_out = (after_cross + gate_m * branch_m).astype(BF)
 
     grad_mlp = gate_m * cot
     low_full = gather_pair(grad_mlp.astype(BF))
@@ -555,7 +608,13 @@
     low_cross = gather_pair(grad_cross.astype(BF))
     dcatt = [heads_in(cout_w, p, none)[0] for p in low_cross]
     dcq, dckv = attend_backward(cq_parts, ckv, length, clse, dcatt, half)
-    grad_res = grad_cross + reduce_pair(cq_w, dcq)[0]
+
+    def cross_cover(other):
+        pairs = [(cross_full, dcq), ([text_t], dckv), (low_cross, [after(catt[0], other), catt[1]])]
+        return outer_blocks(pairs, rows, half)
+
+    back_cross, cross_blocks = reduce_pair(cq_w, dcq, cover=cross_cover)
+    grad_res = grad_cross + back_cross
     g_cq_b = jnp.sum(sum(p.astype(F32) for p in dcq), axis=1)
     g_cv_b = jnp.sum(dckv[0].astype(F32).reshape(half, 2, feat, texts)[:, 1], axis=2)
     g_gate_a = jnp.sum(grad_res * branch_a, axis=1)
@@ -567,17 +626,19 @@
     dkv = reduce_keys(dkv)
 
     def attention_cover(other):
-        pairs = [(attn_full, dq), (attn_full, dkv), (low_attn, att), (cross_full, dcq), ([text_t], dckv), (low_cross, catt)]
-        return outer_blocks([(pairs[0][0], [after(dq[0], other), dq[1]])] + pairs[1:], rows, half)
+        return tree_outer([(attn_full, [after(dq[0], other), dq[1]]), (attn_full, dkv), (low_attn, att)])
 
     back_att, att_blocks = reduce_pair(qkv_w, dq, dkv, cover=attention_cover)
-    att_grads = scatter(att_blocks)
-    g_q, g_k, g_v, g_out, g_cq, g_ck, g_cv, g_cout = unpack(att_grads, [feat] * 8)
+    cross_grads = scatter(after(cross_blocks, mlp_grads, dq[0]))
+    att_grads = tree_reduce(att_blocks)
+    g_cq, g_ck, g_cv, g_cout = unpack(cross_grads, [feat] * 4)
+    g_q, g_k, g_v, g_out = unpack(att_grads, [feat] * 4)
     g_up, g_down = mlp_grads[:, :ups].astype(F32), mlp_grads[:, ups:].astype(F32)
     g_q_b = jnp.sum(sum(p.astype(F32) for p in dq), axis=1)
     g_v_b = jnp.sum(sum(p.astype(F32) for p in dkv).reshape(half, 2, feat, width)[:, 1], axis=2)
     back_a, g_shift_a, g_scale_a = norm_backward(back_att, normed_a, inv_a, scale_a)
-    grad_input = tokens_out(grad_res + back_a)
+    block_output = tokens_out(after(block_out, back_att))
+    grad_input = tokens_out((grad_res + back_a).astype(BF))
     grad_text = apply_out(ckv_w, dckv, BF)
     grad_text = grad_text.astype(F32) + row_swap(grad_text, rows, 1).astype(F32)
     grad_text = jnp.where(at_home, grad_text, 0.0).astype(BF).reshape(cols, feat, texts)

time: 579 us -> 582 us (level)
  waiting for transfers between devices: 191 us -> 139 us
  Pallas kernels: 179 us -> 197 us
  other arithmetic: 35.7 us -> 50.6 us
  local copies, waits for them, and re-layouts: 52.1 us -> 61.3 us
  starting transfers between devices: 85.2 us -> 93.1 us
    all_gather x2, waiting for transfers between devices: 47.5 us -> 7.32 us  [gather_weights(): lax.all_gather(flat, ('row', 'col'), axis=0, tiled=True, axis_index_group...]
    all_to_all x2, waiting for transfers between devices: 24.7 us -> 2.07 us  [tokens_out(): blocks = lax.all_to_all(blocks, 'col', 0, 0, tiled=True)]
    pallas_call x0 -> x1, Pallas kernels: none -> 14.1 us  [tree_blocks(): pl.pallas_call(functools.partial(tree_kernel, [len(a) for a, _ in pairs])...]
    ppermute x16 -> x8, waiting for transfers between devices: 31.5 us -> 43.3 us  [send_tokens(): part = lax.ppermute(part, ('row', 'col'), pairs)]
    unnamed x254, local copies, waits for them, and re-layouts: 18.6 us -> 28.2 us
    another operation x10, local copies, waits for them, and re-layouts: 11.7 us -> 5.07 us  [shards(): jnp.stack([g_shift_a, g_scale_a, g_gate_a, g_shift_m, g_scale_m, g_gate_m...]
    ppermute x16 -> x8, starting transfers between devices: 38.5 us -> 43 us  [send_tokens(): part = lax.ppermute(part, ('row', 'col'), pairs)]
    ppermute x12 -> x15, starting transfers between devices: 16.4 us -> 19.8 us  [col_swap(): return lax.ppermute(value, 'col', [(i, i ^ mask) for i in range(cols)])]
  transfers between devices with their start and end apart: 43 -> 40, of which waited for: 25 -> 13; matrix products, arithmetic and copies ran while one was open for 13% -> 17% of each run, Pallas kernels for 26% -> 29%
where the time goes in v3:
time: 582 us; the launch traced here: 571 us
  Pallas kernels  197 us (34%)
  waiting for transfers between devices  139 us (24%)
  starting transfers between devices  93.1 us (16%)
  local copies, waits for them, and re-layouts  61.3 us (11%)
  other arithmetic  50.6 us (9%)
  between operations  16.7 us (3%)
  blocking collectives  7.64 us (1%)
    pallas_call x33, Pallas kernels, call_parts(): pl.pallas_call(kernel, grid=(steps,), in_specs=arg_specs, out_specs=out_s...  182 us
    ppermute x15, waiting for transfers between devices, col_swap(): return lax.ppermute(value, 'col', [(i, i ^ mask) for i in range(cols)])  66.5 us
    ppermute x8, waiting for transfers between devices, send_tokens(): part = lax.ppermute(part, ('row', 'col'), pairs)  43.3 us
    ppermute x8, starting transfers between devices, send_tokens(): part = lax.ppermute(part, ('row', 'col'), pairs)  43 us
    unnamed x254, local copies, waits for them, and re-layouts  28.2 us
    ppermute x15, starting transfers between devices, col_swap(): return lax.ppermute(value, 'col', [(i, i ^ mask) for i in range(cols)])  19.8 us
    pallas_call x1, Pallas kernels, tree_blocks(): pl.pallas_call(functools.partial(tree_kernel, [len(a) for a, _ in pairs])...  14.1 us
  transfers between devices with their start and end apart: 40, of which 13 were waited for; matrix products, arithmetic and copies ran while one was open for 17% of the time, Pallas kernels for 29%

profile of v3, /device:TPU:0, one launch (start us, length us, event | category | flops | bytes accessed | tf_op | source)
XLA Modules:
  0.0 571.1 jit_solution(7710129674564668647)
XLA Ops:
  36.8 8.9 %collective-permute-start.2 = (bf16[1,144,686]{2,1,0:T(8,128)(2,1)}, bf16[1,144,686]{2,1,0:T(8,128)(2,1)S(1)}, u32[]{:S(2)}, u32[]{:S(2)}) collective-permute-start(bf16[1,144,686]{2,1,0:T(8,128)(2,1)} %get-tuple-element.143), channel_id=1, source_target_pairs={{0,8},{1,9},{2,0},{3,1},{4,12},{5,13},{6,4},{7,5},{8,10},{9,11},{1... | collective-permute-start | bytes 592712 | tf_op jit(solution)/shard_map/ppermute | solution.py:435
  45.9 9.2 %collective-permute-start.3 = (bf16[1,144,686]{2,1,0:T(8,128)(2,1)S(1)}, bf16[1,144,686]{2,1,0:T(8,128)(2,1)S(1)}, u32[]{:S(2)}, u32[]{:S(2)}) collective-permute-start(bf16[1,144,686]{2,1,0:T(8,128)(2,1)S(1)} %copy-done.71), channel_id=1, source_target_pairs={{0,9},{1,8},{2,1},{3,0},{4,13},{5,12},{6,5},{7,4},{8,11},{9,10},{1... | collective-permute-start | bytes 592712 | tf_op jit(solution)/shard_map/ppermute | solution.py:435
  55.2 5.5 collective-permute-done.2
  60.6 14.7 %collective-permute-start.4 = (bf16[1,144,686]{2,1,0:T(8,128)(2,1)S(1)}, bf16[1,144,686]{2,1,0:T(8,128)(2,1)S(1)}, u32[]{:S(2)}, u32[]{:S(2)}) collective-permute-start(bf16[1,144,686]{2,1,0:T(8,128)(2,1)S(1)} %copy-done.70), channel_id=1, source_target_pairs={{0,4},{1,5},{2,12},{3,13},{4,0},{5,1},{6,8},{7,9},{8,6},{9,7},{10,... | collective-permute-start | bytes 592712 | tf_op jit(solution)/shard_map/ppermute | solution.py:435
  75.4 37.8 %collective-permute-done.4 = bf16[1,144,686]{2,1,0:T(8,128)(2,1)S(1)} collective-permute-done((bf16[1,144,686]{2,1,0:T(8,128)(2,1)S(1)}, bf16[1,144,686]{2,1,0:T(8,128)(2,1)S(1)}, u32[]{:S(2)}, u32[]{:S(2)}) %collective-permute-start.4) | collective-permute-done | bytes 197600 | tf_op jit(solution)/shard_map/ppermute | solution.py:435
  128.0 7.3 %all-gather.5.cloned.1.call-done = bf16[4608,1152]{1,0:T(8,128)(2,1)} async-done(((bf16[288,1152]{1,0:T(8,128)(2,1)}), bf16[4608,1152]{1,0:T(8,128)(2,1)}) %all-gather.5.cloned.1.call-update) | async-done | bytes 10616848 | tf_op jit(solution)/shard_map/all_gather | solution.py:479
  146.4 8.9 %shard_map.419 = (bf16[576,256]{1,0:T(8,128)(2,1)S(1)}, bf16[576,256]{1,0:T(8,128)(2,1)S(1)}, f32[4,512,2]{2,1,0:T(8,128)}) custom-call(bf16[576,256]{1,0:T(8,128)(2,1)S(1)} %get-tuple-element.64.refs_0_, bf16[576,256]{1,0:T(8,128)(2,1)S(1)} %get-tuple-element.65.refs_1_, bf16[1152,256]{1,0:T(8,128)(2,1)S(1)} %get-tuple-element.66.refs_2_, ...), custom_call_target="tpu_custom_call" | custom-call | tf_op jit(solution)/shard_map/pallas_call | solution.py:135
  164.7 10.1 %collective-permute-done.11 = bf16[1152,256]{1,0:T(8,128)(2,1)S(1)} collective-permute-done((bf16[1152,256]{1,0:T(8,128)(2,1)S(1)}, bf16[1152,256]{1,0:T(8,128)(2,1)S(1)}, u32[]{:S(2)}, u32[]{:S(2)}) %collective-permute-start.11) | collective-permute-done | bytes 589856 | tf_op jit(solution)/shard_map/ppermute | solution.py:42
  209.1 9.9 %collective-permute-done.13 = bf16[1152,256]{1,0:T(8,128)(2,1)S(1)} collective-permute-done((bf16[1152,256]{1,0:T(8,128)(2,1)S(1)}, bf16[1152,256]{1,0:T(8,128)(2,1)S(1)}, u32[]{:S(2)}, u32[]{:S(2)}) %collective-permute-start.13) | collective-permute-done | bytes 589856 | tf_op jit(solution)/shard_map/ppermute | solution.py:42
  226.4 13.0 %collective-permute-done.14.refs_2_.refs_1_ = bf16[1152,256]{1,0:T(8,128)(2,1)} collective-permute-done((bf16[1152,256]{1,0:T(8,128)(2,1)}, bf16[1152,256]{1,0:T(8,128)(2,1)}, u32[]{:S(2)}, u32[]{:S(2)}) %collective-permute-start.14) | collective-permute-done | bytes 589856 | tf_op jit(solution)/shard_map/ppermute | solution.py:42
  239.4 9.4 %shard_map.428 = (bf16[2304,256]{1,0:T(8,128)(2,1)S(1)}, bf16[2304,256]{1,0:T(8,128)(2,1)S(1)}, f32[2304,512]{1,0:T(8,128)}) custom-call(bf16[4,1152,1152]{2,1,0:T(8,128)(2,1)} %bitcast.172, bf16[1152,256]{1,0:T(8,128)(2,1)} %add_convert_fusion.5.refs_1_.refs_0_, bf16[1152,256]{1,0:T(8,128)(2,1)} %collective-permute-done.14.refs_2_.refs_1_, ...), custom_call_target="tpu_custom_call" | custom-call | tf_op jit(solution)/shard_map/pallas_call | solution.py:135
  250.8 9.8 %shard_map.431 = (bf16[2304,256]{1,0:T(8,128)(2,1)S(1)}, bf16[2304,256]{1,0:T(8,128)(2,1)S(1)}, f32[2304,1]{1,0:T(8,128)}) custom-call(bf16[4,1152,1152]{2,1,0:T(8,128)(2,1)} %bitcast.173, bf16[4,1152,1152]{2,1,0:T(8,128)(2,1)} %bitcast.174, bf16[1152,256]{1,0:T(8,128)(2,1)S(1)} %get-tuple-element.137.refs_2_.refs_4_, ...), custom_call_target="tpu_custom_call" | custom-call | tf_op jit(solution)/shard_map/pallas_call | solution.py:135
  260.7 6.0 %shard_map.432 = bf16[1152,256]{1,0:T(8,128)(2,1)S(1)} custom-call(bf16[4,1152,1152]{2,1,0:T(8,128)(2,1)} %bitcast.175, bf16[2304,256]{1,0:T(8,128)(2,1)S(1)} %get-tuple-element.77.refs_1_.refs_3_), custom_call_target="tpu_custom_call" | custom-call | tf_op jit(solution)/shard_map/pallas_call | solution.py:135
  267.5 11.9 %shard_map.433 = bf16[16,288,1152]{2,1,0:T(8,128)(2,1)} custom-call(bf16[1152,256]{1,0:T(8,128)(2,1)} %add_convert_fusion.5.refs_1_.refs_0_, bf16[1152,256]{1,0:T(8,128)(2,1)} %collective-permute-done.14.refs_2_.refs_1_, bf16[2304,256]{1,0:T(8,128)(2,1)S(1)} %get-tuple-element.79.refs_2_.refs_1_, bf16[2304,256]{1,0:T(8,128)(2,1)} %copy-done.9, ...), custom_call_target="tpu_custom_call" | custom-call | tf_op jit(solution)/shard_map/pallas_call | solution.py:135
  282.3 13.7 %shard_map.434 = f32[1152,256]{1,0:T(8,128)S(1)} custom-call(bf16[4,1152,1152]{2,1,0:T(8,128)(2,1)} %bitcast.176, bf16[2304,256]{1,0:T(8,128)(2,1)S(1)} %copy-done.8), custom_call_target="tpu_custom_call" | custom-call | tf_op jit(solution)/shard_map/pallas_call | solution.py:135
  305.2 5.7 %collective-permute-done.18.refs_2_.refs_7_ = bf16[1152,256]{1,0:T(8,128)(2,1)S(1)} collective-permute-done((bf16[1152,256]{1,0:T(8,128)(2,1)S(1)}, bf16[1152,256]{1,0:T(8,128)(2,1)S(1)}, u32[]{:S(2)}, u32[]{:S(2)}) %collective-permute-start.18) | collective-permute-done | bytes 589856 | tf_op jit(solution)/shard_map/ppermute | solution.py:42
  314.9 5.3 shard_map.437
  325.7 6.8 %shard_map.439 = bf16[16,288,576]{2,1,0:T(8,128)(2,1)} custom-call(bf16[1152,256]{1,0:T(8,128)(2,1)} %fusion.35.refs_1_.refs_0_, bf16[1152,256]{1,0:T(8,128)(2,1)} %collective-permute-done.12.refs_1_, bf16[576,256]{1,0:T(8,128)(2,1)S(1)} %get-tuple-element.85.refs_2_.refs_1_, bf16[576,256]{1,0:T(8,128)(2,1)S(1)} %get-tuple-element.82.refs_1_.refs_3_, ...), custom_call_target="tpu_custom_call" | custom-call | tf_op jit(solution)/shard_map/pallas_call | solution.py:135
  345.5 6.4 %shard_map.430 = bf16[1152,256]{1,0:T(8,128)(2,1)} custom-call(bf16[4,1152,1152]{2,1,0:T(8,128)(2,1)} %bitcast.177, bf16[4,1152,1152]{2,1,0:T(8,128)(2,1)} %bitcast.178, bf16[2304,256]{1,0:T(8,128)(2,1)S(1)} %copy-done.6), custom_call_target="tpu_custom_call" | custom-call | tf_op jit(solution)/shard_map/pallas_call | solution.py:135
  351.9 5.6 shard_map.429
  374.2 14.7 %shard_map.443 = (bf16[576,256]{1,0:T(8,128)(2,1)S(1)}, bf16[576,256]{1,0:T(8,128)(2,1)S(1)}, bf16[1152,256]{1,0:T(8,128)(2,1)S(1)}, bf16[1152,256]{1,0:T(8,128)...) custom-call(bf16[576,256]{1,0:T(8,128)(2,1)S(1)} %copy-done.27, bf16[576,256]{1,0:T(8,128)(2,1)S(1)} %copy-done.29, ...), custom_call_target="tpu_custom_call" | custom-call | tf_op jit(solution)/shard_map/pallas_call | solution.py:135
  389.4 8.8 %reduce-scatter.3.cloned.1.call-done = bf16[288,1152]{1,0:T(8,128)(2,1)} async-done(((bf16[4608,1152]{1,0:T(8,128)(2,1)}), bf16[288,1152]{1,0:T(8,128)(2,1)}) %reduce-scatter.3.cloned.1.call-update) | async-done | bytes 663568 | tf_op jit(solution)/shard_map/reduce_scatter | solution.py:484
  409.9 6.1 %shard_map.444 = bf16[1152,256]{1,0:T(8,128)(2,1)} custom-call(bf16[4,1152,1152]{2,1,0:T(8,128)(2,1)} %bitcast.170, bf16[576,256]{1,0:T(8,128)(2,1)S(1)} %get-tuple-element.87.refs_1_.refs_3_, bf16[1152,256]{1,0:T(8,128)(2,1)S(1)} %get-tuple-element.132.refs_2_.refs_7_), custom_call_target="tpu_custom_call" | custom-call | tf_op jit(solution)/shard_map/pallas_call | solution.py:135
  418.0 14.1 %shard_map.445 = bf16[4,4,288,576]{3,2,1,0:T(8,128)(2,1)} custom-call(s32[8]{0:T(128)S(1)} %stack.85.order_ref, bf16[1152,256]{1,0:T(8,128)(2,1)S(1)} %fusion.9.refs_1_.refs_0_.refs_4_, bf16[1152,256]{1,0:T(8,128)(2,1)S(1)} %collective-permute-done.8.refs_1_.refs_5_, bf16[576,256]{1,0:T(8,128)(2,1)S(1)} %get-tuple-element.93.refs_2_.refs_1_, ...), custom_call_target="tpu_custom_call" | custom-call | tf_op jit(solution)/shard_map/pallas_call | solution.py:361
  436.2 5.2 shard_map.446
  450.6 6.1 %all-to-all-start.3 = ((f32[8,1,2448]{2,1,0:T(1,128)}), f32[8,1,2448]{2,1,0:T(1,128)}, u32[]{:S(2)}, u32[]{:S(2)}) async-start(f32[8,1,2448]{2,1,0:T(1,128)} %reshape.310), calls=%async_computation.3 | async-start | bytes 163840 | tf_op jit(solution)/shard_map/all_to_all | solution.py:662
  462.9 9.5 %all-to-all-done.3 = f32[8,1,2448]{2,1,0:T(1,128)} async-done(((f32[8,1,2448]{2,1,0:T(1,128)}), f32[8,1,2448]{2,1,0:T(1,128)}, u32[]{:S(2)}, u32[]{:S(2)}) %all-to-all-start.3) | async-done | bytes 78368 | tf_op jit(solution)/shard_map/all_to_all | solution.py:662
  478.5 6.0 %collective-permute-start.24 = (bf16[1152,256]{1,0:T(8,128)(2,1)}, bf16[1152,256]{1,0:T(8,128)(2,1)}, u32[]{:S(2)}, u32[]{:S(2)}) collective-permute-start(bf16[1152,256]{1,0:T(8,128)(2,1)} %get-tuple-element.94), channel_id=1, source_target_pairs={{0,0},{1,1},{2,8},{3,9},{4,4},{5,5},{6,12},{7,13},{8,2},{9,3},{10,... | collective-permute-start | bytes 1769480 | tf_op jit(solution)/shard_map/ppermute | solution.py:424
  493.6 7.6 %all-gather.1 = f32[4,37,144]{2,1,0:T(8,128)S(1)} all-gather(f32[1,37,144]{2,1,0:T(8,128)S(1)} %maximum_bitcast_fusion), channel_id=2, replica_groups=mesh['row'=4,'col'=8] {'row'}, dimensions={0}, use_global_device_ids=true | all-gather | bytes 106560 | tf_op jit(solution)/shard_map/all_gather | solution.py:666
  504.0 6.0 %all-to-all-start = ((bf16[8,144,256]{2,1,0:T(8,128)(2,1)}), bf16[8,144,256]{2,1,0:T(8,128)(2,1)}, u32[]{:S(2)}, u32[]{:S(2)}) async-start(bf16[8,144,256]{2,1,0:T(8,128)(2,1)} %bitcast.44), calls=%async_computation | async-start | bytes 1179648 | tf_op jit(solution)/shard_map/all_to_all | solution.py:444
  530.4 10.5 %collective-permute-done.31 = bf16[288,576]{1,0:T(8,128)(2,1)S(1)} collective-permute-done((bf16[288,576]{1,0:T(8,128)(2,1)S(1)}, bf16[288,576]{1,0:T(8,128)(2,1)S(1)}, u32[]{:S(2)}, u32[]{:S(2)}) %collective-permute-start.31) | collective-permute-done | bytes 331808 | tf_op jit(solution)/shard_map/ppermute | solution.py:42
  540.9 17.2 %collective-permute-done.30 = bf16[288,576]{1,0:T(8,128)(2,1)} collective-permute-done((bf16[288,576]{1,0:T(8,128)(2,1)S(1)}, bf16[288,576]{1,0:T(8,128)(2,1)}, u32[]{:S(2)}, u32[]{:S(2)}) %collective-permute-start.30) | collective-permute-done | bytes 331808 | tf_op jit(solution)/shard_map/ppermute | solution.py:42
  (474 shorter events, 236.6 us)
Async XLA Ops:
  7.2 128.1 %all-gather.5.cloned.1.call-start = ((), (), s32[]{:S(2)}) async-start(), calls=%async_computation.6 | async-start | bytes 11280384 | tf_op jit(solution)/shard_map/all_gather | solution.py:479
  16.2 210.2 %all-gather.7.cloned.1.call-start = ((), (), s32[]{:S(2)}) async-start(), calls=%async_computation.7 | async-start | bytes 11280384 | tf_op jit(solution)/shard_map/all_gather | solution.py:479
  18.4 379.8 %reduce-scatter.3.cloned.1.call-start = ((), (), s32[]{:S(2)}) async-start(), calls=%async_computation.8 | async-start | bytes 11280384 | tf_op jit(solution)/shard_map/reduce_scatter | solution.py:484
  26.9 19.1 %collective-permute-start.1 = (bf16[1,144,686]{2,1,0:T(8,128)(2,1)}, bf16[1,144,686]{2,1,0:T(8,128)(2,1)S(1)}, u32[]{:S(2)}, u32[]{:S(2)}) collective-permute-start(bf16[1,144,686]{2,1,0:T(8,128)(2,1)} %get-tuple-element.144), channel_id=1, source_target_pairs={{0,1},{1,0},{2,9},{3,8},{4,5},{5,4},{6,13},{7,12},{8,3},{9,2},{10,... | collective-permute-start | bytes 592712 | tf_op jit(solution)/shard_map/ppermute | solution.py:435
  29.9 83.4 %collective-permute-start.7 = (bf16[1,144,686]{2,1,0:T(8,128)(2,1)}, bf16[1,144,686]{2,1,0:T(8,128)(2,1)S(1)}, u32[]{:S(2)}, u32[]{:S(2)}) collective-permute-start(bf16[1,144,686]{2,1,0:T(8,128)(2,1)} %get-tuple-element.138), channel_id=1, source_target_pairs={{0,13},{1,12},{2,5},{3,4},{4,9},{5,8},{6,1},{7,0},{8,15},{9,14},{1... | collective-permute-start | bytes 592712 | tf_op jit(solution)/shard_map/ppermute | solution.py:435
  34.6 78.7 %collective-permute-start.6 = (bf16[1,144,686]{2,1,0:T(8,128)(2,1)}, bf16[1,144,686]{2,1,0:T(8,128)(2,1)S(1)}, u32[]{:S(2)}, u32[]{:S(2)}) collective-permute-start(bf16[1,144,686]{2,1,0:T(8,128)(2,1)} %get-tuple-element.139), channel_id=1, source_target_pairs={{0,12},{1,13},{2,4},{3,5},{4,8},{5,9},{6,0},{7,1},{8,14},{9,15},{1... | collective-permute-start | bytes 592712 | tf_op jit(solution)/shard_map/ppermute | solution.py:435
  34.6 78.6 %collective-permute-start.5 = (bf16[1,144,686]{2,1,0:T(8,128)(2,1)}, bf16[1,144,686]{2,1,0:T(8,128)(2,1)S(1)}, u32[]{:S(2)}, u32[]{:S(2)}) collective-permute-start(bf16[1,144,686]{2,1,0:T(8,128)(2,1)} %get-tuple-element.140), channel_id=1, source_target_pairs={{0,5},{1,4},{2,13},{3,12},{4,1},{5,0},{6,9},{7,8},{8,7},{9,6},{10,... | collective-permute-start | bytes 592712 | tf_op jit(solution)/shard_map/ppermute | solution.py:435
  36.8 23.8 %collective-permute-start.2 = (bf16[1,144,686]{2,1,0:T(8,128)(2,1)}, bf16[1,144,686]{2,1,0:T(8,128)(2,1)S(1)}, u32[]{:S(2)}, u32[]{:S(2)}) collective-permute-start(bf16[1,144,686]{2,1,0:T(8,128)(2,1)} %get-tuple-element.143), channel_id=1, source_target_pairs={{0,8},{1,9},{2,0},{3,1},{4,12},{5,13},{6,4},{7,5},{8,10},{9,11},{1... | collective-permute-start | bytes 592712 | tf_op jit(solution)/shard_map/ppermute | solution.py:435
  45.9 29.4 %collective-permute-start.3 = (bf16[1,144,686]{2,1,0:T(8,128)(2,1)S(1)}, bf16[1,144,686]{2,1,0:T(8,128)(2,1)S(1)}, u32[]{:S(2)}, u32[]{:S(2)}) collective-permute-start(bf16[1,144,686]{2,1,0:T(8,128)(2,1)S(1)} %copy-done.71), channel_id=1, source_target_pairs={{0,9},{1,8},{2,1},{3,0},{4,13},{5,12},{6,5},{7,4},{8,11},{9,10},{1... | collective-permute-start | bytes 592712 | tf_op jit(solution)/shard_map/ppermute | solution.py:435
  60.6 52.5 %collective-permute-start.4 = (bf16[1,144,686]{2,1,0:T(8,128)(2,1)S(1)}, bf16[1,144,686]{2,1,0:T(8,128)(2,1)S(1)}, u32[]{:S(2)}, u32[]{:S(2)}) collective-permute-start(bf16[1,144,686]{2,1,0:T(8,128)(2,1)S(1)} %copy-done.70), channel_id=1, source_target_pairs={{0,4},{1,5},{2,12},{3,13},{4,0},{5,1},{6,8},{7,9},{8,6},{9,7},{10,... | collective-permute-start | bytes 592712 | tf_op jit(solution)/shard_map/ppermute | solution.py:435
  121.1 19.0 %collective-permute-start.8 = (bf16[1152,256]{1,0:T(8,128)(2,1)S(1)}, bf16[1152,256]{1,0:T(8,128)(2,1)S(1)}, u32[]{:S(2)}, u32[]{:S(2)}) collective-permute-start(bf16[1152,256]{1,0:T(8,128)(2,1)S(1)} %fusion.9.refs_1_.refs_0_.refs_4_), channel_id=1, source_target_pairs={{0,1},{1,0},{2,3},{3,2},{4,5},{5,4},{6,7},{7,6},{8,9},{9,8},{10,11... | collective-permute-start | bytes 1769480 | tf_op jit(solution)/shard_map/ppermute | solution.py:42
  176.0 17.1 %collective-permute-start.12 = (bf16[1152,256]{1,0:T(8,128)(2,1)}, bf16[1152,256]{1,0:T(8,128)(2,1)}, u32[]{:S(2)}, u32[]{:S(2)}) collective-permute-start(bf16[1152,256]{1,0:T(8,128)(2,1)} %fusion.35.refs_1_.refs_0_), channel_id=1, source_target_pairs={{0,1},{1,0},{2,3},{3,2},{4,5},{5,4},{6,7},{7,6},{8,9},{9,8},{10,11... | collective-permute-start | bytes 1769480 | tf_op jit(solution)/shard_map/ppermute | solution.py:42
  222.9 16.5 %collective-permute-start.14 = (bf16[1152,256]{1,0:T(8,128)(2,1)}, bf16[1152,256]{1,0:T(8,128)(2,1)}, u32[]{:S(2)}, u32[]{:S(2)}) collective-permute-start(bf16[1152,256]{1,0:T(8,128)(2,1)} %add_convert_fusion.5.refs_1_.refs_0_), channel_id=1, source_target_pairs={{0,1},{1,0},{2,3},{3,2},{4,5},{5,4},{6,7},{7,6},{8,9},{9,8},{10,11... | collective-permute-start | bytes 1769480 | tf_op jit(solution)/shard_map/ppermute | solution.py:42
  223.5 27.3 %collective-permute-start.16 = (bf16[1152,256]{1,0:T(8,128)(2,1)S(1)}, bf16[1152,256]{1,0:T(8,128)(2,1)}, u32[]{:S(2)}, u32[]{:S(2)}) collective-permute-start(bf16[1152,256]{1,0:T(8,128)(2,1)S(1)} %get-tuple-element.137.refs_2_.refs_4_), channel_id=1, source_target_pairs={{0,1},{1,0},{2,3},{3,2},{4,5},{5,4},{6,7},{7,6},{8,9},{9,8},{10,11... | collective-permute-start | bytes 1769480 | tf_op jit(solution)/shard_map/ppermute | solution.py:42
  279.4 282.6 %reduce-scatter.5.cloned.1.call-start = ((), (), s32[]{:S(2)}) async-start(), calls=%async_computation.9 | async-start | bytes 6266880 | tf_op jit(solution)/shard_map/reduce_scatter | solution.py:484
  280.4 15.7 %collective-permute-start.17 = (bf16[1152,256]{1,0:T(8,128)(2,1)S(1)}, bf16[1152,256]{1,0:T(8,128)(2,1)S(1)}, u32[]{:S(2)}, u32[]{:S(2)}) collective-permute-start(bf16[1152,256]{1,0:T(8,128)(2,1)S(1)} %copy-done.43), channel_id=1, source_target_pairs={{0,1},{1,0},{2,3},{3,2},{4,5},{5,4},{6,7},{7,6},{8,9},{9,8},{10,11... | collective-permute-start | bytes 1769480 | tf_op jit(solution)/shard_map/ppermute | solution.py:42
  338.1 31.8 %collective-permute-start.20 = (bf16[1152,256]{1,0:T(8,128)(2,1)S(1)}, bf16[1152,256]{1,0:T(8,128)(2,1)}, u32[]{:S(2)}, u32[]{:S(2)}) collective-permute-start(bf16[1152,256]{1,0:T(8,128)(2,1)S(1)} %multiply_convert_fusion.refs_2_.refs_8_), channel_id=1, source_target_pairs={{0,1},{1,0},{2,3},{3,2},{4,5},{5,4},{6,7},{7,6},{8,9},{9,8},{10,11... | collective-permute-start | bytes 1769480 | tf_op jit(solution)/shard_map/ppermute | solution.py:42
  343.5 54.7 %collective-permute-start.26 = (bf16[1152,120]{1,0:T(8,128)(2,1)}, bf16[1152,120]{1,0:T(8,128)(2,1)}, u32[]{:S(2)}, u32[]{:S(2)}) collective-permute-start(bf16[1152,120]{1,0:T(8,128)(2,1)} %shard_map.447), channel_id=1, source_target_pairs={{0,8},{8,0},{16,24},{24,16},{1,9},{9,1},{17,25},{25,17},{2,10},{10... | collective-permute-start | bytes 829448 | tf_op jit(solution)/shard_map/ppermute | solution.py:38
  360.9 80.7 %collective-permute-start.15 = (bf16[1152,256]{1,0:T(8,128)(2,1)}, bf16[1152,256]{1,0:T(8,128)(2,1)}, u32[]{:S(2)}, u32[]{:S(2)}) collective-permute-start(bf16[1152,256]{1,0:T(8,128)(2,1)} %shard_map.430), channel_id=1, source_target_pairs={{0,1},{1,0},{2,3},{3,2},{4,5},{5,4},{6,7},{7,6},{8,9},{9,8},{10,11... | collective-permute-start | bytes 1769480 | tf_op jit(solution)/shard_map/ppermute | solution.py:42
  388.8 18.9 %collective-permute-start.21 = (bf16[1152,256]{1,0:T(8,128)(2,1)}, bf16[1152,256]{1,0:T(8,128)(2,1)}, u32[]{:S(2)}, u32[]{:S(2)}) collective-permute-start(bf16[1152,256]{1,0:T(8,128)(2,1)} %get-tuple-element.89), channel_id=1, source_target_pairs={{0,8},{8,0},{16,24},{24,16},{1,9},{9,1},{17,25},{25,17},{2,10},{10... | collective-permute-start | bytes 1769480 | tf_op jit(solution)/shard_map/ppermute | solution.py:38
  389.1 18.7 %collective-permute-start.22 = (bf16[1152,256]{1,0:T(8,128)(2,1)S(1)}, bf16[1152,256]{1,0:T(8,128)(2,1)}, u32[]{:S(2)}, u32[]{:S(2)}) collective-permute-start(bf16[1152,256]{1,0:T(8,128)(2,1)S(1)} %get-tuple-element.92), channel_id=1, source_target_pairs={{0,8},{8,0},{16,24},{24,16},{1,9},{9,1},{17,25},{25,17},{2,10},{10... | collective-permute-start | bytes 1769480 | tf_op jit(solution)/shard_map/ppermute | solution.py:38
  400.1 50.6 %all-to-all-start.2 = ((bf16[8,144,120]{2,1,0:T(8,128)(2,1)}), bf16[8,144,120]{2,1,0:T(8,128)(2,1)}, u32[]{:S(2)}, u32[]{:S(2)}) async-start(bf16[8,144,120]{2,1,0:T(8,128)(2,1)} %bitcast.201), calls=%async_computation.2 | async-start | bytes 589824 | tf_op jit(solution)/shard_map/all_to_all | solution.py:645
  416.0 25.6 %collective-permute-start.23 = (bf16[1152,256]{1,0:T(8,128)(2,1)}, bf16[1152,256]{1,0:T(8,128)(2,1)}, u32[]{:S(2)}, u32[]{:S(2)}) collective-permute-start(bf16[1152,256]{1,0:T(8,128)(2,1)} %shard_map.444), channel_id=1, source_target_pairs={{0,1},{1,0},{2,3},{3,2},{4,5},{5,4},{6,7},{7,6},{8,9},{9,8},{10,11... | collective-permute-start | bytes 1769480 | tf_op jit(solution)/shard_map/ppermute | solution.py:42
  447.7 24.6 %collective-permute-start.25 = (bf16[1152,256]{1,0:T(8,128)(2,1)}, bf16[1152,256]{1,0:T(8,128)(2,1)S(1)}, u32[]{:S(2)}, u32[]{:S(2)}) collective-permute-start(bf16[1152,256]{1,0:T(8,128)(2,1)} %fusion.14), channel_id=1, source_target_pairs={{0,0},{1,1},{2,8},{3,9},{4,4},{5,5},{6,12},{7,13},{8,2},{9,3},{10,... | collective-permute-start | bytes 1769480 | tf_op jit(solution)/shard_map/ppermute | solution.py:424
  450.6 21.7 %all-to-all-start.3 = ((f32[8,1,2448]{2,1,0:T(1,128)}), f32[8,1,2448]{2,1,0:T(1,128)}, u32[]{:S(2)}, u32[]{:S(2)}) async-start(f32[8,1,2448]{2,1,0:T(1,128)} %reshape.310), calls=%async_computation.3 | async-start | bytes 163840 | tf_op jit(solution)/shard_map/all_to_all | solution.py:662
  461.4 49.8 %collective-permute-start.28 = (bf16[1,4,288,576]{3,2,1,0:T(8,128)(2,1)}, bf16[1,4,288,576]{3,2,1,0:T(8,128)(2,1)}, u32[]{:S(2)}, u32[]{:S(2)}) collective-permute-start(bf16[1,4,288,576]{3,2,1,0:T(8,128)(2,1)} %slice.294), channel_id=1, source_target_pairs={{0,16},{8,24},{16,0},{24,8},{1,17},{9,25},{17,1},{25,9},{2,18},{10... | collective-permute-start | bytes 3981320 | tf_op jit(solution)/shard_map/ppermute | solution.py:38
  473.2 30.9 %all-to-all-start.1 = ((bf16[8,144,256]{2,1,0:T(8,128)(2,1)}), bf16[8,144,256]{2,1,0:T(8,128)(2,1)S(1)}, u32[]{:S(2)}, u32[]{:S(2)}) async-start(bf16[8,144,256]{2,1,0:T(8,128)(2,1)} %bitcast.202), calls=%async_computation.1 | async-start | bytes 1179648 | tf_op jit(solution)/shard_map/all_to_all | solution.py:444
  478.5 25.5 %collective-permute-start.24 = (bf16[1152,256]{1,0:T(8,128)(2,1)}, bf16[1152,256]{1,0:T(8,128)(2,1)}, u32[]{:S(2)}, u32[]{:S(2)}) collective-permute-start(bf16[1152,256]{1,0:T(8,128)(2,1)} %get-tuple-element.94), channel_id=1, source_target_pairs={{0,0},{1,1},{2,8},{3,9},{4,4},{5,5},{6,12},{7,13},{8,2},{9,3},{10,... | collective-permute-start | bytes 1769480 | tf_op jit(solution)/shard_map/ppermute | solution.py:424
  504.0 23.3 %all-to-all-start = ((bf16[8,144,256]{2,1,0:T(8,128)(2,1)}), bf16[8,144,256]{2,1,0:T(8,128)(2,1)}, u32[]{:S(2)}, u32[]{:S(2)}) async-start(bf16[8,144,256]{2,1,0:T(8,128)(2,1)} %bitcast.44), calls=%async_computation | async-start | bytes 1179648 | tf_op jit(solution)/shard_map/all_to_all | solution.py:444
  513.9 16.5 %collective-permute-start.29 = (bf16[288,576]{1,0:T(8,128)(2,1)}, bf16[288,576]{1,0:T(8,128)(2,1)S(1)}, u32[]{:S(2)}, u32[]{:S(2)}) collective-permute-start(bf16[288,576]{1,0:T(8,128)(2,1)} %get-tuple-element.146), channel_id=1, source_target_pairs={{0,2},{1,3},{2,0},{3,1},{4,6},{5,7},{6,4},{7,5},{8,10},{9,11},{10,... | collective-permute-start | bytes 995336 | tf_op jit(solution)/shard_map/ppermute | solution.py:42
  515.9 25.0 %collective-permute-start.31 = (bf16[288,576]{1,0:T(8,128)(2,1)S(1)}, bf16[288,576]{1,0:T(8,128)(2,1)S(1)}, u32[]{:S(2)}, u32[]{:S(2)}) collective-permute-start(bf16[288,576]{1,0:T(8,128)(2,1)S(1)} %get-tuple-element.147), channel_id=1, source_target_pairs={{0,6},{1,7},{2,4},{3,5},{4,2},{5,3},{6,0},{7,1},{8,14},{9,15},{10,... | collective-permute-start | bytes 995336 | tf_op jit(solution)/shard_map/ppermute | solution.py:42
  518.3 39.8 %collective-permute-start.30 = (bf16[288,576]{1,0:T(8,128)(2,1)S(1)}, bf16[288,576]{1,0:T(8,128)(2,1)}, u32[]{:S(2)}, u32[]{:S(2)}) collective-permute-start(bf16[288,576]{1,0:T(8,128)(2,1)S(1)} %get-tuple-element.148), channel_id=1, source_target_pairs={{0,4},{1,5},{2,6},{3,7},{4,0},{5,1},{6,2},{7,3},{8,12},{9,13},{10,... | collective-permute-start | bytes 995336 | tf_op jit(solution)/shard_map/ppermute | solution.py:42
  (127 other events, 757.6 us)
Sparse Core Ops, SparseCore 0:
  16.3 118.9 all-gather.4
  138.1 87.1 all-gather.6
  279.5 118.6 reduce-scatter.2
  402.0 99.0 reduce-scatter.4

commit v4 on v3

--- a/solution.py
+++ b/solution.py
@@ -13,6 +13,7 @@
 
 NORM_EPS = 1e-06
 MASK_FILL = -1e30
+COST_SCALE = 3
 BF = jnp.bfloat16
 F32 = jnp.float32
 LOG_SCALE = HD ** -0.5 * 1.4426950408889634
@@ -131,9 +132,20 @@
     return pl.BlockSpec(tuple(shape), lambda z: (0,) * len(shape))
 
 
-def call_parts(kernel, steps, args, arg_specs, outs, out_specs, scratch=()):
+def cost_of(args, outs, flops):
+    total = sum(a.size * a.dtype.itemsize for a in args)
+    for out in jax.tree.leaves(outs):
+        size = 1
+        for n in out.shape:
+            size *= n
+        total += size * jnp.dtype(out.dtype).itemsize
+    return pl.CostEstimate(flops=int(flops), bytes_accessed=int(total), transcendentals=0)
+
+
+def call_parts(kernel, steps, args, arg_specs, outs, out_specs, scratch=(), flops=0):
     return pl.pallas_call(
         kernel,
+        cost_estimate=cost_of(args, outs, COST_SCALE * flops),
         grid=(steps,),
         in_specs=arg_specs,
         out_specs=out_specs,
@@ -152,7 +164,8 @@
     if length is not None:
         args, specs = [length] + args, [pl.BlockSpec(memory_space=pltpu.SMEM)] + specs
     kernel = functools.partial(forward_kernel, len(q_parts), len(kv_parts), length is not None)
-    res = call_parts(kernel, half, args, specs, outs, [part_spec(o.shape, half) for o in outs])
+    flops = 4 * sum(q.size for q in q_parts) * sum(k.shape[1] for k in kv_parts)
+    res = call_parts(kernel, half, args, specs, outs, [part_spec(o.shape, half) for o in outs], flops=4 * flops)
     return res[:-1], res[-1]
 
 
@@ -163,7 +176,8 @@
     if length is not None:
         args, specs = [length] + args, [pl.BlockSpec(memory_space=pltpu.SMEM)] + specs
     kernel = functools.partial(backward_kernel, len(q_parts), len(kv_parts), length is not None)
-    res = call_parts(kernel, half, args, specs, outs, [part_spec(o.shape, half) for o in outs])
+    flops = 10 * sum(q.size for q in q_parts) * sum(k.shape[1] for k in kv_parts)
+    res = call_parts(kernel, half, args, specs, outs, [part_spec(o.shape, half) for o in outs], flops=3 * flops)
     return res[: len(q_parts)], res[len(q_parts) :]
 
 
@@ -240,7 +254,8 @@
     specs = view.specs() + [whole_spec(v.shape) for v in values] + [part_spec(extra.shape, half)]
     outs = [jax.ShapeDtypeStruct((rows, cols), dtype) for rows, cols, dtype in outs]
     kernel = functools.partial(kernel, view, len(values))
-    return call_parts(kernel, half, args, specs, outs, [part_spec(o.shape, half) for o in outs])
+    flops = 2 * half * view.size * sum(v.size for v in values)
+    return call_parts(kernel, half, args, specs, outs, [part_spec(o.shape, half) for o in outs], flops=flops)
 
 
 def out_kernel(view, *refs):
@@ -279,6 +294,7 @@
         out,
         whole_spec(out.shape),
         [pltpu.VMEM((D, tokens), F32)],
+        flops=2 * D * sum(v.size for v in values),
     )
 
 
@@ -335,7 +351,8 @@
     out = jax.ShapeDtypeStruct((half * rows, chunk, sum(sizes)), BF)
     out_spec = pl.BlockSpec((rows, chunk, sum(sizes)), lambda z: (z, 0, 0))
     kernel = functools.partial(outer_kernel, [len(a) for a, _ in pairs])
-    return call_parts(kernel, half, args, specs, out, out_spec)
+    flops = sum(2 * p.size * D for _, b in pairs for p in b)
+    return call_parts(kernel, half, args, specs, out, out_spec, flops=flops)
 
 
 def tree_kernel(terms, order_ref, *refs):
@@ -350,8 +367,8 @@
         start, at = end, at + 2 * count
 
 
-def tree_blocks(pairs, rows, half, row_order, col_order):
-    chunk = D // rows
+def tree_blocks(pairs, chunk, half, row_order, col_order):
+    rows = len(row_order)
     sizes = [b[0].shape[0] // half for _, b in pairs]
     specs, args = [], []
     for (a, b), n in zip(pairs, sizes):
@@ -360,6 +377,7 @@
         args += list(a) + list(b)
     return pl.pallas_call(
         functools.partial(tree_kernel, [len(a) for a, _ in pairs]),
+        cost_estimate=cost_of(args, [], COST_SCALE * sum(2 * p.size * D for _, b in pairs for p in b) * rows * chunk // D),
         grid_spec=pltpu.PrefetchScalarGridSpec(
             num_scalar_prefetch=1,
             grid=(rows, half),
@@ -489,14 +507,13 @@
         order = [i for j in order for i in (j, j | (1 << (row_bits - 1 - b)))]
     order = sorted(order, key=lambda i: int(format(i, f"0{row_bits}b")[::-1], 2))
 
-    def tree_outer(pairs):
-        return tree_blocks(pairs, rows, half, [r ^ i for i in order], [(c >> 1) ^ e for e in range(half)])
-
-    def tree_reduce(blocks):
-        for b in range(row_bits):
-            h = blocks.shape[0] // 2
-            received = row_swap(blocks[h:], rows, 1 << b)
-            blocks = (blocks[:h].astype(F32) + received.astype(F32)).astype(BF)
+    def tree_outer(pairs, part):
+        return tree_blocks(pairs, D // rows, half, [r ^ i for i in part], [(c >> 1) ^ e for e in range(half)])
+
+    def tree_add(kept, sent, bit):
+        return (kept.astype(F32) + row_swap(sent, rows, bit).astype(F32)).astype(BF)
+
+    def tree_columns(blocks):
         total = blocks[0, 0].astype(F32)
         for e in range(1, half):
             total = total + col_swap(blocks[0, e], cols, e << 1).astype(F32)
@@ -588,13 +605,10 @@
     mlp_full = gather_pair((normed_m * (1.0 + scale_m) + shift_m).astype(BF))
     hidden_outs = [(hidden_w, width, BF)] * 2
     *hidden, slope = apply_in(gelu_kernel, up_w, mlp_full, up_b, hidden_outs + [(hidden_w, 2 * width, F32)])
-    branch_m = reduce_pair(down_w, hidden)[0] + down_b
-    block_out = (after_cross + gate_m * branch_m).astype(BF)
 
     grad_mlp = gate_m * cot
     low_full = gather_pair(grad_mlp.astype(BF))
     g_down_b = jnp.sum(grad_mlp, axis=1)
-    g_gate_m = jnp.sum(cot * branch_m, axis=1)
     *grad_pre, g_up_b = apply_in(slope_kernel, down_w, low_full, slope, hidden_outs + [(hidden_w, 1, F32)])
 
     def mlp_cover(other):
@@ -625,19 +639,29 @@
     dq, dkv = attend_backward(q_parts, kv_all, None, lse, datt, half)
     dkv = reduce_keys(dkv)
 
+    def attention_pairs(tie):
+        return [(attn_full, [after(dq[0], tie), dq[1]]), (attn_full, dkv), (low_attn, att)]
+
     def attention_cover(other):
-        return tree_outer([(attn_full, [after(dq[0], other), dq[1]]), (attn_full, dkv), (low_attn, att)])
-
-    back_att, att_blocks = reduce_pair(qkv_w, dq, dkv, cover=attention_cover)
-    cross_grads = scatter(after(cross_blocks, mlp_grads, dq[0]))
-    att_grads = tree_reduce(att_blocks)
+        return tree_outer(attention_pairs(other), order[rows // 2 :])
+
+    back_att, sent = reduce_pair(qkv_w, dq, dkv, cover=attention_cover)
+    cross_grads = scatter(after(cross_blocks, mlp_grads, sent))
+    tree = tree_add(tree_outer(attention_pairs(sent), order[: rows // 2]), sent, 1)
+    branch_m = reduce_pair(down_w, [after(hidden[0], tree), hidden[1]])[0] + down_b
+    g_gate_m = jnp.sum(cot * branch_m, axis=1)
+    for b in range(1, row_bits):
+        h = tree.shape[0] // 2
+        tree = tree_add(tree[:h], tree[h:], 1 << b)
+    att_grads = tree_columns(tree)
     g_cq, g_ck, g_cv, g_cout = unpack(cross_grads, [feat] * 4)
     g_q, g_k, g_v, g_out = unpack(att_grads, [feat] * 4)
     g_up, g_down = mlp_grads[:, :ups].astype(F32), mlp_grads[:, ups:].astype(F32)
     g_q_b = jnp.sum(sum(p.astype(F32) for p in dq), axis=1)
     g_v_b = jnp.sum(sum(p.astype(F32) for p in dkv).reshape(half, 2, feat, width)[:, 1], axis=2)
     back_a, g_shift_a, g_scale_a = norm_backward(back_att, normed_a, inv_a, scale_a)
-    block_output = tokens_out(after(block_out, back_att))
+    block_out = (after_cross + gate_m * branch_m).astype(BF)
+    block_output = tokens_out(block_out)
     grad_input = tokens_out((grad_res + back_a).astype(BF))
     grad_text = apply_out(ckv_w, dckv, BF)
     grad_text = grad_text.astype(F32) + row_swap(grad_text, rows, 1).astype(F32)
@@ -658,7 +682,7 @@
     blocks = []
     for j in range(cols):
         blocks.append(jnp.where(side == (j & 1), col_g[j >> 1], 0.0))
-    small_g = jnp.concatenate([model_g, jnp.stack(blocks)], axis=1)
+    small_g = after(jnp.concatenate([model_g, jnp.stack(blocks)], axis=1), tree)
     small_g = lax.all_to_all(small_g, "col", 0, 0, tiled=True)
     mod_g = small_g[:, :6].reshape(2, cols // 8, 2, 2, 6, feat).sum(axis=(1, 3))
     bias_g = small_g[:, 6:].sum(axis=0)

time: 582 us -> 596 us (1.024)
  waiting for transfers between devices: 139 us -> 162 us
    ppermute x7, waiting for transfers between devices: 1.76 us -> 38.6 us  [row_swap(): return lax.ppermute(value, 'row', [(i, i ^ bit) for i in range(rows)])]
    ppermute x15, waiting for transfers between devices: 66.5 us -> 39.1 us  [col_swap(): return lax.ppermute(value, 'col', [(i, i ^ mask) for i in range(cols)])]
    all_to_all x2, waiting for transfers between devices: 2.07 us -> 21.8 us  [tokens_out(): blocks = lax.all_to_all(blocks, 'col', 0, 0, tiled=True)]
    reduce_scatter x2, waiting for transfers between devices: 8.76 us -> 0.01 us  [scatter(): lax.psum_scatter(flat, ('row', 'col'), scatter_dimension=0, tiled=True, a...]
    pallas_call x33, Pallas kernels: 182 us -> 176 us  [call_parts(): pl.pallas_call(kernel, cost_estimate=cost_of(args, outs, COST_SCALE * flo...]
    all_to_all x2, starting transfers between devices: 9.53 us -> 15.8 us  [tokens_out(): blocks = lax.all_to_all(blocks, 'col', 0, 0, tiled=True)]
    unnamed x254 -> x332, local copies, waits for them, and re-layouts: 28.2 us -> 31.4 us
    pallas_call x1 -> x2, Pallas kernels: 14.1 us -> 15.9 us  [tree_blocks(): pl.pallas_call(functools.partial(tree_kernel, [len(a) for a, _ in pairs])...]
  transfers between devices with their start and end apart: 40 -> 40, of which waited for: 13 -> 15; matrix products, arithmetic and copies ran while one was open for 17% -> 15% of each run, Pallas kernels for 29% -> 28%
where the time goes in v4:
time: 596 us; the launch traced here: 585 us
  Pallas kernels  192 us (32%)
  waiting for transfers between devices  162 us (27%)
  starting transfers between devices  96.9 us (16%)
  local copies, waits for them, and re-layouts  56 us (9%)
  other arithmetic  50.2 us (8%)
  between operations  16.9 us (3%)
    pallas_call x33, Pallas kernels, call_parts(): pl.pallas_call(kernel, cost_estimate=cost_of(args, outs, COST_SCALE * flo...  176 us
    ppermute x8, waiting for transfers between devices, send_tokens(): part = lax.ppermute(part, ('row', 'col'), pairs)  43.6 us
    ppermute x8, starting transfers between devices, send_tokens(): part = lax.ppermute(part, ('row', 'col'), pairs)  42.6 us
    ppermute x15, waiting for transfers between devices, col_swap(): return lax.ppermute(value, 'col', [(i, i ^ mask) for i in range(cols)])  39.1 us
    ppermute x7, waiting for transfers between devices, row_swap(): return lax.ppermute(value, 'row', [(i, i ^ bit) for i in range(rows)])  38.6 us
    unnamed x332, local copies, waits for them, and re-layouts  31.4 us
    all_to_all x2, waiting for transfers between devices, tokens_out(): blocks = lax.all_to_all(blocks, 'col', 0, 0, tiled=True)  21.8 us
    ppermute x15, starting transfers between devices, col_swap(): return lax.ppermute(value, 'col', [(i, i ^ mask) for i in range(cols)])  20 us
  transfers between devices with their start and end apart: 40, of which 15 were waited for; matrix products, arithmetic and copies ran while one was open for 15% of the time, Pallas kernels for 28%

profile of v4, /device:TPU:0, one launch (start us, length us, event | category | flops | bytes accessed | tf_op | source)
XLA Modules:
  0.0 585.3 jit_solution(4896252580914755082)
XLA Ops:
  36.6 8.5 %collective-permute-start.2 = (bf16[1,144,686]{2,1,0:T(8,128)(2,1)}, bf16[1,144,686]{2,1,0:T(8,128)(2,1)S(1)}, u32[]{:S(2)}, u32[]{:S(2)}) collective-permute-start(bf16[1,144,686]{2,1,0:T(8,128)(2,1)} %get-tuple-element.144), channel_id=1, source_target_pairs={{0,8},{1,9},{2,0},{3,1},{4,12},{5,13},{6,4},{7,5},{8,10},{9,11},{1... | collective-permute-start | bytes 592712 | tf_op jit(solution)/shard_map/ppermute | solution.py:453
  45.3 9.2 %collective-permute-start.3 = (bf16[1,144,686]{2,1,0:T(8,128)(2,1)S(1)}, bf16[1,144,686]{2,1,0:T(8,128)(2,1)S(1)}, u32[]{:S(2)}, u32[]{:S(2)}) collective-permute-start(bf16[1,144,686]{2,1,0:T(8,128)(2,1)S(1)} %copy-done.104), channel_id=1, source_target_pairs={{0,9},{1,8},{2,1},{3,0},{4,13},{5,12},{6,5},{7,4},{8,11},{9,10},{1... | collective-permute-start | bytes 592712 | tf_op jit(solution)/shard_map/ppermute | solution.py:453
  54.5 5.9 %collective-permute-done.2 = bf16[1,144,686]{2,1,0:T(8,128)(2,1)S(1)} collective-permute-done((bf16[1,144,686]{2,1,0:T(8,128)(2,1)}, bf16[1,144,686]{2,1,0:T(8,128)(2,1)S(1)}, u32[]{:S(2)}, u32[]{:S(2)}) %collective-permute-start.2) | collective-permute-done | bytes 197600 | tf_op jit(solution)/shard_map/ppermute | solution.py:453
  60.5 14.8 %collective-permute-start.4 = (bf16[1,144,686]{2,1,0:T(8,128)(2,1)S(1)}, bf16[1,144,686]{2,1,0:T(8,128)(2,1)S(1)}, u32[]{:S(2)}, u32[]{:S(2)}) collective-permute-start(bf16[1,144,686]{2,1,0:T(8,128)(2,1)S(1)} %copy-done.103), channel_id=1, source_target_pairs={{0,4},{1,5},{2,12},{3,13},{4,0},{5,1},{6,8},{7,9},{8,6},{9,7},{10,... | collective-permute-start | bytes 592712 | tf_op jit(solution)/shard_map/ppermute | solution.py:453
  75.4 37.6 %collective-permute-done.4 = bf16[1,144,686]{2,1,0:T(8,128)(2,1)S(1)} collective-permute-done((bf16[1,144,686]{2,1,0:T(8,128)(2,1)S(1)}, bf16[1,144,686]{2,1,0:T(8,128)(2,1)S(1)}, u32[]{:S(2)}, u32[]{:S(2)}) %collective-permute-start.4) | collective-permute-done | bytes 197600 | tf_op jit(solution)/shard_map/ppermute | solution.py:453
  127.3 8.1 %all-gather.5.cloned.1.call-done = bf16[4608,1152]{1,0:T(8,128)(2,1)} async-done(((bf16[288,1152]{1,0:T(8,128)(2,1)}), bf16[4608,1152]{1,0:T(8,128)(2,1)}) %all-gather.5.cloned.1.call-update) | async-done | bytes 10616848 | tf_op jit(solution)/shard_map/all_gather | solution.py:497
  146.6 8.9 %shard_map.419 = (bf16[576,256]{1,0:T(8,128)(2,1)S(1)}, bf16[576,256]{1,0:T(8,128)(2,1)S(1)}, f32[4,512,2]{2,1,0:T(8,128)}) custom-call(bf16[576,256]{1,0:T(8,128)(2,1)S(1)} %get-tuple-element.65.refs_0_, bf16[576,256]{1,0:T(8,128)(2,1)S(1)} %get-tuple-element.66.refs_1_, bf16[1152,256]{1,0:T(8,128)(2,1)S(1)} %get-tuple-element.67.refs_2_, ...), custom_call_target="tpu_custom_call" | custom-call | flops 14495514624 | bytes 3555328 | tf_op jit(solution)/shard_map/pallas_call | solution.py:146
  164.9 10.2 %collective-permute-done.11 = bf16[1152,256]{1,0:T(8,128)(2,1)S(1)} collective-permute-done((bf16[1152,256]{1,0:T(8,128)(2,1)S(1)}, bf16[1152,256]{1,0:T(8,128)(2,1)S(1)}, u32[]{:S(2)}, u32[]{:S(2)}) %collective-permute-start.11) | collective-permute-done | bytes 589856 | tf_op jit(solution)/shard_map/ppermute | solution.py:43
  179.8 5.1 shard_map.424.refs_3_
  207.3 8.6 %collective-permute-done.13 = bf16[1152,256]{1,0:T(8,128)(2,1)S(1)} collective-permute-done((bf16[1152,256]{1,0:T(8,128)(2,1)S(1)}, bf16[1152,256]{1,0:T(8,128)(2,1)S(1)}, u32[]{:S(2)}, u32[]{:S(2)}) %collective-permute-start.13) | collective-permute-done | bytes 589856 | tf_op jit(solution)/shard_map/ppermute | solution.py:43
  225.3 9.9 %collective-permute-done.14.refs_2_.refs_1_ = bf16[1152,256]{1,0:T(8,128)(2,1)S(1)} collective-permute-done((bf16[1152,256]{1,0:T(8,128)(2,1)S(1)}, bf16[1152,256]{1,0:T(8,128)(2,1)S(1)}, u32[]{:S(2)}, u32[]{:S(2)}) %collective-permute-start.14) | collective-permute-done | bytes 589856 | tf_op jit(solution)/shard_map/ppermute | solution.py:43
  238.2 9.1 %shard_map.428 = (bf16[2304,256]{1,0:T(8,128)(2,1)S(1)}, bf16[2304,256]{1,0:T(8,128)(2,1)S(1)}, f32[2304,512]{1,0:T(8,128)}) custom-call(bf16[4,1152,1152]{2,1,0:T(8,128)(2,1)} %bitcast.172, bf16[1152,256]{1,0:T(8,128)(2,1)S(1)} %copy-done.41, bf16[1152,256]{1,0:T(8,128)(2,1)S(1)} %copy-done.72, f32[2304,1]{1,0:T(8,128)} %reshape.295.refs_3_), custom_call_target="tpu_custom_call" | custom-call | flops 8153726976 | bytes 18883584 | tf_op jit(solution)/shard_map/pallas_call | solution.py:146
  249.3 10.2 %shard_map.429 = (bf16[2304,256]{1,0:T(8,128)(2,1)S(1)}, bf16[2304,256]{1,0:T(8,128)(2,1)S(1)}, f32[2304,1]{1,0:T(8,128)}) custom-call(bf16[4,1152,1152]{2,1,0:T(8,128)(2,1)} %bitcast.173, bf16[4,1152,1152]{2,1,0:T(8,128)(2,1)} %bitcast.174, bf16[1152,256]{1,0:T(8,128)(2,1)} %get-tuple-element.138.refs_2_.refs_4_, ...), custom_call_target="tpu_custom_call" | custom-call | flops 8153726976 | bytes 29500416 | tf_op jit(solution)/shard_map/pallas_call | solution.py:146
  259.5 6.8 %shard_map.430 = bf16[1152,256]{1,0:T(8,128)(2,1)} custom-call(bf16[4,1152,1152]{2,1,0:T(8,128)(2,1)} %bitcast.175, bf16[2304,256]{1,0:T(8,128)(2,1)S(1)} %get-tuple-element.77.refs_1_.refs_3_), custom_call_target="tpu_custom_call" | custom-call | flops 4076863488 | bytes 12386304 | tf_op jit(solution)/shard_map/pallas_call | solution.py:146
  266.4 11.7 %shard_map.431 = bf16[16,288,1152]{2,1,0:T(8,128)(2,1)} custom-call(bf16[1152,256]{1,0:T(8,128)(2,1)S(1)} %copy-done.42, bf16[1152,256]{1,0:T(8,128)(2,1)S(1)} %copy-done.73, bf16[2304,256]{1,0:T(8,128)(2,1)S(1)} %get-tuple-element.80.refs_2_.refs_1_, bf16[2304,256]{1,0:T(8,128)(2,1)} %copy-done.80, bf16[1152,256]{1,0:T(8,128)(2,1)} %get-tuple-element.138.refs_2_.refs_4_, ...), custom_call_target="tpu_custom_call" | custom-call | flops 16307453952 | bytes 17694720 | tf_op jit(solution)/shard_map/pallas_call | solution.py:146
  279.6 5.2 shard_map.432
  307.0 5.3 shard_map.435
  327.7 6.6 %shard_map.437 = bf16[16,288,576]{2,1,0:T(8,128)(2,1)} custom-call(bf16[1152,256]{1,0:T(8,128)(2,1)S(1)} %copy-done.15, bf16[1152,256]{1,0:T(8,128)(2,1)} %collective-permute-done.12.refs_1_, bf16[576,256]{1,0:T(8,128)(2,1)S(1)} %copy-done.23, bf16[576,256]{1,0:T(8,128)(2,1)S(1)} %copy-done.25, bf16[1152,120]{1,0:T(8,128)(2,1)S(1)} %copy-done.21, ...), custom_call_target="tpu_custom_call" | custom-call | flops 5032378368 | bytes 9400320 | tf_op jit(solution)/shard_map/pallas_call | solution.py:146
  342.9 6.4 %shard_map.446 = bf16[1152,256]{1,0:T(8,128)(2,1)} custom-call(bf16[4,1152,1152]{2,1,0:T(8,128)(2,1)} %bitcast.177, bf16[4,1152,1152]{2,1,0:T(8,128)(2,1)} %bitcast.178, bf16[2304,256]{1,0:T(8,128)(2,1)S(1)} %copy-done.19), custom_call_target="tpu_custom_call" | custom-call | flops 4076863488 | bytes 23003136 | tf_op jit(solution)/shard_map/pallas_call | solution.py:146
  352.4 5.0 shard_map.448
  365.5 14.0 %shard_map.441 = (bf16[576,256]{1,0:T(8,128)(2,1)S(1)}, bf16[576,256]{1,0:T(8,128)(2,1)S(1)}, bf16[1152,256]{1,0:T(8,128)(2,1)S(1)}, bf16[1152,256]{1,0:T(8,128)...) custom-call(bf16[576,256]{1,0:T(8,128)(2,1)S(1)} %copy-done.75, bf16[576,256]{1,0:T(8,128)(2,1)S(1)} %copy-done.77, ...), custom_call_target="tpu_custom_call" | custom-call | flops 27179089920 | bytes 6504448 | tf_op jit(solution)/shard_map/pallas_call | solution.py:146
  394.8 6.6 %shard_map.442 = bf16[1152,256]{1,0:T(8,128)(2,1)} custom-call(bf16[4,1152,1152]{2,1,0:T(8,128)(2,1)} %bitcast.170, bf16[576,256]{1,0:T(8,128)(2,1)S(1)} %copy-done.30, bf16[1152,256]{1,0:T(8,128)(2,1)S(1)} %get-tuple-element.134.refs_2_.refs_7_), custom_call_target="tpu_custom_call" | custom-call | flops 3057647616 | bytes 12091392 | tf_op jit(solution)/shard_map/pallas_call | solution.py:146
  401.4 7.9 %shard_map.443 = bf16[2,4,288,576]{3,2,1,0:T(8,128)(2,1)} custom-call(s32[6]{0:T(128)S(1)} %stack.93.order_ref, bf16[1152,256]{1,0:T(8,128)(2,1)S(1)} %copy-done.12, bf16[1152,256]{1,0:T(8,128)(2,1)S(1)} %copy-done.35, bf16[576,256]{1,0:T(8,128)(2,1)S(1)} %copy-done.27, bf16[576,256]{1,0:T(8,128)(2,1)S(1)} %copy-done.30, bf16[1152,256]{1,0:T(8,128)(2,1)S(1)} %copy-done.12, ...), custom_call_target="tpu_custom_call" | custom-call | flops 4076863488 | bytes 5898240 | tf_op jit(solution)/shard_map/pallas_call | solution.py:378
  418.0 5.5 shard_map.447
  423.6 8.0 %shard_map.444 = bf16[2,4,288,576]{3,2,1,0:T(8,128)(2,1)} custom-call(s32[6]{0:T(128)S(1)} %stack.90.order_ref, bf16[1152,256]{1,0:T(8,128)(2,1)S(1)} %copy-done.13, bf16[1152,256]{1,0:T(8,128)(2,1)S(1)} %copy-done.36, bf16[576,256]{1,0:T(8,128)(2,1)S(1)} %copy-done.28, bf16[576,256]{1,0:T(8,128)(2,1)S(1)} %copy-done.31, bf16[1152,256]{1,0:T(8,128)(2,1)S(1)} %copy-done.13, ...), custom_call_target="tpu_custom_call" | custom-call | flops 4076863488 | bytes 5898240 | tf_op jit(solution)/shard_map/pallas_call | solution.py:378
  438.9 5.5 shard_map.445
  451.0 36.8 %collective-permute-done.28 = bf16[1,4,288,576]{3,2,1,0:T(8,128)(2,1)} collective-permute-done((bf16[1,4,288,576]{3,2,1,0:T(8,128)(2,1)}, bf16[1,4,288,576]{3,2,1,0:T(8,128)(2,1)}, u32[]{:S(2)}, u32[]{:S(2)}) %collective-permute-start.28) | collective-permute-done | bytes 1327136 | tf_op jit(solution)/shard_map/ppermute | solution.py:39
  495.4 8.0 %all-to-all-done.3 = f32[8,1,2448]{2,1,0:T(1,128)S(1)} async-done(((f32[8,1,2448]{2,1,0:T(1,128)}), f32[8,1,2448]{2,1,0:T(1,128)S(1)}, u32[]{:S(2)}, u32[]{:S(2)}) %all-to-all-start.3) | async-done | bytes 78368 | tf_op jit(solution)/shard_map/all_to_all | solution.py:686
  507.1 6.0 %collective-permute-start.24 = (bf16[1152,256]{1,0:T(8,128)(2,1)}, bf16[1152,256]{1,0:T(8,128)(2,1)}, u32[]{:S(2)}, u32[]{:S(2)}) collective-permute-start(bf16[1152,256]{1,0:T(8,128)(2,1)} %get-tuple-element.137), channel_id=1, source_target_pairs={{0,0},{1,1},{2,8},{3,9},{4,4},{5,5},{6,12},{7,13},{8,2},{9,3},{10,... | collective-permute-start | bytes 1769480 | tf_op jit(solution)/shard_map/ppermute | solution.py:442
  525.6 12.2 %all-to-all-start = ((bf16[8,144,256]{2,1,0:T(8,128)(2,1)}), bf16[8,144,256]{2,1,0:T(8,128)(2,1)}, u32[]{:S(2)}, u32[]{:S(2)}) async-start(bf16[8,144,256]{2,1,0:T(8,128)(2,1)} %bitcast.44), calls=%async_computation | async-start | bytes 1179648 | tf_op jit(solution)/shard_map/all_to_all | solution.py:462
  537.9 5.7 all-gather.1
  551.4 17.8 %all-to-all-done = bf16[8,144,256]{2,1,0:T(8,128)(2,1)} async-done(((bf16[8,144,256]{2,1,0:T(8,128)(2,1)}), bf16[8,144,256]{2,1,0:T(8,128)(2,1)}, u32[]{:S(2)}, u32[]{:S(2)}) %all-to-all-start) | async-done | bytes 589856 | tf_op jit(solution)/shard_map/all_to_all | solution.py:462
  (553 shorter events, 241.1 us)
Async XLA Ops:
  7.2 128.2 %all-gather.5.cloned.1.call-start = ((), (), s32[]{:S(2)}) async-start(), calls=%async_computation.6 | async-start | bytes 11280384 | tf_op jit(solution)/shard_map/all_gather | solution.py:497
  16.2 209.1 %all-gather.7.cloned.1.call-start = ((), (), s32[]{:S(2)}) async-start(), calls=%async_computation.7 | async-start | bytes 11280384 | tf_op jit(solution)/shard_map/all_gather | solution.py:497
  18.4 395.3 %reduce-scatter.3.cloned.1.call-start = ((), (), s32[]{:S(2)}) async-start(), calls=%async_computation.8 | async-start | bytes 11280384 | tf_op jit(solution)/shard_map/reduce_scatter | solution.py:502
  26.6 18.7 %collective-permute-start.1 = (bf16[1,144,686]{2,1,0:T(8,128)(2,1)}, bf16[1,144,686]{2,1,0:T(8,128)(2,1)S(1)}, u32[]{:S(2)}, u32[]{:S(2)}) collective-permute-start(bf16[1,144,686]{2,1,0:T(8,128)(2,1)} %get-tuple-element.145), channel_id=1, source_target_pairs={{0,1},{1,0},{2,9},{3,8},{4,5},{5,4},{6,13},{7,12},{8,3},{9,2},{10,... | collective-permute-start | bytes 592712 | tf_op jit(solution)/shard_map/ppermute | solution.py:453
  29.7 83.4 %collective-permute-start.7 = (bf16[1,144,686]{2,1,0:T(8,128)(2,1)S(1)}, bf16[1,144,686]{2,1,0:T(8,128)(2,1)S(1)}, u32[]{:S(2)}, u32[]{:S(2)}) collective-permute-start(bf16[1,144,686]{2,1,0:T(8,128)(2,1)S(1)} %get-tuple-element.139), channel_id=1, source_target_pairs={{0,13},{1,12},{2,5},{3,4},{4,9},{5,8},{6,1},{7,0},{8,15},{9,14},{1... | collective-permute-start | bytes 592712 | tf_op jit(solution)/shard_map/ppermute | solution.py:453
  34.4 78.7 %collective-permute-start.6 = (bf16[1,144,686]{2,1,0:T(8,128)(2,1)}, bf16[1,144,686]{2,1,0:T(8,128)(2,1)S(1)}, u32[]{:S(2)}, u32[]{:S(2)}) collective-permute-start(bf16[1,144,686]{2,1,0:T(8,128)(2,1)} %get-tuple-element.140), channel_id=1, source_target_pairs={{0,12},{1,13},{2,4},{3,5},{4,8},{5,9},{6,0},{7,1},{8,14},{9,15},{1... | collective-permute-start | bytes 592712 | tf_op jit(solution)/shard_map/ppermute | solution.py:453
  34.4 78.7 %collective-permute-start.5 = (bf16[1,144,686]{2,1,0:T(8,128)(2,1)}, bf16[1,144,686]{2,1,0:T(8,128)(2,1)S(1)}, u32[]{:S(2)}, u32[]{:S(2)}) collective-permute-start(bf16[1,144,686]{2,1,0:T(8,128)(2,1)} %get-tuple-element.141), channel_id=1, source_target_pairs={{0,5},{1,4},{2,13},{3,12},{4,1},{5,0},{6,9},{7,8},{8,7},{9,6},{10,... | collective-permute-start | bytes 592712 | tf_op jit(solution)/shard_map/ppermute | solution.py:453
  36.6 23.9 %collective-permute-start.2 = (bf16[1,144,686]{2,1,0:T(8,128)(2,1)}, bf16[1,144,686]{2,1,0:T(8,128)(2,1)S(1)}, u32[]{:S(2)}, u32[]{:S(2)}) collective-permute-start(bf16[1,144,686]{2,1,0:T(8,128)(2,1)} %get-tuple-element.144), channel_id=1, source_target_pairs={{0,8},{1,9},{2,0},{3,1},{4,12},{5,13},{6,4},{7,5},{8,10},{9,11},{1... | collective-permute-start | bytes 592712 | tf_op jit(solution)/shard_map/ppermute | solution.py:453
  45.3 30.0 %collective-permute-start.3 = (bf16[1,144,686]{2,1,0:T(8,128)(2,1)S(1)}, bf16[1,144,686]{2,1,0:T(8,128)(2,1)S(1)}, u32[]{:S(2)}, u32[]{:S(2)}) collective-permute-start(bf16[1,144,686]{2,1,0:T(8,128)(2,1)S(1)} %copy-done.104), channel_id=1, source_target_pairs={{0,9},{1,8},{2,1},{3,0},{4,13},{5,12},{6,5},{7,4},{8,11},{9,10},{1... | collective-permute-start | bytes 592712 | tf_op jit(solution)/shard_map/ppermute | solution.py:453
  60.5 52.5 %collective-permute-start.4 = (bf16[1,144,686]{2,1,0:T(8,128)(2,1)S(1)}, bf16[1,144,686]{2,1,0:T(8,128)(2,1)S(1)}, u32[]{:S(2)}, u32[]{:S(2)}) collective-permute-start(bf16[1,144,686]{2,1,0:T(8,128)(2,1)S(1)} %copy-done.103), channel_id=1, source_target_pairs={{0,4},{1,5},{2,12},{3,13},{4,0},{5,1},{6,8},{7,9},{8,6},{9,7},{10,... | collective-permute-start | bytes 592712 | tf_op jit(solution)/shard_map/ppermute | solution.py:453
  122.3 17.8 %collective-permute-start.8 = (bf16[1152,256]{1,0:T(8,128)(2,1)S(1)}, bf16[1152,256]{1,0:T(8,128)(2,1)S(1)}, u32[]{:S(2)}, u32[]{:S(2)}) collective-permute-start(bf16[1152,256]{1,0:T(8,128)(2,1)S(1)} %fusion.9.refs_1_.refs_0_.refs_4_), channel_id=1, source_target_pairs={{0,1},{1,0},{2,3},{3,2},{4,5},{5,4},{6,7},{7,6},{8,9},{9,8},{10,11... | collective-permute-start | bytes 1769480 | tf_op jit(solution)/shard_map/ppermute | solution.py:43
  159.5 15.5 %collective-permute-start.11 = (bf16[1152,256]{1,0:T(8,128)(2,1)S(1)}, bf16[1152,256]{1,0:T(8,128)(2,1)S(1)}, u32[]{:S(2)}, u32[]{:S(2)}) collective-permute-start(bf16[1152,256]{1,0:T(8,128)(2,1)S(1)} %shard_map.421), channel_id=1, source_target_pairs={{0,1},{1,0},{2,3},{3,2},{4,5},{5,4},{6,7},{7,6},{8,9},{9,8},{10,11... | collective-permute-start | bytes 1769480 | tf_op jit(solution)/shard_map/ppermute | solution.py:43
  175.9 14.7 %collective-permute-start.12 = (bf16[1152,256]{1,0:T(8,128)(2,1)S(1)}, bf16[1152,256]{1,0:T(8,128)(2,1)}, u32[]{:S(2)}, u32[]{:S(2)}) collective-permute-start(bf16[1152,256]{1,0:T(8,128)(2,1)S(1)} %fusion.36.refs_1_.refs_0_), channel_id=1, source_target_pairs={{0,1},{1,0},{2,3},{3,2},{4,5},{5,4},{6,7},{7,6},{8,9},{9,8},{10,11... | collective-permute-start | bytes 1769480 | tf_op jit(solution)/shard_map/ppermute | solution.py:43
  202.0 13.9 %collective-permute-start.13 = (bf16[1152,256]{1,0:T(8,128)(2,1)S(1)}, bf16[1152,256]{1,0:T(8,128)(2,1)S(1)}, u32[]{:S(2)}, u32[]{:S(2)}) collective-permute-start(bf16[1152,256]{1,0:T(8,128)(2,1)S(1)} %shard_map.427), channel_id=1, source_target_pairs={{0,1},{1,0},{2,3},{3,2},{4,5},{5,4},{6,7},{7,6},{8,9},{9,8},{10,11... | collective-permute-start | bytes 1769480 | tf_op jit(solution)/shard_map/ppermute | solution.py:43
  219.0 16.3 %collective-permute-start.14 = (bf16[1152,256]{1,0:T(8,128)(2,1)S(1)}, bf16[1152,256]{1,0:T(8,128)(2,1)S(1)}, u32[]{:S(2)}, u32[]{:S(2)}) collective-permute-start(bf16[1152,256]{1,0:T(8,128)(2,1)S(1)} %add_convert_fusion.5.refs_1_.refs_0_), channel_id=1, source_target_pairs={{0,1},{1,0},{2,3},{3,2},{4,5},{5,4},{6,7},{7,6},{8,9},{9,8},{10,11... | collective-permute-start | bytes 1769480 | tf_op jit(solution)/shard_map/ppermute | solution.py:43
  220.5 28.8 %collective-permute-start.15 = (bf16[1152,256]{1,0:T(8,128)(2,1)}, bf16[1152,256]{1,0:T(8,128)(2,1)}, u32[]{:S(2)}, u32[]{:S(2)}) collective-permute-start(bf16[1152,256]{1,0:T(8,128)(2,1)} %get-tuple-element.138.refs_2_.refs_4_), channel_id=1, source_target_pairs={{0,1},{1,0},{2,3},{3,2},{4,5},{5,4},{6,7},{7,6},{8,9},{9,8},{10,11... | collective-permute-start | bytes 1769480 | tf_op jit(solution)/shard_map/ppermute | solution.py:43
  317.2 21.4 %collective-permute-start.18 = (bf16[1152,256]{1,0:T(8,128)(2,1)}, bf16[1152,256]{1,0:T(8,128)(2,1)}, u32[]{:S(2)}, u32[]{:S(2)}) collective-permute-start(bf16[1152,256]{1,0:T(8,128)(2,1)} %shard_map.436), channel_id=1, source_target_pairs={{0,1},{1,0},{2,3},{3,2},{4,5},{5,4},{6,7},{7,6},{8,9},{9,8},{10,11... | collective-permute-start | bytes 1769480 | tf_op jit(solution)/shard_map/ppermute | solution.py:43
  341.3 20.0 %collective-permute-start.19 = (bf16[1152,256]{1,0:T(8,128)(2,1)S(1)}, bf16[1152,256]{1,0:T(8,128)(2,1)S(1)}, u32[]{:S(2)}, u32[]{:S(2)}) collective-permute-start(bf16[1152,256]{1,0:T(8,128)(2,1)S(1)} %multiply_convert_fusion.refs_2_.refs_8_), channel_id=1, source_target_pairs={{0,1},{1,0},{2,3},{3,2},{4,5},{5,4},{6,7},{7,6},{8,9},{9,8},{10,11... | collective-permute-start | bytes 1769480 | tf_op jit(solution)/shard_map/ppermute | solution.py:43
  349.3 95.2 %collective-permute-start.23 = (bf16[1152,256]{1,0:T(8,128)(2,1)}, bf16[1152,256]{1,0:T(8,128)(2,1)}, u32[]{:S(2)}, u32[]{:S(2)}) collective-permute-start(bf16[1152,256]{1,0:T(8,128)(2,1)} %shard_map.446), channel_id=1, source_target_pairs={{0,1},{1,0},{2,3},{3,2},{4,5},{5,4},{6,7},{7,6},{8,9},{9,8},{10,11... | collective-permute-start | bytes 1769480 | tf_op jit(solution)/shard_map/ppermute | solution.py:43
  357.4 26.2 %collective-permute-start.27 = (bf16[1152,120]{1,0:T(8,128)(2,1)}, bf16[1152,120]{1,0:T(8,128)(2,1)}, u32[]{:S(2)}, u32[]{:S(2)}) collective-permute-start(bf16[1152,120]{1,0:T(8,128)(2,1)} %shard_map.448), channel_id=1, source_target_pairs={{0,8},{8,0},{16,24},{24,16},{1,9},{9,1},{17,25},{25,17},{2,10},{10... | collective-permute-start | bytes 829448 | tf_op jit(solution)/shard_map/ppermute | solution.py:39
  385.4 105.4 %all-to-all-start.2 = ((bf16[8,144,120]{2,1,0:T(8,128)(2,1)}), bf16[8,144,120]{2,1,0:T(8,128)(2,1)}, u32[]{:S(2)}, u32[]{:S(2)}) async-start(bf16[8,144,120]{2,1,0:T(8,128)(2,1)} %bitcast.50), calls=%async_computation.2 | async-start | bytes 589824 | tf_op jit(solution)/shard_map/all_to_all | solution.py:669
  389.5 186.8 %reduce-scatter.5.cloned.1.call-start = ((), (), s32[]{:S(2)}) async-start(), calls=%async_computation.9 | async-start | bytes 6266880 | tf_op jit(solution)/shard_map/reduce_scatter | solution.py:502
  409.3 22.3 %collective-permute-start.22 = (bf16[2,4,288,576]{3,2,1,0:T(8,128)(2,1)}, bf16[2,4,288,576]{3,2,1,0:T(8,128)(2,1)}, u32[]{:S(2)}, u32[]{:S(2)}) collective-permute-start(bf16[2,4,288,576]{3,2,1,0:T(8,128)(2,1)} %shard_map.443), channel_id=1, source_target_pairs={{0,8},{8,0},{16,24},{24,16},{1,9},{9,1},{17,25},{25,17},{2,10},{10... | collective-permute-start | bytes 7962632 | tf_op jit(solution)/shard_map/ppermute | solution.py:39
  410.1 34.4 %collective-permute-start.25 = (bf16[1152,256]{1,0:T(8,128)(2,1)}, bf16[1152,256]{1,0:T(8,128)(2,1)}, u32[]{:S(2)}, u32[]{:S(2)}) collective-permute-start(bf16[1152,256]{1,0:T(8,128)(2,1)} %shard_map.442), channel_id=1, source_target_pairs={{0,1},{1,0},{2,3},{3,2},{4,5},{5,4},{6,7},{7,6},{8,9},{9,8},{10,11... | collective-permute-start | bytes 1769480 | tf_op jit(solution)/shard_map/ppermute | solution.py:43
  437.6 50.2 %collective-permute-start.28 = (bf16[1,4,288,576]{3,2,1,0:T(8,128)(2,1)}, bf16[1,4,288,576]{3,2,1,0:T(8,128)(2,1)}, u32[]{:S(2)}, u32[]{:S(2)}) collective-permute-start(bf16[1,4,288,576]{3,2,1,0:T(8,128)(2,1)} %slice.280), channel_id=1, source_target_pairs={{0,16},{8,24},{16,0},{24,8},{1,17},{9,25},{17,1},{25,9},{2,18},{10... | collective-permute-start | bytes 3981320 | tf_op jit(solution)/shard_map/ppermute | solution.py:39
  449.4 46.0 %collective-permute-start.26 = (bf16[1152,256]{1,0:T(8,128)(2,1)S(1)}, bf16[1152,256]{1,0:T(8,128)(2,1)S(1)}, u32[]{:S(2)}, u32[]{:S(2)}) collective-permute-start(bf16[1152,256]{1,0:T(8,128)(2,1)S(1)} %fusion.14), channel_id=1, source_target_pairs={{0,0},{1,1},{2,8},{3,9},{4,4},{5,5},{6,12},{7,13},{8,2},{9,3},{10,... | collective-permute-start | bytes 1769480 | tf_op jit(solution)/shard_map/ppermute | solution.py:442
  503.4 22.2 %all-to-all-start.1 = ((bf16[8,144,256]{2,1,0:T(8,128)(2,1)}), bf16[8,144,256]{2,1,0:T(8,128)(2,1)S(1)}, u32[]{:S(2)}, u32[]{:S(2)}) async-start(bf16[8,144,256]{2,1,0:T(8,128)(2,1)} %bitcast.201), calls=%async_computation.1 | async-start | bytes 1179648 | tf_op jit(solution)/shard_map/all_to_all | solution.py:462
  507.1 14.5 %collective-permute-start.24 = (bf16[1152,256]{1,0:T(8,128)(2,1)}, bf16[1152,256]{1,0:T(8,128)(2,1)}, u32[]{:S(2)}, u32[]{:S(2)}) collective-permute-start(bf16[1152,256]{1,0:T(8,128)(2,1)} %get-tuple-element.137), channel_id=1, source_target_pairs={{0,0},{1,1},{2,8},{3,9},{4,4},{5,5},{6,12},{7,13},{8,2},{9,3},{10,... | collective-permute-start | bytes 1769480 | tf_op jit(solution)/shard_map/ppermute | solution.py:442
  515.8 56.4 %collective-permute-start.29 = (bf16[288,576]{1,0:T(8,128)(2,1)}, bf16[288,576]{1,0:T(8,128)(2,1)}, u32[]{:S(2)}, u32[]{:S(2)}) collective-permute-start(bf16[288,576]{1,0:T(8,128)(2,1)} %get-tuple-element.147), channel_id=1, source_target_pairs={{0,2},{1,3},{2,0},{3,1},{4,6},{5,7},{6,4},{7,5},{8,10},{9,11},{10,... | collective-permute-start | bytes 995336 | tf_op jit(solution)/shard_map/ppermute | solution.py:43
  515.8 56.4 %collective-permute-start.31 = (bf16[288,576]{1,0:T(8,128)(2,1)}, bf16[288,576]{1,0:T(8,128)(2,1)}, u32[]{:S(2)}, u32[]{:S(2)}) collective-permute-start(bf16[288,576]{1,0:T(8,128)(2,1)} %get-tuple-element.148), channel_id=1, source_target_pairs={{0,6},{1,7},{2,4},{3,5},{4,2},{5,3},{6,0},{7,1},{8,14},{9,15},{10,... | collective-permute-start | bytes 995336 | tf_op jit(solution)/shard_map/ppermute | solution.py:43
  520.1 52.2 %collective-permute-start.30 = (bf16[288,576]{1,0:T(8,128)(2,1)}, bf16[288,576]{1,0:T(8,128)(2,1)}, u32[]{:S(2)}, u32[]{:S(2)}) collective-permute-start(bf16[288,576]{1,0:T(8,128)(2,1)} %get-tuple-element.149), channel_id=1, source_target_pairs={{0,4},{1,5},{2,6},{3,7},{4,0},{5,1},{6,2},{7,3},{8,12},{9,13},{10,... | collective-permute-start | bytes 995336 | tf_op jit(solution)/shard_map/ppermute | solution.py:43
  525.6 43.6 %all-to-all-start = ((bf16[8,144,256]{2,1,0:T(8,128)(2,1)}), bf16[8,144,256]{2,1,0:T(8,128)(2,1)}, u32[]{:S(2)}, u32[]{:S(2)}) async-start(bf16[8,144,256]{2,1,0:T(8,128)(2,1)} %bitcast.44), calls=%async_computation | async-start | bytes 1179648 | tf_op jit(solution)/shard_map/all_to_all | solution.py:462
  (166 other events, 947.6 us)
Sparse Core Ops, SparseCore 0:
  16.3 119.0 all-gather.4
  138.2 87.0 all-gather.6
  278.2 122.1 reduce-scatter.2
  413.8 102.7 reduce-scatter.4
